TPU v7x, 32 devices: a whole 2x2x4 slice. The times are simulated.
32 devices in a mesh: slab: 8 (over y, x, core), grid: 4 (over z).
Axes of the slice: x: 2, y: 2, z: 4, core: 2. Of those that a mesh axis runs over, the one named last changes fastest.
Arguments:
- blocks: bfloat16 [8, 4, 16, 64, 4096], P('slab', 'grid')
- coords: int32 [8, 4, 16, 3], P('slab', 'grid'), may hold values from 0 to 15, as said below
- counts: int32 [8, 4], P('slab', 'grid'), may hold values from 2 to 16, as said below
- b_init: float32 [4096, 256], P(('slab', 'grid'))
- c_init: float32 [256, 256], replicated
Outputs:
- factor_a: float32 [8192, 256], P(('slab', 'grid'))
- factor_b: float32 [4096, 256], P(('slab', 'grid'))
- factor_c: float32 [256, 256], replicated
Inputs may be any that keep to these rules, and one draw needn't show every extreme that they name: `coords`: column 0 is below 16, column 1 below 16, column 2 below 4; the 16 slots of one device name different blocks. Slots 0 to counts - 1 of a device hold its blocks and the other slots are padding; at least one device uses all 16 slots.
All inputs are finite; a program needn't handle non-finite values.
Results may differ from a plain program's by a relative error of at most 0.0007.
The roundings to bfloat16 on the way count: a program that leaves them out, or rounds other values in their place, can miss the bound.
Values may be sent and summed in bfloat16 or wider, within the bound.
No kernel may reach another device: no remote copies, remote signals or barrier semaphores. Data moves between devices by JAX's collectives and lax.ppermute only.
A program may use at most 64 MiB of HBM per device.

v0:
```python
import functools

import jax
import jax.numpy as jnp
from jax import lax
from jax.experimental import pallas as pl
from jax.experimental.pallas import tpu as pltpu
from jax.sharding import PartitionSpec as P

W = 64
IBP = 16
JBP = 16
LANES = 128
PANEL = 128
GROUP = 4

HIGH = lax.Precision.HIGHEST
EPS = 1e-05
BOTH = ("slab", "grid")
F32 = jnp.float32
BF16 = jnp.bfloat16


def product_rows(first, second, start):
    rank = first.shape[1]
    pieces = []
    for row in range(start, start + GROUP):
        spread = jnp.broadcast_to(first[row : row + 1, :], (16, rank)).astype(BF16)
        pieces.append((second * spread[None]).reshape(W, rank))
    return jnp.concatenate(pieces, 0)


def slot_rows(coords_ref, slot, mode, order):
    block = coords_ref[slot * 3 + mode]
    if order is not None:
        each = IBP // lax.axis_size(order)
        block = ((block // each) ^ lax.axis_index(order)) * each + block % each
    return pl.multiple_of(block * W, W)


def fetch(blocks_ref, held_ref, sems, slot):
    return pltpu.make_async_copy(blocks_ref.at[slot], held_ref.at[slot], sems.at[slot])


def fetch_all(count, blocks_ref, held_ref, sems):
    for slot in range(blocks_ref.shape[0]):

        @pl.when(slot < count)
        def _():
            fetch(blocks_ref, held_ref, sems, slot).start()


def moments_kernel(
    mode, orders, count_ref, coords_ref, blocks_ref, first_ref, second_ref, out_ref, held_ref, sems, order_ref
):
    rank = out_ref.shape[1]
    count = count_ref[0]
    fetch_all(count, blocks_ref, held_ref, sems)
    out_ref[...] = jnp.zeros_like(out_ref)
    spread_mode, tile_mode = ((1, 2), (0, 2), (1, 0))[mode]

    def add_block(slot, carry):
        first = first_ref[pl.ds(slot_rows(coords_ref, slot, spread_mode, orders[0]), W), :].astype(F32)
        second = second_ref[pl.ds(slot_rows(coords_ref, slot, tile_mode, orders[1]), W), :].reshape(4, 16, rank)
        target = slot_rows(coords_ref, slot, mode, orders[2])
        fetch(blocks_ref, held_ref, sems, slot).wait()
        total = jnp.zeros((W, rank), F32)
        for step in range(W // GROUP):
            left = held_ref[slot, :, step * GROUP * W : (step + 1) * GROUP * W]
            right = product_rows(first, second, step * GROUP)
            total = total + jnp.dot(left, right, preferred_element_type=F32)
        if mode == 1:
            halves = []
            for part in range(rank // LANES):
                for parity in range(2):
                    order_ref[part, pl.ds(parity, W // 2, stride=2), :] = total[
                        parity * W // 2 : (parity + 1) * W // 2, part * LANES : (part + 1) * LANES
                    ]
                halves.append(order_ref[part])
            total = jnp.concatenate(halves, 1)
        out_ref[pl.ds(target, W), :] += total
        return carry

    lax.fori_loop(0, count, add_block, 0)


SMEM_SPEC = pl.BlockSpec(memory_space=pltpu.SMEM)
HBM_SPEC = pl.BlockSpec(memory_space=pltpu.HBM)
VMEM_SPEC = pl.BlockSpec(memory_space=pltpu.VMEM)


def block_moments(mode, orders, blocks, coords, count, first, second, out_rows):
    slots = blocks.shape[0]
    rank = first.shape[1]
    return pl.pallas_call(
        functools.partial(moments_kernel, mode, orders),
        in_specs=[SMEM_SPEC, SMEM_SPEC, HBM_SPEC, VMEM_SPEC, VMEM_SPEC],
        out_specs=VMEM_SPEC,
        out_shape=jax.ShapeDtypeStruct((out_rows, rank), F32),
        scratch_shapes=[
            pltpu.VMEM(blocks.shape, BF16),
            pltpu.SemaphoreType.DMA((slots,)),
            pltpu.VMEM((rank // LANES, W, LANES), F32),
        ],
        compiler_params=pltpu.CompilerParams(vmem_limit_bytes=18 << 20),
        cost_estimate=pl.CostEstimate(
            flops=2 * slots * W**3 * rank, bytes_accessed=blocks.size * 2, transcendentals=0
        ),
    )(count, coords, pltpu.with_memory_space_constraint(blocks, pltpu.HBM), first, second)


def turn_kernel(mode, count_ref, blocks_ref, out_ref, held_ref, turned_ref, in_sems, out_sems, lanes_ref):
    count = count_ref[0]
    fetch_all(count, blocks_ref, held_ref, in_sems)
    columns = W * W // LANES

    def turn(slot, carry):
        fetch(blocks_ref, held_ref, in_sems, slot).wait()
        if mode == 1:
            for column in range(columns):
                lanes_ref[pl.ds(column, W, stride=columns), :] = held_ref[
                    slot, :, column * LANES : (column + 1) * LANES
                ].astype(F32)
            low = lax.broadcasted_iota(jnp.int32, (columns, LANES), 1) < W
            for pair in range(W // 2):
                one = lanes_ref[2 * pair * columns : (2 * pair + 1) * columns, :]
                two = lanes_ref[(2 * pair + 1) * columns : (2 * pair + 2) * columns, :]
                even = jnp.where(low, one, pltpu.roll(two, W, 1)).astype(BF16)
                odd = jnp.where(low, pltpu.roll(one, W, 1), two).astype(BF16)
                turned_ref[slot, :, pair * LANES : (pair + 1) * LANES] = jnp.concatenate([even, odd], 0)
        else:
            for pair in range(W // 2):
                turned = held_ref[slot, :, pair * LANES : (pair + 1) * LANES].T
                turned_ref[slot, :, pair * LANES : (pair + 1) * LANES] = jnp.concatenate(
                    [turned[:W], turned[W:]], 1
                )
        fetch(turned_ref, out_ref, out_sems, slot).start()
        return carry

    lax.fori_loop(0, count, turn, 0)

    def finish(slot, carry):
        fetch(turned_ref, out_ref, out_sems, slot).wait()
        return carry

    lax.fori_loop(0, count, finish, 0)


def turned_blocks(mode, blocks, count):
    slots = blocks.shape[0]
    return pl.pallas_call(
        functools.partial(turn_kernel, mode),
        in_specs=[SMEM_SPEC, HBM_SPEC],
        out_specs=HBM_SPEC,
        out_shape=pltpu.HBM(blocks.shape, blocks.dtype),
        scratch_shapes=[
            pltpu.VMEM(blocks.shape, BF16),
            pltpu.VMEM(blocks.shape, BF16),
            pltpu.SemaphoreType.DMA((slots,)),
            pltpu.SemaphoreType.DMA((slots,)),
            pltpu.VMEM((W * W * W // LANES, LANES), F32),
        ],
        compiler_params=pltpu.CompilerParams(vmem_limit_bytes=24 << 20),
        cost_estimate=pl.CostEstimate(flops=0, bytes_accessed=blocks.size * 8, transcendentals=0),
    )(count, pltpu.with_memory_space_constraint(blocks, pltpu.HBM))


def exchange(rows, axes):
    devices = lax.axis_size(axes)
    parts = lax.all_to_all(rows, axes, split_axis=0, concat_axis=0, tiled=True)
    return parts.reshape(devices, rows.shape[0] // devices, rows.shape[1])


def spread_rows(rows, axes):
    devices = lax.axis_size(axes)
    return lax.all_to_all(jnp.tile(rows, (devices, 1)), axes, split_axis=0, concat_axis=0, tiled=True)


def swap(rows, axis, step):
    return lax.ppermute(rows, axis, [(i, i ^ step) for i in range(lax.axis_size(axis))])


def swap_pieces(rows, axis):
    devices = lax.axis_size(axis)
    each = rows.shape[0] // devices
    return [swap(rows[k * each : (k + 1) * each], axis, k) for k in range(1, devices)]


def swap_gather(rows, axis):
    return jnp.concatenate([rows] + [swap(rows, axis, k) for k in range(1, lax.axis_size(axis))], 0)


def gram_local(factor):
    return jnp.dot(factor.T, factor, precision=HIGH, preferred_element_type=F32)


def exact_dot(left, right, contract):
    return lax.dot_general(left, right, (contract, ((), ())), precision=HIGH, preferred_element_type=F32)


def across_lanes(tile, lane):
    return jnp.broadcast_to(tile[:, lane : lane + 1], tile.shape)


def across_rows(tile, row):
    return jnp.broadcast_to(tile[row : row + 1, :], tile.shape)


def tree_sum(terms):
    while len(terms) > 1:
        terms = [a + b for a, b in zip(terms[::2], terms[1::2])]
    return terms[0]


def sweep_corner(entries):
    for k in range(0, 8, 2):
        at = lambda i, j: entries[(min(i, j), max(i, j))]
        a, o, d = at(k, k), at(k, k + 1), at(k + 1, k + 1)
        inverse = 1.0 / (a * d - o * o)
        w00, w01, w11 = d * inverse, -(o * inverse), a * inverse
        rest = [j for j in range(8) if j not in (k, k + 1)]
        top = {j: w00 * at(k, j) + w01 * at(k + 1, j) for j in rest}
        low = {j: w01 * at(k, j) + w11 * at(k + 1, j) for j in rest}
        swept = {(k, k): -w00, (k, k + 1): -w01, (k + 1, k + 1): -w11}
        for i in rest:
            swept[(min(k, i), max(k, i))] = top[i]
            swept[(min(k + 1, i), max(k + 1, i))] = low[i]
            for j in rest:
                if i <= j:
                    swept[(i, j)] = at(i, j) - (at(k, i) * top[j] + at(k + 1, i) * low[j])
        entries = swept
    return entries


def panel_inverse(tiles):
    shape = tiles[0].shape
    lane = lax.broadcasted_iota(jnp.int32, shape, 1)
    row = lax.broadcasted_iota(jnp.int32, shape, 0)
    for pivot in range(len(tiles)):
        tile = tiles[pivot]
        first = 8 * pivot
        columns = [across_lanes(tile, first + j) for j in range(8)]
        corner = sweep_corner({(i, j): across_rows(columns[j], i) for j in range(8) for i in range(j + 1)})
        here = (lane >= first) & (lane < first + 8)
        turned = jnp.where(here, jnp.where(lane - first == row, 1.0, 0.0), -tile)
        rows = [across_rows(turned, i) for i in range(8)]
        scaled = [tree_sum([corner[(min(i, j), max(i, j))] * rows[j] for j in range(8)]) for i in range(8)]
        swept = []
        for other, held in enumerate(tiles):
            if other == pivot:
                mine = scaled[0]
                for i in range(1, 8):
                    mine = jnp.where(row == i, scaled[i], mine)
            else:
                change = tree_sum([across_lanes(held, first + j) * scaled[j] for j in range(8)])
                mine = jnp.where(here, 0.0, held) - change
            swept.append(mine)
        tiles = swept
    return -jnp.concatenate(tiles, 0)


def on_diagonal(size):
    shape = (size, size)
    return lax.broadcasted_iota(jnp.int32, shape, 0) == lax.broadcasted_iota(jnp.int32, shape, 1)


def turned_down(across, diagonal):
    return jnp.sum(jnp.where(diagonal, across, 0.0), 1, keepdims=True)


def message_rows(devices):
    own = -(-3 * LANES // devices)
    return own, -(-(own + 2) // 8) * 8


def pack_gram(message_ref, gram, squares, devices):
    own, rows = message_rows(devices)
    packed = jnp.concatenate([gram[:LANES, :LANES], gram[:LANES, LANES:], gram[LANES:, LANES:]], 0)
    if devices * own > 3 * LANES or rows > own + 2:
        message_ref[...] = jnp.zeros_like(message_ref)
    for e in range(own):
        held = min(devices, 3 * LANES - devices * e)
        message_ref[pl.ds(e, held, stride=rows), :] = packed[devices * e : devices * e + held]
    for half in range(2):
        part = squares[:, half * LANES : (half + 1) * LANES]
        message_ref[pl.ds(own + half, devices, stride=rows), :] = jnp.broadcast_to(part, (devices, LANES))


def fold_messages(parts_ref, spread_ref, devices):
    own, rows = message_rows(devices)
    terms = [parts_ref[rows * d : rows * (d + 1), :] for d in range(devices)]
    total = functools.reduce(jnp.add, terms)
    for d in range(devices):
        spread_ref[rows * d : rows * (d + 1), :] = total
    return jnp.concatenate([total[own : own + 1], total[own + 1 : own + 2]], 1)


def unpack_gram(ref, devices):
    if ref.shape[1] != LANES:
        return ref[...]
    own, rows = message_rows(devices)
    pieces = []
    for e in range(own):
        held = min(devices, 3 * LANES - devices * e)
        pieces.append(ref[pl.ds(e, held, stride=rows), :])
    packed = jnp.concatenate(pieces, 0)
    first, corner, last = packed[:LANES], packed[LANES : 2 * LANES], packed[2 * LANES :]
    return jnp.concatenate(
        [jnp.concatenate([first, corner], 1), jnp.concatenate([corner.T, last], 1)], 0
    )


def swap_all(messages):
    return lax.all_to_all(messages, BOTH, split_axis=0, concat_axis=0, tiled=True)


def gram_message_kernel(devices, factor_ref, message_ref):
    factor = factor_ref[...]
    squares = jnp.sum(factor * factor, 0, keepdims=True)
    pack_gram(message_ref, exact_dot(factor, factor, ((0,), (0,))), squares, devices)


def fold_kernel(devices, parts_ref, spread_ref):
    fold_messages(parts_ref, spread_ref, devices)


def message_shape(devices):
    return jax.ShapeDtypeStruct((devices * message_rows(devices)[1], LANES), F32)


def gram_message(factor, devices):
    return pl.pallas_call(
        functools.partial(gram_message_kernel, devices),
        out_shape=message_shape(devices),
        compiler_params=pltpu.CompilerParams(vmem_limit_bytes=10 << 20),
    )(factor)


def fold(parts, devices):
    return pl.pallas_call(
        functools.partial(fold_kernel, devices),
        out_shape=message_shape(devices),
        compiler_params=pltpu.CompilerParams(vmem_limit_bytes=10 << 20),
    )(parts)


def on_diagonal(size):
    shape = (size, size)
    return lax.broadcasted_iota(jnp.int32, shape, 0) == lax.broadcasted_iota(jnp.int32, shape, 1)


def turned_down(across, diagonal):
    return jnp.sum(jnp.where(diagonal, across, 0.0), 1, keepdims=True)


def inverse_kernel(devices, totals, one_ref, one_scale_ref, two_ref, two_scale_ref, out_ref, held_ref):
    size = held_ref.shape[0]
    diagonal = on_diagonal(size)
    system = None
    for total, gram_ref, scale_ref in zip(totals, (one_ref, two_ref), (one_scale_ref, two_scale_ref)):
        inverse_scale = 1.0 / scale_ref[...]
        gram = unpack_gram(gram_ref, devices) * (inverse_scale / total) * turned_down(inverse_scale, diagonal)
        system = gram if system is None else system * gram
    across = lax.rsqrt(jnp.sum(jnp.where(diagonal, system, 0.0), 0, keepdims=True))
    down = turned_down(across, diagonal)
    held_ref[...] = system * across * down
    here = lax.broadcasted_iota(jnp.int32, (1, size), 1) < PANEL
    rest = size - PANEL

    def eliminate(step, carry):
        pivot = panel_inverse([held_ref[8 * g : 8 * g + 8, :PANEL] for g in range(PANEL // 8)])
        rows = held_ref[:PANEL, :]
        scaled = exact_dot(pivot, rows, ((1,), (0,)))
        minus = jnp.concatenate([-pivot, jnp.zeros((PANEL, rest), F32)], 1)
        scaled = jnp.where(here, minus, scaled)
        others = jnp.where(here, 0.0, held_ref[PANEL:, :]) - exact_dot(
            rows[:, PANEL:], scaled, ((0,), (0,))
        )
        held_ref[:rest, :] = pltpu.roll(others, rest, 1)
        held_ref[rest:, :] = pltpu.roll(scaled, rest, 1)
        return carry

    lax.fori_loop(0, size // PANEL, eliminate, 0)
    out_ref[...] = -held_ref[...] * across * down


def product_inverse(one, two, devices):
    rank = one[2].shape[1]
    return pl.pallas_call(
        functools.partial(inverse_kernel, devices, (one[1], two[1])),
        out_shape=jax.ShapeDtypeStruct((rank, rank), F32),
        scratch_shapes=[pltpu.VMEM((rank, rank), F32)],
        compiler_params=pltpu.CompilerParams(vmem_limit_bytes=10 << 20),
        cost_estimate=pl.CostEstimate(flops=10**10, bytes_accessed=3 << 18, transcendentals=0),
    )(one[0], one[2], two[0], two[2])


def solve_kernel(devices, stacked, parts, *refs):
    inverse_ref, outs = refs[parts], refs[parts + 1 :]
    if stacked:
        terms = [refs[0][part] for part in range(refs[0].shape[0])]
    else:
        terms = [ref[...] for ref in refs[:parts]]
    raw = exact_dot(functools.reduce(jnp.add, terms), inverse_ref[...], ((1,), (0,)))
    outs[0][...] = raw
    if len(outs) > 1:
        squares = jnp.sum(raw * raw, 0, keepdims=True)
        pack_gram(outs[1], exact_dot(raw, raw, ((0,), (0,))), squares, devices)


def solve_swapped(own, others, inverse, devices):
    rows, rank = others[0].shape
    whole = pl.BlockSpec((rows, rank), lambda step: (0, 0))
    square = pl.BlockSpec((rank, rank), lambda step: (0, 0))
    messages = message_shape(devices)
    return pl.pallas_call(
        functools.partial(solve_kernel, devices, False, 1 + len(others)),
        grid=(1,),
        in_specs=[whole] * (1 + len(others)) + [square],
        out_specs=[whole, pl.BlockSpec(messages.shape, lambda step: (0, 0))],
        out_shape=[jax.ShapeDtypeStruct((rows, rank), F32), messages],
        compiler_params=pltpu.CompilerParams(vmem_limit_bytes=12 << 20),
    )(own, *others, inverse)


def solve_stacked(parts, inverse, devices, with_gram):
    out_shape = [jax.ShapeDtypeStruct(parts.shape[1:], F32)]
    if with_gram:
        out_shape.append(message_shape(devices))
    return pl.pallas_call(
        functools.partial(solve_kernel, devices, True, 1),
        out_shape=out_shape,
        compiler_params=pltpu.CompilerParams(vmem_limit_bytes=10 << 20),
    )(parts, inverse)


def scale_kernel(devices, row_total, parts_ref, raw_ref, factor_ref, rounded_ref, scale_ref, spread_ref):
    squares = fold_messages(parts_ref, spread_ref, devices)
    scale = jnp.sqrt(squares / row_total + EPS)
    scale_ref[...] = scale
    factor = raw_ref[...] / scale
    factor_ref[...] = factor
    rounded_ref[...] = factor.astype(BF16)


def scale_rows(messages, raw, row_total, devices):
    return pl.pallas_call(
        functools.partial(scale_kernel, devices, row_total),
        out_shape=[
            jax.ShapeDtypeStruct(raw.shape, F32),
            jax.ShapeDtypeStruct(raw.shape, BF16),
            jax.ShapeDtypeStruct((1, raw.shape[1]), F32),
            message_shape(devices),
        ],
        compiler_params=pltpu.CompilerParams(vmem_limit_bytes=10 << 20),
    )(messages, raw)


def on_device(blocks, coords, counts, b_init, c_init):
    slab_count = lax.axis_size("slab")
    grid_count = lax.axis_size("grid")
    local_blocks = blocks[0, 0]
    local_coords = coords.reshape(-1)
    filled = counts.reshape(-1)
    doc_rows = IBP * W
    term_rows = JBP * W
    doc_total = doc_rows * slab_count
    term_total = term_rows * grid_count
    month_total = c_init.shape[0]
    month_bf = c_init.astype(BF16)
    devices = slab_count * grid_count
    ones = jnp.ones((1, c_init.shape[1]), F32)
    messages_b = gram_message(b_init, devices)
    messages_b, b_rounded = lax.optimization_barrier((messages_b, b_init.astype(BF16)))
    term_panel = lax.all_gather(b_rounded, "slab", axis=0, tiled=True)
    messages_b, term_panel = lax.optimization_barrier((swap_all(messages_b), term_panel))
    spread_b = fold(messages_b, devices)
    spread_b, term_panel = lax.optimization_barrier((spread_b, term_panel))
    gram_b = (swap_all(spread_b), term_total, ones)
    moments_a = block_moments(
        0, (None, None, "grid"), local_blocks, local_coords, filled, term_panel, month_bf, doc_rows
    )
    others_a = swap_pieces(moments_a, "grid")
    blocks_b, _ = lax.optimization_barrier((local_blocks, moments_a))
    blocks_b = turned_blocks(1, blocks_b, filled)
    gram_c = (gram_local(c_init), month_total, ones)
    inverse_a = product_inverse(gram_b, gram_c, devices)
    inverse_a, blocks_b = lax.optimization_barrier((inverse_a, blocks_b))
    raw_a, messages_a = solve_swapped(moments_a, others_a, inverse_a, devices)
    factor_a, rounded_a, scale_a, spread_a = scale_rows(swap_all(messages_a), raw_a, doc_total, devices)
    doc_panel = swap_gather(rounded_a, "grid")
    blocks_c, _ = lax.optimization_barrier((local_blocks, rounded_a))
    blocks_c = turned_blocks(2, blocks_c, filled)
    doc_panel, spread_a, blocks_c = lax.optimization_barrier((doc_panel, spread_a, blocks_c))
    gram_a = (swap_all(spread_a), doc_total, scale_a)

    moments_b = block_moments(
        1, ("grid", None, None), blocks_b, local_coords, filled, doc_panel, month_bf, term_rows
    )
    parts_b = exchange(moments_b, "slab")
    inverse_b = product_inverse(gram_a, gram_c, devices)
    raw_b, messages_n = solve_stacked(parts_b, inverse_b, devices, True)
    factor_b, rounded_b, scale_b, spread_b = scale_rows(swap_all(messages_n), raw_b, term_total, devices)
    term_panel_new = lax.all_gather(rounded_b, "slab", axis=0, tiled=True)
    gram_bn = (swap_all(spread_b), term_total, scale_b)

    moments_c = block_moments(
        2, (None, "grid", None), blocks_c, local_coords, filled, term_panel_new, doc_panel, month_total
    )
    parts_c = exchange(moments_c, BOTH)
    inverse_c = product_inverse(gram_a, gram_bn, devices)
    (raw_own,) = solve_stacked(parts_c, inverse_c, devices, False)
    raw_c = spread_rows(raw_own, BOTH)
    column_scale = jnp.sqrt(jnp.mean(raw_c * raw_c, axis=0) + EPS)
    return (factor_a, factor_b, raw_c / column_scale)


def solution(mesh):
    in_specs = (
        P("slab", "grid", None, None, None),
        P("slab", "grid", None, None),
        P("slab", "grid"),
        P(("slab", "grid"), None),
        P(),
    )
    out_specs = (P(("slab", "grid"), None), P(("slab", "grid"), None), P())
    return jax.shard_map(
        on_device, mesh=mesh, in_specs=in_specs, out_specs=out_specs, check_vma=False
    )
```

profile of v0, /device:TPU:0, one launch (start us, length us, event | category | flops | bytes accessed | tf_op | source)
XLA Modules:
  0.0 195.6 jit_solution(17193956925472905869)
XLA Ops:
  0.6 0.0 copy-start
  0.6 0.9 copy-done
  1.5 1.1 shard_map.76
  2.7 0.9 convert_element_type.6
  3.6 7.3 %all-to-all-start = ((f32[32,16,128]{2,1,0:T(8,128)}), f32[32,16,128]{2,1,0:T(8,128)S(1)}, u32[]{:S(2)}, u32[]{:S(2)}) async-start(f32[32,16,128]{2,1,0:T(8,128)} %bitcast.2), calls=%async_computation | async-start | bytes 524288 | tf_op jit(solution)/shard_map/all_to_all | solution.py:314
  10.9 10.6 %all_gather.6.first_ref = bf16[1024,256]{1,0:T(8,128)(2,1)S(1)} all-gather(bf16[128,256]{1,0:T(8,128)(2,1)S(1)} %convert_element_type.6), channel_id=1, replica_groups=mesh['slab'=8,'grid'=4] {'slab'}, dimensions={0}, use_global_device_ids=true | all-gather | bytes 589824 | tf_op jit(solution)/shard_map/all_gather | solution.py:475
  21.5 0.0 all-to-all-done
  21.5 0.8 shard_map.77
  22.2 4.4 %all-to-all-start.1 = ((f32[32,16,128]{2,1,0:T(8,128)}), f32[32,16,128]{2,1,0:T(8,128)S(1)}, u32[]{:S(2)}, u32[]{:S(2)}) async-start(f32[32,16,128]{2,1,0:T(8,128)} %bitcast.4), calls=%async_computation.1 | async-start | bytes 524288 | tf_op jit(solution)/shard_map/all_to_all | solution.py:314
  26.7 1.7 fusion.1.two_ref
  28.4 1.0 convert_element_type.7.second_ref
  30.0 0.8 copy.9
  30.8 0.1 reshape.45.coords_ref
  30.9 5.2 %shard_map.78.refs_0_ = f32[1024,256]{1,0:T(8,128)S(1)} custom-call(s32[1]{0:T(128)} %bitcast.22.count_ref, s32[48]{0:T(128)S(1)} %reshape.45.coords_ref, bf16[16,64,4096]{2,1,0:T(8,128)(2,1)} %bitcast.36, bf16[1024,256]{1,0:T(8,128)(2,1)S(1)} %all_gather.6.first_ref, bf16[256,256]{1,0:T(8,128)(2,1)S(1)} %convert_element_type.7.second_ref), custom_call_target="tpu_custom_call" | custom-call | flops 2147483648 | bytes 8388608 | tf_op jit(solution)/shard_map/pallas_call | solution.py:95
  36.1 0.1 fusion
  36.1 0.1 collective-permute-start
  36.2 4.2 %collective-permute-start.1 = (f32[256,256]{1,0:T(8,128)S(1)}, f32[256,256]{1,0:T(8,128)S(1)}, u32[]{:S(2)}, u32[]{:S(2)}) collective-permute-start(f32[256,256]{1,0:T(8,128)S(1)} %get-tuple-element.54), channel_id=1, source_target_pairs={{0,2},{1,3},{2,0},{3,1},{4,6},{5,7},{6,4},{7,5},{8,10},{9,11},{10,... | collective-permute-start | bytes 786440 | tf_op jit(solution)/shard_map/ppermute | solution.py:180
  40.4 0.2 collective-permute-start.2
  40.6 7.3 %shard_map.80.blocks_ref = bf16[16,64,4096]{2,1,0:T(8,128)(2,1)} custom-call(s32[1]{0:T(128)} %bitcast.23.count_ref, bf16[16,64,4096]{2,1,0:T(8,128)(2,1)} %bitcast.37), custom_call_target="tpu_custom_call" | custom-call | bytes 33554432 | tf_op jit(solution)/shard_map/pallas_call | solution.py:151
  47.8 0.0 all-to-all-done.1
  47.9 11.0 %shard_map.79.refs_4_ = f32[256,256]{1,0:T(8,128)S(1)} custom-call(f32[512,128]{1,0:T(8,128)S(1)} %bitcast.32, f32[1,256]{1,0:T(1,128)S(1)} %broadcast_in_dim.4.one_scale_ref.two_scale_ref, f32[256,256]{1,0:T(8,128)S(1)} %fusion.1.two_ref, f32[1,256]{1,0:T(1,128)S(1)} %broadcast_in_dim.4.one_scale_ref.two_scale_ref), custom_call_target="tpu_custom_call" | custom-call | flops 10000000000 | bytes 786432 | tf_op jit(solution)/shard_map/pallas_call | solution.py:389
  58.8 0.0 collective-permute-done.refs_1_
  58.8 0.0 collective-permute-done.1.refs_2_
  58.9 0.0 collective-permute-done.2.refs_3_
  58.9 1.2 shard_map.81
  60.0 21.3 %all_to_all.94 = f32[32,16,128]{2,1,0:T(8,128)S(1)} all-to-all(f32[32,16,128]{2,1,0:T(8,128)S(1)} %bitcast.34), channel_id=1, replica_groups=mesh['slab'=8,'grid'=4] {'slab','grid'}, dimensions={0} | all-to-all | bytes 524288 | tf_op jit(solution)/shard_map/all_to_all | solution.py:314
  81.3 0.8 shard_map.82
  82.1 1.1 collective-permute-start.3
  83.2 1.2 collective-permute-start.4
  84.5 2.1 %collective-permute-start.5 = (bf16[256,256]{1,0:T(8,128)(2,1)S(1)}, bf16[256,256]{1,0:T(8,128)(2,1)S(1)}, u32[]{:S(2)}, u32[]{:S(2)}) collective-permute-start(bf16[256,256]{1,0:T(8,128)(2,1)S(1)} %get-tuple-element.40), channel_id=1, source_target_pairs={{0,3},{1,2},{2,1},{3,0},{4,7},{5,6},{6,5},{7,4},{8,11},{9,10},{10,... | collective-permute-start | bytes 393224 | tf_op jit(solution)/shard_map/ppermute | solution.py:180
  86.5 5.6 %shard_map.83.blocks_ref = bf16[16,64,4096]{2,1,0:T(8,128)(2,1)} custom-call(s32[1]{0:T(128)} %bitcast.24.count_ref, bf16[16,64,4096]{2,1,0:T(8,128)(2,1)} %bitcast.38), custom_call_target="tpu_custom_call" | custom-call | bytes 33554432 | tf_op jit(solution)/shard_map/pallas_call | solution.py:151
  92.1 0.0 collective-permute-done.3
  92.1 3.8 %collective-permute-done.4 = bf16[256,256]{1,0:T(8,128)(2,1)S(1)} collective-permute-done((bf16[256,256]{1,0:T(8,128)(2,1)S(1)}, bf16[256,256]{1,0:T(8,128)(2,1)S(1)}, u32[]{:S(2)}, u32[]{:S(2)}) %collective-permute-start.4) | collective-permute-done | bytes 131104 | tf_op jit(solution)/shard_map/ppermute | solution.py:180
  95.9 0.0 collective-permute-done.5
  96.0 3.1 %all-to-all-start.4 = ((f32[32,16,128]{2,1,0:T(8,128)}), f32[32,16,128]{2,1,0:T(8,128)S(1)}, u32[]{:S(2)}, u32[]{:S(2)}) async-start(f32[32,16,128]{2,1,0:T(8,128)} %bitcast.9), calls=%async_computation.4 | async-start | bytes 524288 | tf_op jit(solution)/shard_map/all_to_all | solution.py:314
  99.1 6.2 %shard_map.84 = f32[1024,256]{1,0:T(8,128)} custom-call(s32[1]{0:T(128)} %bitcast.25.count_ref, s32[48]{0:T(128)S(1)} %reshape.45.coords_ref, bf16[16,64,4096]{2,1,0:T(8,128)(2,1)} %shard_map.80.blocks_ref, bf16[1024,256]{1,0:T(8,128)(2,1)S(1)} %pad_maximum_fusion.first_ref.second_ref, bf16[256,256]{1,0:T(8,128)(2,1)S(1)} %convert_element_type.7.second_ref), custom_call_target="tpu_custom_call" | custom-call | flops 2147483648 | bytes 8388608 | tf_op jit(solution)/shard_map/pallas_call | solution.py:95
  105.3 4.0 %all-to-all-done.4 = f32[32,16,128]{2,1,0:T(8,128)S(1)} async-done(((f32[32,16,128]{2,1,0:T(8,128)}), f32[32,16,128]{2,1,0:T(8,128)S(1)}, u32[]{:S(2)}, u32[]{:S(2)}) %all-to-all-start.4) | async-done | bytes 262176 | tf_op jit(solution)/shard_map/all_to_all | solution.py:314
  109.3 3.7 %all-to-all-start.3 = ((f32[8,128,256]{2,1,0:T(8,128)}), f32[8,128,256]{2,1,0:T(8,128)S(1)}, u32[]{:S(2)}, u32[]{:S(2)}) async-start(f32[8,128,256]{2,1,0:T(8,128)} %bitcast.8), calls=%async_computation.3 | async-start | bytes 2097152 | tf_op jit(solution)/shard_map/all_to_all | solution.py:170
  113.0 11.0 %shard_map.85.refs_1_ = f32[256,256]{1,0:T(8,128)S(1)} custom-call(f32[512,128]{1,0:T(8,128)S(1)} %bitcast.30, f32[1,256]{1,0:T(1,128)S(1)} %get-tuple-element.45.one_scale_ref, f32[256,256]{1,0:T(8,128)S(1)} %fusion.1.two_ref, f32[1,256]{1,0:T(1,128)S(1)} %broadcast_in_dim.4.one_scale_ref.two_scale_ref), custom_call_target="tpu_custom_call" | custom-call | flops 10000000000 | bytes 786432 | tf_op jit(solution)/shard_map/pallas_call | solution.py:389
  124.0 4.2 %all-to-all-done.3.refs_0_ = f32[8,128,256]{2,1,0:T(8,128)S(1)} async-done(((f32[8,128,256]{2,1,0:T(8,128)}), f32[8,128,256]{2,1,0:T(8,128)S(1)}, u32[]{:S(2)}, u32[]{:S(2)}) %all-to-all-start.3) | async-done | bytes 1048608 | tf_op jit(solution)/shard_map/all_to_all | solution.py:170
  128.2 0.9 shard_map.86
  129.1 12.2 %all_to_all.95 = f32[32,16,128]{2,1,0:T(8,128)S(1)} all-to-all(f32[32,16,128]{2,1,0:T(8,128)S(1)} %bitcast.35), channel_id=1, replica_groups=mesh['slab'=8,'grid'=4] {'slab','grid'}, dimensions={0} | all-to-all | bytes 524288 | tf_op jit(solution)/shard_map/all_to_all | solution.py:314
  141.3 0.8 shard_map.87
  142.0 2.7 %all-to-all-start.7 = ((f32[32,16,128]{2,1,0:T(8,128)}), f32[32,16,128]{2,1,0:T(8,128)S(1)}, u32[]{:S(2)}, u32[]{:S(2)}) async-start(f32[32,16,128]{2,1,0:T(8,128)} %bitcast.14), calls=%async_computation.7 | async-start | bytes 524288 | tf_op jit(solution)/shard_map/all_to_all | solution.py:314
  144.8 10.6 %all_gather.7.first_ref = bf16[1024,256]{1,0:T(8,128)(2,1)S(1)} all-gather(bf16[128,256]{1,0:T(8,128)(2,1)S(1)} %get-tuple-element.50), channel_id=1, replica_groups=mesh['slab'=8,'grid'=4] {'slab'}, dimensions={0}, use_global_device_ids=true | all-gather | bytes 589824 | tf_op jit(solution)/shard_map/all_gather | solution.py:504
  155.4 5.9 %shard_map.88 = f32[256,256]{1,0:T(8,128)} custom-call(s32[1]{0:T(128)} %bitcast.26.count_ref, s32[48]{0:T(128)S(1)} %reshape.45.coords_ref, bf16[16,64,4096]{2,1,0:T(8,128)(2,1)} %shard_map.83.blocks_ref, bf16[1024,256]{1,0:T(8,128)(2,1)S(1)} %all_gather.7.first_ref, bf16[1024,256]{1,0:T(8,128)(2,1)S(1)} %pad_maximum_fusion.first_ref.second_ref), custom_call_target="tpu_custom_call" | custom-call | flops 2147483648 | bytes 8388608 | tf_op jit(solution)/shard_map/pallas_call | solution.py:95
  161.3 0.0 all-to-all-done.7
  161.3 6.5 %all-to-all-start.6 = ((f32[32,8,256]{2,1,0:T(8,128)}), f32[32,8,256]{2,1,0:T(8,128)S(1)}, u32[]{:S(2)}, u32[]{:S(2)}) async-start(f32[32,8,256]{2,1,0:T(8,128)} %bitcast.13), calls=%async_computation.6 | async-start | bytes 524288 | tf_op jit(solution)/shard_map/all_to_all | solution.py:170
  167.8 11.0 %shard_map.89.refs_1_ = f32[256,256]{1,0:T(8,128)S(1)} custom-call(f32[512,128]{1,0:T(8,128)S(1)} %bitcast.31, f32[1,256]{1,0:T(1,128)S(1)} %get-tuple-element.45.one_scale_ref, f32[512,128]{1,0:T(8,128)S(1)} %bitcast.33, f32[1,256]{1,0:T(1,128)S(1)} %get-tuple-element.52.two_scale_ref), custom_call_target="tpu_custom_call" | custom-call | flops 10000000000 | bytes 786432 | tf_op jit(solution)/shard_map/pallas_call | solution.py:389
  178.9 0.0 all-to-all-done.6.refs_0_
  178.9 0.2 shard_map.90
  179.1 15.6 %all_to_all.96 = f32[32,8,256]{2,1,0:T(8,128)S(1)} all-to-all(f32[32,8,256]{2,1,0:T(8,128)S(1)} %tile.2), channel_id=1, replica_groups=mesh['slab'=8,'grid'=4] {'slab','grid'}, dimensions={0} | all-to-all | bytes 524288 | tf_op jit(solution)/shard_map/all_to_all | solution.py:176
  194.8 0.7 bitcast_divide_fusion
  (5 shorter events, 0.1 us)
Async XLA Ops:
  0.6 0.9 copy-start
  3.6 17.9 %all-to-all-start = ((f32[32,16,128]{2,1,0:T(8,128)}), f32[32,16,128]{2,1,0:T(8,128)S(1)}, u32[]{:S(2)}, u32[]{:S(2)}) async-start(f32[32,16,128]{2,1,0:T(8,128)} %bitcast.2), calls=%async_computation | async-start | bytes 524288 | tf_op jit(solution)/shard_map/all_to_all | solution.py:314
  22.2 25.6 %all-to-all-start.1 = ((f32[32,16,128]{2,1,0:T(8,128)}), f32[32,16,128]{2,1,0:T(8,128)S(1)}, u32[]{:S(2)}, u32[]{:S(2)}) async-start(f32[32,16,128]{2,1,0:T(8,128)} %bitcast.4), calls=%async_computation.1 | async-start | bytes 524288 | tf_op jit(solution)/shard_map/all_to_all | solution.py:314
  36.1 22.7 %collective-permute-start = (f32[256,256]{1,0:T(8,128)S(1)}, f32[256,256]{1,0:T(8,128)S(1)}, u32[]{:S(2)}, u32[]{:S(2)}) collective-permute-start(f32[256,256]{1,0:T(8,128)S(1)} %get-tuple-element.55), channel_id=1, source_target_pairs={{0,1},{1,0},{2,3},{3,2},{4,5},{5,4},{6,7},{7,6},{8,9},{9,8},{10,11... | collective-permute-start | bytes 786440 | tf_op jit(solution)/shard_map/ppermute | solution.py:180
  36.2 22.7 %collective-permute-start.1 = (f32[256,256]{1,0:T(8,128)S(1)}, f32[256,256]{1,0:T(8,128)S(1)}, u32[]{:S(2)}, u32[]{:S(2)}) collective-permute-start(f32[256,256]{1,0:T(8,128)S(1)} %get-tuple-element.54), channel_id=1, source_target_pairs={{0,2},{1,3},{2,0},{3,1},{4,6},{5,7},{6,4},{7,5},{8,10},{9,11},{10,... | collective-permute-start | bytes 786440 | tf_op jit(solution)/shard_map/ppermute | solution.py:180
  40.4 18.5 %collective-permute-start.2 = (f32[256,256]{1,0:T(8,128)S(1)}, f32[256,256]{1,0:T(8,128)S(1)}, u32[]{:S(2)}, u32[]{:S(2)}) collective-permute-start(f32[256,256]{1,0:T(8,128)S(1)} %get-tuple-element.53), channel_id=1, source_target_pairs={{0,3},{1,2},{2,1},{3,0},{4,7},{5,6},{6,5},{7,4},{8,11},{9,10},{10,... | collective-permute-start | bytes 786440 | tf_op jit(solution)/shard_map/ppermute | solution.py:180
  82.1 10.0 %collective-permute-start.3 = (bf16[256,256]{1,0:T(8,128)(2,1)S(1)}, bf16[256,256]{1,0:T(8,128)(2,1)S(1)}, u32[]{:S(2)}, u32[]{:S(2)}) collective-permute-start(bf16[256,256]{1,0:T(8,128)(2,1)S(1)} %get-tuple-element.40), channel_id=1, source_target_pairs={{0,1},{1,0},{2,3},{3,2},{4,5},{5,4},{6,7},{7,6},{8,9},{9,8},{10,11... | collective-permute-start | bytes 393224 | tf_op jit(solution)/shard_map/ppermute | solution.py:180
  83.2 12.7 %collective-permute-start.4 = (bf16[256,256]{1,0:T(8,128)(2,1)S(1)}, bf16[256,256]{1,0:T(8,128)(2,1)S(1)}, u32[]{:S(2)}, u32[]{:S(2)}) collective-permute-start(bf16[256,256]{1,0:T(8,128)(2,1)S(1)} %get-tuple-element.40), channel_id=1, source_target_pairs={{0,2},{1,3},{2,0},{3,1},{4,6},{5,7},{6,4},{7,5},{8,10},{9,11},{10,... | collective-permute-start | bytes 393224 | tf_op jit(solution)/shard_map/ppermute | solution.py:180
  84.5 11.4 %collective-permute-start.5 = (bf16[256,256]{1,0:T(8,128)(2,1)S(1)}, bf16[256,256]{1,0:T(8,128)(2,1)S(1)}, u32[]{:S(2)}, u32[]{:S(2)}) collective-permute-start(bf16[256,256]{1,0:T(8,128)(2,1)S(1)} %get-tuple-element.40), channel_id=1, source_target_pairs={{0,3},{1,2},{2,1},{3,0},{4,7},{5,6},{6,5},{7,4},{8,11},{9,10},{10,... | collective-permute-start | bytes 393224 | tf_op jit(solution)/shard_map/ppermute | solution.py:180
  96.0 13.3 %all-to-all-start.4 = ((f32[32,16,128]{2,1,0:T(8,128)}), f32[32,16,128]{2,1,0:T(8,128)S(1)}, u32[]{:S(2)}, u32[]{:S(2)}) async-start(f32[32,16,128]{2,1,0:T(8,128)} %bitcast.9), calls=%async_computation.4 | async-start | bytes 524288 | tf_op jit(solution)/shard_map/all_to_all | solution.py:314
  109.3 18.9 %all-to-all-start.3 = ((f32[8,128,256]{2,1,0:T(8,128)}), f32[8,128,256]{2,1,0:T(8,128)S(1)}, u32[]{:S(2)}, u32[]{:S(2)}) async-start(f32[8,128,256]{2,1,0:T(8,128)} %bitcast.8), calls=%async_computation.3 | async-start | bytes 2097152 | tf_op jit(solution)/shard_map/all_to_all | solution.py:170
  142.0 19.2 %all-to-all-start.7 = ((f32[32,16,128]{2,1,0:T(8,128)}), f32[32,16,128]{2,1,0:T(8,128)S(1)}, u32[]{:S(2)}, u32[]{:S(2)}) async-start(f32[32,16,128]{2,1,0:T(8,128)} %bitcast.14), calls=%async_computation.7 | async-start | bytes 524288 | tf_op jit(solution)/shard_map/all_to_all | solution.py:314
  161.3 17.6 %all-to-all-start.6 = ((f32[32,8,256]{2,1,0:T(8,128)}), f32[32,8,256]{2,1,0:T(8,128)S(1)}, u32[]{:S(2)}, u32[]{:S(2)}) async-start(f32[32,8,256]{2,1,0:T(8,128)} %bitcast.13), calls=%async_computation.6 | async-start | bytes 524288 | tf_op jit(solution)/shard_map/all_to_all | solution.py:170
where the time goes:
time: 197 us; the launch traced here: 196 us
  blocking collectives  70.2 us (36%)
  Pallas kernels  69 us (35%)
  starting transfers between devices  36.7 us (19%)
  waiting for transfers between devices  11.9 us (6%)
  other arithmetic  2.71 us (1%)
    all_to_all x2, blocking collectives, swap_all(): lax.all_to_all(messages, BOTH, split_axis=0, concat_axis=0, tiled=True)  33.4 us
    pallas_call x3, Pallas kernels, product_inverse(): pl.pallas_call(functools.partial(inverse_kernel, devices, (one[1], two[1]...  33 us
    all_to_all x4, starting transfers between devices, swap_all(): lax.all_to_all(messages, BOTH, split_axis=0, concat_axis=0, tiled=True)  17.6 us
    pallas_call x3, Pallas kernels, block_moments(): pl.pallas_call(functools.partial(moments_kernel, mode, orders), in_specs=...  17.3 us
    all_to_all x1, blocking collectives, spread_rows(): lax.all_to_all(jnp.tile(rows, (devices, 1)), axes, split_axis=0, concat_a...  15.6 us
    pallas_call x2, Pallas kernels, turned_blocks(): pl.pallas_call(functools.partial(turn_kernel, mode), in_specs=[SMEM_SPEC,...  12.8 us
    all_gather x1, blocking collectives, on_device(): term_panel_new = lax.all_gather(rounded_b, 'slab', axis=0, tiled=True)  10.6 us
    all_gather x1, blocking collectives, on_device(): term_panel = lax.all_gather(b_rounded, 'slab', axis=0, tiled=True)  10.6 us
  transfers between devices with their start and end apart: 12, of which 3 were waited for; matrix products, arithmetic and copies ran while one was open for 2% of the time, Pallas kernels for 32%

commit v1 on v0

--- a/solution.py
+++ b/solution.py
@@ -11,12 +11,14 @@
 IBP = 16
 JBP = 16
 LANES = 128
+STRIDE = 40
 PANEL = 128
 GROUP = 4
 
 HIGH = lax.Precision.HIGHEST
 EPS = 1e-05
 BOTH = ("slab", "grid")
+TERM_ORDER, DOC_ORDER = ("slab", True), ("grid", False)
 F32 = jnp.float32
 BF16 = jnp.bfloat16
 
@@ -31,10 +33,15 @@
 
 
 def slot_rows(coords_ref, slot, mode, order):
-    block = coords_ref[slot * 3 + mode]
+    block = coords_ref[0, 0, slot, mode]
     if order is not None:
-        each = IBP // lax.axis_size(order)
-        block = ((block // each) ^ lax.axis_index(order)) * each + block % each
+        axis, paired = order
+        devices = lax.axis_size(axis)
+        each = IBP // devices
+        place = (block // each) ^ lax.axis_index(axis)
+        if paired:
+            place = place // 2 + place % 2 * (devices // 2)
+        block = place * each + block % each
     return pl.multiple_of(block * W, W)
 
 
@@ -54,14 +61,14 @@
     mode, orders, count_ref, coords_ref, blocks_ref, first_ref, second_ref, out_ref, held_ref, sems, order_ref
 ):
     rank = out_ref.shape[1]
-    count = count_ref[0]
+    count = count_ref[0, 0]
     fetch_all(count, blocks_ref, held_ref, sems)
     out_ref[...] = jnp.zeros_like(out_ref)
     spread_mode, tile_mode = ((1, 2), (0, 2), (1, 0))[mode]
 
     def add_block(slot, carry):
         first = first_ref[pl.ds(slot_rows(coords_ref, slot, spread_mode, orders[0]), W), :].astype(F32)
-        second = second_ref[pl.ds(slot_rows(coords_ref, slot, tile_mode, orders[1]), W), :].reshape(4, 16, rank)
+        second = second_ref[pl.ds(slot_rows(coords_ref, slot, tile_mode, orders[1]), W), :].astype(BF16).reshape(4, 16, rank)
         target = slot_rows(coords_ref, slot, mode, orders[2])
         fetch(blocks_ref, held_ref, sems, slot).wait()
         total = jnp.zeros((W, rank), F32)
@@ -110,7 +117,7 @@
 
 
 def turn_kernel(mode, count_ref, blocks_ref, out_ref, held_ref, turned_ref, in_sems, out_sems, lanes_ref):
-    count = count_ref[0]
+    count = count_ref[0, 0]
     fetch_all(count, blocks_ref, held_ref, in_sems)
     columns = W * W // LANES
 
@@ -118,13 +125,13 @@
         fetch(blocks_ref, held_ref, in_sems, slot).wait()
         if mode == 1:
             for column in range(columns):
-                lanes_ref[pl.ds(column, W, stride=columns), :] = held_ref[
+                lanes_ref[pl.ds(column, W, stride=STRIDE), :] = held_ref[
                     slot, :, column * LANES : (column + 1) * LANES
                 ].astype(F32)
             low = lax.broadcasted_iota(jnp.int32, (columns, LANES), 1) < W
             for pair in range(W // 2):
-                one = lanes_ref[2 * pair * columns : (2 * pair + 1) * columns, :]
-                two = lanes_ref[(2 * pair + 1) * columns : (2 * pair + 2) * columns, :]
+                one = lanes_ref[2 * pair * STRIDE : 2 * pair * STRIDE + columns, :]
+                two = lanes_ref[(2 * pair + 1) * STRIDE : (2 * pair + 1) * STRIDE + columns, :]
                 even = jnp.where(low, one, pltpu.roll(two, W, 1)).astype(BF16)
                 odd = jnp.where(low, pltpu.roll(one, W, 1), two).astype(BF16)
                 turned_ref[slot, :, pair * LANES : (pair + 1) * LANES] = jnp.concatenate([even, odd], 0)
@@ -158,7 +165,7 @@
             pltpu.VMEM(blocks.shape, BF16),
             pltpu.SemaphoreType.DMA((slots,)),
             pltpu.SemaphoreType.DMA((slots,)),
-            pltpu.VMEM((W * W * W // LANES, LANES), F32),
+            pltpu.VMEM((W * STRIDE, LANES), F32),
         ],
         compiler_params=pltpu.CompilerParams(vmem_limit_bytes=24 << 20),
         cost_estimate=pl.CostEstimate(flops=0, bytes_accessed=blocks.size * 8, transcendentals=0),
@@ -187,7 +194,9 @@
 
 
 def swap_gather(rows, axis):
-    return jnp.concatenate([rows] + [swap(rows, axis, k) for k in range(1, lax.axis_size(axis))], 0)
+    even = [rows] + [swap(rows, axis, k) for k in range(2, lax.axis_size(axis), 2)]
+    rows = jnp.concatenate(even, 0)
+    return jnp.concatenate([rows, swap(rows, axis, 1)], 0)
 
 
 def gram_local(factor):
@@ -287,12 +296,11 @@
 
 
 def fold_messages(parts_ref, spread_ref, devices):
-    own, rows = message_rows(devices)
+    rows = message_rows(devices)[1]
     terms = [parts_ref[rows * d : rows * (d + 1), :] for d in range(devices)]
     total = functools.reduce(jnp.add, terms)
     for d in range(devices):
         spread_ref[rows * d : rows * (d + 1), :] = total
-    return jnp.concatenate([total[own : own + 1], total[own + 1 : own + 2]], 1)
 
 
 def unpack_gram(ref, devices):
@@ -434,8 +442,10 @@
     )(parts, inverse)
 
 
-def scale_kernel(devices, row_total, parts_ref, raw_ref, factor_ref, rounded_ref, scale_ref, spread_ref):
-    squares = fold_messages(parts_ref, spread_ref, devices)
+def scale_kernel(devices, row_total, parts_ref, raw_ref, factor_ref, rounded_ref, scale_ref):
+    own, rows = message_rows(devices)
+    total = functools.reduce(jnp.add, [parts_ref[rows * d + own : rows * d + own + 2, :] for d in range(devices)])
+    squares = jnp.concatenate([total[:1], total[1:2]], 1)
     scale = jnp.sqrt(squares / row_total + EPS)
     scale_ref[...] = scale
     factor = raw_ref[...] / scale
@@ -450,7 +460,6 @@
             jax.ShapeDtypeStruct(raw.shape, F32),
             jax.ShapeDtypeStruct(raw.shape, BF16),
             jax.ShapeDtypeStruct((1, raw.shape[1]), F32),
-            message_shape(devices),
         ],
         compiler_params=pltpu.CompilerParams(vmem_limit_bytes=10 << 20),
     )(messages, raw)
@@ -460,52 +469,54 @@
     slab_count = lax.axis_size("slab")
     grid_count = lax.axis_size("grid")
     local_blocks = blocks[0, 0]
-    local_coords = coords.reshape(-1)
-    filled = counts.reshape(-1)
     doc_rows = IBP * W
     term_rows = JBP * W
     doc_total = doc_rows * slab_count
     term_total = term_rows * grid_count
     month_total = c_init.shape[0]
-    month_bf = c_init.astype(BF16)
     devices = slab_count * grid_count
     ones = jnp.ones((1, c_init.shape[1]), F32)
-    messages_b = gram_message(b_init, devices)
-    messages_b, b_rounded = lax.optimization_barrier((messages_b, b_init.astype(BF16)))
-    term_panel = lax.all_gather(b_rounded, "slab", axis=0, tiled=True)
-    messages_b, term_panel = lax.optimization_barrier((swap_all(messages_b), term_panel))
-    spread_b = fold(messages_b, devices)
-    spread_b, term_panel = lax.optimization_barrier((spread_b, term_panel))
+    b_rounded, b_held = lax.optimization_barrier((b_init.astype(BF16), b_init))
+    term_panel = swap_gather(b_rounded, "slab")
+    messages_b = swap_all(gram_message(b_held, devices))
+    spread_b, term_panel = lax.optimization_barrier((fold(messages_b, devices), term_panel))
     gram_b = (swap_all(spread_b), term_total, ones)
     moments_a = block_moments(
-        0, (None, None, "grid"), local_blocks, local_coords, filled, term_panel, month_bf, doc_rows
+        0, (TERM_ORDER, None, DOC_ORDER), local_blocks, coords, counts, term_panel, c_init, doc_rows
     )
     others_a = swap_pieces(moments_a, "grid")
-    blocks_b, _ = lax.optimization_barrier((local_blocks, moments_a))
-    blocks_b = turned_blocks(1, blocks_b, filled)
-    gram_c = (gram_local(c_init), month_total, ones)
+    c_held, _ = lax.optimization_barrier((c_init, moments_a))
+    gram_c = (gram_local(c_held), month_total, ones)
     inverse_a = product_inverse(gram_b, gram_c, devices)
+    blocks_b, inverse_a = lax.optimization_barrier((local_blocks, inverse_a))
+    blocks_b = turned_blocks(1, blocks_b, counts)
     inverse_a, blocks_b = lax.optimization_barrier((inverse_a, blocks_b))
     raw_a, messages_a = solve_swapped(moments_a, others_a, inverse_a, devices)
-    factor_a, rounded_a, scale_a, spread_a = scale_rows(swap_all(messages_a), raw_a, doc_total, devices)
-    doc_panel = swap_gather(rounded_a, "grid")
-    blocks_c, _ = lax.optimization_barrier((local_blocks, rounded_a))
-    blocks_c = turned_blocks(2, blocks_c, filled)
-    doc_panel, spread_a, blocks_c = lax.optimization_barrier((doc_panel, spread_a, blocks_c))
+    blocks_c, messages_a = lax.optimization_barrier((local_blocks, messages_a))
+    blocks_c = turned_blocks(2, blocks_c, counts)
+    messages_a, blocks_c = lax.optimization_barrier((swap_all(messages_a), blocks_c))
+    factor_a, rounded_a, scale_a = scale_rows(messages_a, raw_a, doc_total, devices)
+    pieces = [rounded_a] + [swap(rounded_a, "grid", k) for k in range(1, grid_count)]
+    messages_a, pieces[1] = lax.optimization_barrier((messages_a, pieces[1]))
+    doc_panel = jnp.concatenate(pieces, 0)
+    spread_a = fold(messages_a, devices)
     gram_a = (swap_all(spread_a), doc_total, scale_a)
 
     moments_b = block_moments(
-        1, ("grid", None, None), blocks_b, local_coords, filled, doc_panel, month_bf, term_rows
+        1, (DOC_ORDER, None, None), blocks_b, coords, counts, doc_panel, c_init, term_rows
     )
     parts_b = exchange(moments_b, "slab")
     inverse_b = product_inverse(gram_a, gram_c, devices)
     raw_b, messages_n = solve_stacked(parts_b, inverse_b, devices, True)
-    factor_b, rounded_b, scale_b, spread_b = scale_rows(swap_all(messages_n), raw_b, term_total, devices)
-    term_panel_new = lax.all_gather(rounded_b, "slab", axis=0, tiled=True)
-    gram_bn = (swap_all(spread_b), term_total, scale_b)
+    messages_n = swap_all(messages_n)
+    factor_b, rounded_b, scale_b = scale_rows(messages_n, raw_b, term_total, devices)
+    term_panel_new = swap_gather(rounded_b, "slab")
+    messages_n, _ = lax.optimization_barrier((messages_n, rounded_b))
+    spread_n = fold(messages_n, devices)
+    gram_bn = (swap_all(spread_n), term_total, scale_b)
 
     moments_c = block_moments(
-        2, (None, "grid", None), blocks_c, local_coords, filled, term_panel_new, doc_panel, month_total
+        2, (TERM_ORDER, DOC_ORDER, None), blocks_c, coords, counts, term_panel_new, doc_panel, month_total
     )
     parts_c = exchange(moments_c, BOTH)
     inverse_c = product_inverse(gram_a, gram_bn, devices)

time: 197 us -> 187 us (0.949)
  blocking collectives: 70.2 us -> 27.7 us
  waiting for transfers between devices: 11.9 us -> 35.2 us
  starting transfers between devices: 36.7 us -> 50 us
  Pallas kernels: 69 us -> 66.3 us
    all_to_all x2 -> x1, blocking collectives: 33.4 us -> 11.9 us  [swap_all(): lax.all_to_all(messages, BOTH, split_axis=0, concat_axis=0, tiled=True)]
    all_gather x2 -> x0, blocking collectives: 21.2 us -> none  [the longest x1 10.6 us: on_device(): term_panel_new = lax.all_gather(rounded_b, 'slab', axis=0, tiled=True)]
    all_to_all x4 -> x5, waiting for transfers between devices: 3.97 us -> 15.6 us  [swap_all(): lax.all_to_all(messages, BOTH, split_axis=0, concat_axis=0, tiled=True)]
    ppermute x6 -> x14, waiting for transfers between devices: 3.8 us -> 15.1 us  [swap(): lax.ppermute(rows, axis, [(i, i ^ step) for i in range(lax.axis_size(axis...]
    ppermute x6 -> x14, starting transfers between devices: 8.83 us -> 17 us  [swap(): lax.ppermute(rows, axis, [(i, i ^ step) for i in range(lax.axis_size(axis...]
    pallas_call x2, Pallas kernels: 12.8 us -> 9.11 us  [turned_blocks(): pl.pallas_call(functools.partial(turn_kernel, mode), in_specs=[SMEM_SPEC,...]
    all_to_all x4 -> x5, starting transfers between devices: 17.6 us -> 21.2 us  [swap_all(): lax.all_to_all(messages, BOTH, split_axis=0, concat_axis=0, tiled=True)]
  transfers between devices with their start and end apart: 12 -> 21, of which waited for: 3 -> 10; matrix products, arithmetic and copies ran while one was open for 2% -> 1% of each run, Pallas kernels for 32% -> 33%
where the time goes in v1:
time: 187 us; the launch traced here: 186 us
  Pallas kernels  66.3 us (35%)
  starting transfers between devices  50 us (27%)
  waiting for transfers between devices  35.2 us (19%)
  blocking collectives  27.7 us (15%)
  local copies, waits for them, and re-layouts  2.83 us (2%)
    pallas_call x3, Pallas kernels, product_inverse(): pl.pallas_call(functools.partial(inverse_kernel, devices, (one[1], two[1]...  33 us
    all_to_all x5, starting transfers between devices, swap_all(): lax.all_to_all(messages, BOTH, split_axis=0, concat_axis=0, tiled=True)  21.2 us
    ppermute x14, starting transfers between devices, swap(): lax.ppermute(rows, axis, [(i, i ^ step) for i in range(lax.axis_size(axis...  17 us
    pallas_call x3, Pallas kernels, block_moments(): pl.pallas_call(functools.partial(moments_kernel, mode, orders), in_specs=...  16.3 us
    all_to_all x1, blocking collectives, spread_rows(): lax.all_to_all(jnp.tile(rows, (devices, 1)), axes, split_axis=0, concat_a...  15.8 us
    all_to_all x5, waiting for transfers between devices, swap_all(): lax.all_to_all(messages, BOTH, split_axis=0, concat_axis=0, tiled=True)  15.6 us
    ppermute x14, waiting for transfers between devices, swap(): lax.ppermute(rows, axis, [(i, i ^ step) for i in range(lax.axis_size(axis...  15.1 us
    all_to_all x1, blocking collectives, swap_all(): lax.all_to_all(messages, BOTH, split_axis=0, concat_axis=0, tiled=True)  11.9 us
  transfers between devices with their start and end apart: 21, of which 10 were waited for; matrix products, arithmetic and copies ran while one was open for 1% of the time, Pallas kernels for 33%

profile of v1, /device:TPU:0, one launch (start us, length us, event | category | flops | bytes accessed | tf_op | source)
XLA Modules:
  0.0 186.0 jit_solution(3304783932128120291)
XLA Ops:
  0.6 0.9 convert_element_type.3
  1.5 4.0 %collective-permute-start.2 = (bf16[128,256]{1,0:T(8,128)(2,1)S(1)}, bf16[128,256]{1,0:T(8,128)(2,1)S(1)}, u32[]{:S(2)}, u32[]{:S(2)}) collective-permute-start(bf16[128,256]{1,0:T(8,128)(2,1)S(1)} %convert_element_type.3), channel_id=1, source_target_pairs={{0,24},{4,28},{8,16},{12,20},{16,8},{20,12},{24,0},{28,4},{1,25},{... | collective-permute-start | bytes 196616 | tf_op jit(solution)/shard_map/ppermute | solution.py:187
  5.5 0.5 collective-permute-start.1
  6.0 0.1 collective-permute-start
  6.1 0.9 copy-done.2
  7.0 1.1 shard_map.76
  8.2 6.2 %all-to-all-start = ((f32[32,16,128]{2,1,0:T(8,128)}), f32[32,16,128]{2,1,0:T(8,128)S(1)}, u32[]{:S(2)}, u32[]{:S(2)}) async-start(f32[32,16,128]{2,1,0:T(8,128)} %bitcast.1), calls=%async_computation | async-start | bytes 524288 | tf_op jit(solution)/shard_map/all_to_all | solution.py:322
  15.1 0.8 copy.8.coords_ref
  15.8 0.0 collective-permute-done.2
  15.9 0.0 collective-permute-done
  15.9 0.3 collective-permute-start.3
  16.2 1.3 collective-permute-done.3
  17.5 7.1 %all-to-all-done = f32[32,16,128]{2,1,0:T(8,128)S(1)} async-done(((f32[32,16,128]{2,1,0:T(8,128)}), f32[32,16,128]{2,1,0:T(8,128)S(1)}, u32[]{:S(2)}, u32[]{:S(2)}) %all-to-all-start) | async-done | bytes 262176 | tf_op jit(solution)/shard_map/all_to_all | solution.py:322
  24.6 0.8 shard_map.77
  25.4 2.7 %all-to-all-start.1 = ((f32[32,16,128]{2,1,0:T(8,128)}), f32[32,16,128]{2,1,0:T(8,128)S(1)}, u32[]{:S(2)}, u32[]{:S(2)}) async-start(f32[32,16,128]{2,1,0:T(8,128)} %bitcast.3), calls=%async_computation.1 | async-start | bytes 524288 | tf_op jit(solution)/shard_map/all_to_all | solution.py:322
  28.1 0.0 copy-start
  28.1 0.9 copy-done
  29.1 4.9 %shard_map.78.refs_0_ = f32[1024,256]{1,0:T(8,128)S(1)} custom-call(s32[1,1]{1,0:T(1,128)S(6)} %copy.22.count_ref, s32[1,1,16,3]{3,2,1,0:T(8,128)S(1)} %copy.8.coords_ref, bf16[16,64,4096]{2,1,0:T(8,128)(2,1)} %bitcast.29, bf16[1024,256]{1,0:T(8,128)(2,1)S(1)} %constant_dynamic-update-slice_fusion.first_ref, f32[256,256]{1,0:T(8,128)S(1)} %copy-done), custom_call_target="tpu_custom_call" | custom-call | flops 2147483648 | bytes 8388608 | tf_op jit(solution)/shard_map/pallas_call | solution.py:102
  33.9 0.1 fusion
  34.0 3.7 %collective-permute-start.6 = (f32[256,256]{1,0:T(8,128)S(1)}, f32[256,256]{1,0:T(8,128)S(1)}, u32[]{:S(2)}, u32[]{:S(2)}) collective-permute-start(f32[256,256]{1,0:T(8,128)S(1)} %get-tuple-element.55), channel_id=1, source_target_pairs={{0,3},{1,2},{2,1},{3,0},{4,7},{5,6},{6,5},{7,4},{8,11},{9,10},{10,... | collective-permute-start | bytes 786440 | tf_op jit(solution)/shard_map/ppermute | solution.py:187
  37.7 1.1 collective-permute-start.5
  38.8 0.6 fusion.1.two_ref
  39.4 0.0 all-to-all-done.1
  39.4 11.0 %shard_map.79.refs_4_ = f32[256,256]{1,0:T(8,128)S(1)} custom-call(f32[512,128]{1,0:T(8,128)S(1)} %bitcast.27, f32[1,256]{1,0:T(1,128)S(1)} %broadcast_in_dim.4.one_scale_ref.two_scale_ref, f32[256,256]{1,0:T(8,128)S(1)} %fusion.1.two_ref, f32[1,256]{1,0:T(1,128)S(1)} %broadcast_in_dim.4.one_scale_ref.two_scale_ref), custom_call_target="tpu_custom_call" | custom-call | flops 10000000000 | bytes 786432 | tf_op jit(solution)/shard_map/pallas_call | solution.py:397
  50.4 4.0 %shard_map.80.blocks_ref = bf16[16,64,4096]{2,1,0:T(8,128)(2,1)} custom-call(s32[1,1]{1,0:T(1,128)S(6)} %copy.22.count_ref, bf16[16,64,4096]{2,1,0:T(8,128)(2,1)} %bitcast.30), custom_call_target="tpu_custom_call" | custom-call | bytes 33554432 | tf_op jit(solution)/shard_map/pallas_call | solution.py:158
  54.4 0.0 collective-permute-done.6.refs_3_
  54.4 6.3 %collective-permute-done.5.refs_2_ = f32[256,256]{1,0:T(8,128)S(1)} collective-permute-done((f32[256,256]{1,0:T(8,128)S(1)}, f32[256,256]{1,0:T(8,128)S(1)}, u32[]{:S(2)}, u32[]{:S(2)}) %collective-permute-start.5) | collective-permute-done | bytes 262176 | tf_op jit(solution)/shard_map/ppermute | solution.py:187
  60.7 1.9 %shard_map.81 = (f32[256,256]{1,0:T(8,128)S(1)}, f32[512,128]{1,0:T(8,128)}) custom-call(f32[1024,256]{1,0:T(8,128)S(1)} %shard_map.78.refs_0_, f32[256,256]{1,0:T(8,128)S(1)} %collective-permute-done.4.refs_1_, f32[256,256]{1,0:T(8,128)S(1)} %collective-permute-done.5.refs_2_, f32[256,256]{1,0:T(8,128)S(1)} %collective-permute-done.6.refs_3_, ...), custom_call_target="tpu_custom_call" | custom-call | tf_op jit(solution)/shard_map/pallas_call | solution.py:424
  62.6 4.6 %all-to-all-start.2 = ((f32[32,16,128]{2,1,0:T(8,128)}), f32[32,16,128]{2,1,0:T(8,128)S(1)}, u32[]{:S(2)}, u32[]{:S(2)}) async-start(f32[32,16,128]{2,1,0:T(8,128)} %bitcast.5), calls=%async_computation.2 | async-start | bytes 524288 | tf_op jit(solution)/shard_map/all_to_all | solution.py:322
  67.2 0.0 copy-start.1
  67.2 5.1 %shard_map.82.blocks_ref = bf16[16,64,4096]{2,1,0:T(8,128)(2,1)} custom-call(s32[1,1]{1,0:T(1,128)S(6)} %copy.22.count_ref, bf16[16,64,4096]{2,1,0:T(8,128)(2,1)} %bitcast.31), custom_call_target="tpu_custom_call" | custom-call | bytes 33554432 | tf_op jit(solution)/shard_map/pallas_call | solution.py:158
  72.3 5.0 %all-to-all-done.2 = f32[32,16,128]{2,1,0:T(8,128)S(1)} async-done(((f32[32,16,128]{2,1,0:T(8,128)}), f32[32,16,128]{2,1,0:T(8,128)S(1)}, u32[]{:S(2)}, u32[]{:S(2)}) %all-to-all-start.2) | async-done | bytes 262176 | tf_op jit(solution)/shard_map/all_to_all | solution.py:322
  77.4 0.8 shard_map.83
  78.2 1.1 collective-permute-start.7
  79.3 1.1 collective-permute-start.9
  80.4 1.3 collective-permute-start.8
  81.7 2.6 %collective-permute-done.7 = bf16[256,256]{1,0:T(8,128)(2,1)S(1)} collective-permute-done((bf16[256,256]{1,0:T(8,128)(2,1)S(1)}, bf16[256,256]{1,0:T(8,128)(2,1)S(1)}, u32[]{:S(2)}, u32[]{:S(2)}) %collective-permute-start.7) | collective-permute-done | bytes 131104 | tf_op jit(solution)/shard_map/ppermute | solution.py:187
  84.2 0.8 shard_map.85
  85.0 4.9 %all-to-all-start.4 = ((f32[32,16,128]{2,1,0:T(8,128)}), f32[32,16,128]{2,1,0:T(8,128)S(1)}, u32[]{:S(2)}, u32[]{:S(2)}) async-start(f32[32,16,128]{2,1,0:T(8,128)} %bitcast.8), calls=%async_computation.4 | async-start | bytes 524288 | tf_op jit(solution)/shard_map/all_to_all | solution.py:322
  89.9 3.8 %collective-permute-done.8 = bf16[256,256]{1,0:T(8,128)(2,1)S(1)} collective-permute-done((bf16[256,256]{1,0:T(8,128)(2,1)S(1)}, bf16[256,256]{1,0:T(8,128)(2,1)S(1)}, u32[]{:S(2)}, u32[]{:S(2)}) %collective-permute-start.8) | collective-permute-done | bytes 131104 | tf_op jit(solution)/shard_map/ppermute | solution.py:187
  93.7 0.0 collective-permute-done.9
  93.7 5.8 %shard_map.84 = f32[1024,256]{1,0:T(8,128)} custom-call(s32[1,1]{1,0:T(1,128)S(6)} %copy.22.count_ref, s32[1,1,16,3]{3,2,1,0:T(8,128)S(1)} %copy.8.coords_ref, bf16[16,64,4096]{2,1,0:T(8,128)(2,1)} %shard_map.80.blocks_ref, bf16[1024,256]{1,0:T(8,128)(2,1)S(1)} %constant_dynamic-update-slice_fusion.5.first_ref.second_ref, f32[256,256]{1,0:T(8,128)S(1)} %copy-done.1), custom_call_target="tpu_custom_call" | custom-call | flops 2147483648 | bytes 8388608 | tf_op jit(solution)/shard_map/pallas_call | solution.py:102
  99.6 0.5 all-to-all-done.4
  100.1 6.6 %all-to-all-start.3 = ((f32[8,128,256]{2,1,0:T(8,128)}), f32[8,128,256]{2,1,0:T(8,128)S(1)}, u32[]{:S(2)}, u32[]{:S(2)}) async-start(f32[8,128,256]{2,1,0:T(8,128)} %bitcast.7), calls=%async_computation.3 | async-start | bytes 2097152 | tf_op jit(solution)/shard_map/all_to_all | solution.py:177
  106.7 11.0 %shard_map.86.refs_1_ = f32[256,256]{1,0:T(8,128)S(1)} custom-call(f32[512,128]{1,0:T(8,128)S(1)} %bitcast.24, f32[1,256]{1,0:T(1,128)S(1)} %get-tuple-element.47.one_scale_ref, f32[256,256]{1,0:T(8,128)S(1)} %fusion.1.two_ref, f32[1,256]{1,0:T(1,128)S(1)} %broadcast_in_dim.4.one_scale_ref.two_scale_ref), custom_call_target="tpu_custom_call" | custom-call | flops 10000000000 | bytes 786432 | tf_op jit(solution)/shard_map/pallas_call | solution.py:397
  117.7 4.4 %all-to-all-done.3.refs_0_ = f32[8,128,256]{2,1,0:T(8,128)S(1)} async-done(((f32[8,128,256]{2,1,0:T(8,128)}), f32[8,128,256]{2,1,0:T(8,128)S(1)}, u32[]{:S(2)}, u32[]{:S(2)}) %all-to-all-start.3) | async-done | bytes 1048608 | tf_op jit(solution)/shard_map/all_to_all | solution.py:177
  122.1 0.9 shard_map.87
  123.0 11.9 %all_to_all.94 = f32[32,16,128]{2,1,0:T(8,128)S(1)} all-to-all(f32[32,16,128]{2,1,0:T(8,128)S(1)} %bitcast.28), channel_id=1, replica_groups=mesh['slab'=8,'grid'=4] {'slab','grid'}, dimensions={0} | all-to-all | bytes 524288 | tf_op jit(solution)/shard_map/all_to_all | solution.py:322
  134.9 0.7 shard_map.88
  135.6 1.0 collective-permute-start.12
  136.6 1.5 collective-permute-start.11
  138.1 1.0 collective-permute-start.10
  139.1 0.8 shard_map.90
  139.9 2.7 %all-to-all-start.7 = ((f32[32,16,128]{2,1,0:T(8,128)}), f32[32,16,128]{2,1,0:T(8,128)S(1)}, u32[]{:S(2)}, u32[]{:S(2)}) async-start(f32[32,16,128]{2,1,0:T(8,128)} %bitcast.13), calls=%async_computation.7 | async-start | bytes 524288 | tf_op jit(solution)/shard_map/all_to_all | solution.py:322
  142.6 0.0 collective-permute-done.12
  142.7 0.3 collective-permute-start.13
  143.0 1.3 collective-permute-done.13
  144.3 5.6 %shard_map.89 = f32[256,256]{1,0:T(8,128)} custom-call(s32[1,1]{1,0:T(1,128)S(6)} %copy.22.count_ref, s32[1,1,16,3]{3,2,1,0:T(8,128)S(1)} %copy.8.coords_ref, bf16[16,64,4096]{2,1,0:T(8,128)(2,1)} %shard_map.82.blocks_ref, bf16[1024,256]{1,0:T(8,128)(2,1)S(1)} %constant_dynamic-update-slice_fusion.9.first_ref, ...), custom_call_target="tpu_custom_call" | custom-call | flops 2147483648 | bytes 8388608 | tf_op jit(solution)/shard_map/pallas_call | solution.py:102
  149.9 2.9 %all-to-all-done.7 = f32[32,16,128]{2,1,0:T(8,128)S(1)} async-done(((f32[32,16,128]{2,1,0:T(8,128)}), f32[32,16,128]{2,1,0:T(8,128)S(1)}, u32[]{:S(2)}, u32[]{:S(2)}) %all-to-all-start.7) | async-done | bytes 262176 | tf_op jit(solution)/shard_map/all_to_all | solution.py:322
  152.8 5.3 %all-to-all-start.6 = ((f32[32,8,256]{2,1,0:T(8,128)}), f32[32,8,256]{2,1,0:T(8,128)S(1)}, u32[]{:S(2)}, u32[]{:S(2)}) async-start(f32[32,8,256]{2,1,0:T(8,128)} %bitcast.12), calls=%async_computation.6 | async-start | bytes 524288 | tf_op jit(solution)/shard_map/all_to_all | solution.py:177
  158.0 11.0 %shard_map.91.refs_1_ = f32[256,256]{1,0:T(8,128)S(1)} custom-call(f32[512,128]{1,0:T(8,128)S(1)} %bitcast.25, f32[1,256]{1,0:T(1,128)S(1)} %get-tuple-element.47.one_scale_ref, f32[512,128]{1,0:T(8,128)S(1)} %bitcast.26, f32[1,256]{1,0:T(1,128)S(1)} %get-tuple-element.54.two_scale_ref), custom_call_target="tpu_custom_call" | custom-call | flops 10000000000 | bytes 786432 | tf_op jit(solution)/shard_map/pallas_call | solution.py:397
  169.1 0.2 shard_map.92
  169.4 15.8 %all_to_all.95 = f32[32,8,256]{2,1,0:T(8,128)S(1)} all-to-all(f32[32,8,256]{2,1,0:T(8,128)S(1)} %tile.2), channel_id=1, replica_groups=mesh['slab'=8,'grid'=4] {'slab','grid'}, dimensions={0} | all-to-all | bytes 524288 | tf_op jit(solution)/shard_map/all_to_all | solution.py:183
  185.3 0.7 bitcast_divide_fusion
  (28 shorter events, 0.3 us)
Async XLA Ops:
  1.5 14.3 %collective-permute-start.2 = (bf16[128,256]{1,0:T(8,128)(2,1)S(1)}, bf16[128,256]{1,0:T(8,128)(2,1)S(1)}, u32[]{:S(2)}, u32[]{:S(2)}) collective-permute-start(bf16[128,256]{1,0:T(8,128)(2,1)S(1)} %convert_element_type.3), channel_id=1, source_target_pairs={{0,24},{4,28},{8,16},{12,20},{16,8},{20,12},{24,0},{28,4},{1,25},{... | collective-permute-start | bytes 196616 | tf_op jit(solution)/shard_map/ppermute | solution.py:187
  5.5 10.4 %collective-permute-start.1 = (bf16[128,256]{1,0:T(8,128)(2,1)S(1)}, bf16[128,256]{1,0:T(8,128)(2,1)S(1)}, u32[]{:S(2)}, u32[]{:S(2)}) collective-permute-start(bf16[128,256]{1,0:T(8,128)(2,1)S(1)} %convert_element_type.3), channel_id=1, source_target_pairs={{0,16},{4,20},{8,24},{12,28},{16,0},{20,4},{24,8},{28,12},{1,17},{... | collective-permute-start | bytes 196616 | tf_op jit(solution)/shard_map/ppermute | solution.py:187
  6.0 9.9 %collective-permute-start = (bf16[128,256]{1,0:T(8,128)(2,1)S(1)}, bf16[128,256]{1,0:T(8,128)(2,1)S(1)}, u32[]{:S(2)}, u32[]{:S(2)}) collective-permute-start(bf16[128,256]{1,0:T(8,128)(2,1)S(1)} %convert_element_type.3), channel_id=1, source_target_pairs={{0,8},{4,12},{8,0},{12,4},{16,24},{20,28},{24,16},{28,20},{1,9},{5... | collective-permute-start | bytes 196616 | tf_op jit(solution)/shard_map/ppermute | solution.py:187
  6.1 0.9 copy-start.2
  8.2 16.4 %all-to-all-start = ((f32[32,16,128]{2,1,0:T(8,128)}), f32[32,16,128]{2,1,0:T(8,128)S(1)}, u32[]{:S(2)}, u32[]{:S(2)}) async-start(f32[32,16,128]{2,1,0:T(8,128)} %bitcast.1), calls=%async_computation | async-start | bytes 524288 | tf_op jit(solution)/shard_map/all_to_all | solution.py:322
  15.9 1.6 collective-permute-start.3
  25.4 14.0 %all-to-all-start.1 = ((f32[32,16,128]{2,1,0:T(8,128)}), f32[32,16,128]{2,1,0:T(8,128)S(1)}, u32[]{:S(2)}, u32[]{:S(2)}) async-start(f32[32,16,128]{2,1,0:T(8,128)} %bitcast.3), calls=%async_computation.1 | async-start | bytes 524288 | tf_op jit(solution)/shard_map/all_to_all | solution.py:322
  28.1 1.0 copy-start
  34.0 20.4 %collective-permute-start.6 = (f32[256,256]{1,0:T(8,128)S(1)}, f32[256,256]{1,0:T(8,128)S(1)}, u32[]{:S(2)}, u32[]{:S(2)}) collective-permute-start(f32[256,256]{1,0:T(8,128)S(1)} %get-tuple-element.55), channel_id=1, source_target_pairs={{0,3},{1,2},{2,1},{3,0},{4,7},{5,6},{6,5},{7,4},{8,11},{9,10},{10,... | collective-permute-start | bytes 786440 | tf_op jit(solution)/shard_map/ppermute | solution.py:187
  37.7 23.0 %collective-permute-start.5 = (f32[256,256]{1,0:T(8,128)S(1)}, f32[256,256]{1,0:T(8,128)S(1)}, u32[]{:S(2)}, u32[]{:S(2)}) collective-permute-start(f32[256,256]{1,0:T(8,128)S(1)} %get-tuple-element.56), channel_id=1, source_target_pairs={{0,2},{1,3},{2,0},{3,1},{4,6},{5,7},{6,4},{7,5},{8,10},{9,11},{10,... | collective-permute-start | bytes 786440 | tf_op jit(solution)/shard_map/ppermute | solution.py:187
  38.8 21.9 %collective-permute-start.4 = (f32[256,256]{1,0:T(8,128)S(1)}, f32[256,256]{1,0:T(8,128)S(1)}, u32[]{:S(2)}, u32[]{:S(2)}) collective-permute-start(f32[256,256]{1,0:T(8,128)S(1)} %get-tuple-element.57), channel_id=1, source_target_pairs={{0,1},{1,0},{2,3},{3,2},{4,5},{5,4},{6,7},{7,6},{8,9},{9,8},{10,11... | collective-permute-start | bytes 786440 | tf_op jit(solution)/shard_map/ppermute | solution.py:187
  62.6 14.8 %all-to-all-start.2 = ((f32[32,16,128]{2,1,0:T(8,128)}), f32[32,16,128]{2,1,0:T(8,128)S(1)}, u32[]{:S(2)}, u32[]{:S(2)}) async-start(f32[32,16,128]{2,1,0:T(8,128)} %bitcast.5), calls=%async_computation.2 | async-start | bytes 524288 | tf_op jit(solution)/shard_map/all_to_all | solution.py:322
  67.2 26.5 %copy-start.1 = (f32[256,256]{1,0:T(8,128)S(1)}, f32[256,256]{1,0:T(8,128)}, u32[]{:S(2)}) copy-start(f32[256,256]{1,0:T(8,128)} %second_ref.3) | copy-start | bytes 786436
  78.2 6.1 %collective-permute-start.7 = (bf16[256,256]{1,0:T(8,128)(2,1)S(1)}, bf16[256,256]{1,0:T(8,128)(2,1)S(1)}, u32[]{:S(2)}, u32[]{:S(2)}) collective-permute-start(bf16[256,256]{1,0:T(8,128)(2,1)S(1)} %get-tuple-element.44), channel_id=1, source_target_pairs={{0,1},{1,0},{2,3},{3,2},{4,5},{5,4},{6,7},{7,6},{8,9},{9,8},{10,11... | collective-permute-start | bytes 393224 | tf_op jit(solution)/shard_map/ppermute | solution.py:187
  79.3 14.4 %collective-permute-start.9 = (bf16[256,256]{1,0:T(8,128)(2,1)S(1)}, bf16[256,256]{1,0:T(8,128)(2,1)S(1)}, u32[]{:S(2)}, u32[]{:S(2)}) collective-permute-start(bf16[256,256]{1,0:T(8,128)(2,1)S(1)} %get-tuple-element.44), channel_id=1, source_target_pairs={{0,3},{1,2},{2,1},{3,0},{4,7},{5,6},{6,5},{7,4},{8,11},{9,10},{10,... | collective-permute-start | bytes 393224 | tf_op jit(solution)/shard_map/ppermute | solution.py:187
  80.4 13.3 %collective-permute-start.8 = (bf16[256,256]{1,0:T(8,128)(2,1)S(1)}, bf16[256,256]{1,0:T(8,128)(2,1)S(1)}, u32[]{:S(2)}, u32[]{:S(2)}) collective-permute-start(bf16[256,256]{1,0:T(8,128)(2,1)S(1)} %get-tuple-element.44), channel_id=1, source_target_pairs={{0,2},{1,3},{2,0},{3,1},{4,6},{5,7},{6,4},{7,5},{8,10},{9,11},{10,... | collective-permute-start | bytes 393224 | tf_op jit(solution)/shard_map/ppermute | solution.py:187
  85.0 15.1 %all-to-all-start.4 = ((f32[32,16,128]{2,1,0:T(8,128)}), f32[32,16,128]{2,1,0:T(8,128)S(1)}, u32[]{:S(2)}, u32[]{:S(2)}) async-start(f32[32,16,128]{2,1,0:T(8,128)} %bitcast.8), calls=%async_computation.4 | async-start | bytes 524288 | tf_op jit(solution)/shard_map/all_to_all | solution.py:322
  100.1 22.0 %all-to-all-start.3 = ((f32[8,128,256]{2,1,0:T(8,128)}), f32[8,128,256]{2,1,0:T(8,128)S(1)}, u32[]{:S(2)}, u32[]{:S(2)}) async-start(f32[8,128,256]{2,1,0:T(8,128)} %bitcast.7), calls=%async_computation.3 | async-start | bytes 2097152 | tf_op jit(solution)/shard_map/all_to_all | solution.py:177
  135.6 7.0 %collective-permute-start.12 = (bf16[128,256]{1,0:T(8,128)(2,1)S(1)}, bf16[128,256]{1,0:T(8,128)(2,1)S(1)}, u32[]{:S(2)}, u32[]{:S(2)}) collective-permute-start(bf16[128,256]{1,0:T(8,128)(2,1)S(1)} %get-tuple-element.52), channel_id=1, source_target_pairs={{0,24},{4,28},{8,16},{12,20},{16,8},{20,12},{24,0},{28,4},{1,25},{... | collective-permute-start | bytes 196616 | tf_op jit(solution)/shard_map/ppermute | solution.py:187
  136.6 6.0 %collective-permute-start.11 = (bf16[128,256]{1,0:T(8,128)(2,1)S(1)}, bf16[128,256]{1,0:T(8,128)(2,1)S(1)}, u32[]{:S(2)}, u32[]{:S(2)}) collective-permute-start(bf16[128,256]{1,0:T(8,128)(2,1)S(1)} %get-tuple-element.52), channel_id=1, source_target_pairs={{0,16},{4,20},{8,24},{12,28},{16,0},{20,4},{24,8},{28,12},{1,17},{... | collective-permute-start | bytes 196616 | tf_op jit(solution)/shard_map/ppermute | solution.py:187
  138.1 4.5 %collective-permute-start.10 = (bf16[128,256]{1,0:T(8,128)(2,1)S(1)}, bf16[128,256]{1,0:T(8,128)(2,1)S(1)}, u32[]{:S(2)}, u32[]{:S(2)}) collective-permute-start(bf16[128,256]{1,0:T(8,128)(2,1)S(1)} %get-tuple-element.52), channel_id=1, source_target_pairs={{0,8},{4,12},{8,0},{12,4},{16,24},{20,28},{24,16},{28,20},{1,9},{5... | collective-permute-start | bytes 196616 | tf_op jit(solution)/shard_map/ppermute | solution.py:187
  139.9 12.9 %all-to-all-start.7 = ((f32[32,16,128]{2,1,0:T(8,128)}), f32[32,16,128]{2,1,0:T(8,128)S(1)}, u32[]{:S(2)}, u32[]{:S(2)}) async-start(f32[32,16,128]{2,1,0:T(8,128)} %bitcast.13), calls=%async_computation.7 | async-start | bytes 524288 | tf_op jit(solution)/shard_map/all_to_all | solution.py:322
  142.7 1.6 collective-permute-start.13
  152.8 16.3 %all-to-all-start.6 = ((f32[32,8,256]{2,1,0:T(8,128)}), f32[32,8,256]{2,1,0:T(8,128)S(1)}, u32[]{:S(2)}, u32[]{:S(2)}) async-start(f32[32,8,256]{2,1,0:T(8,128)} %bitcast.12), calls=%async_computation.6 | async-start | bytes 524288 | tf_op jit(solution)/shard_map/all_to_all | solution.py:177

commit v2 on v1

--- a/solution.py
+++ b/solution.py
@@ -45,32 +45,40 @@
     return pl.multiple_of(block * W, W)
 
 
-def fetch(blocks_ref, held_ref, sems, slot):
-    return pltpu.make_async_copy(blocks_ref.at[slot], held_ref.at[slot], sems.at[slot])
-
-
-def fetch_all(count, blocks_ref, held_ref, sems):
-    for slot in range(blocks_ref.shape[0]):
+def fetch(source_ref, source, held_ref, sems, slot):
+    return pltpu.make_async_copy(source_ref.at[source], held_ref.at[slot], sems.at[slot])
+
+
+def fetch_all(count, block_refs, first, held_ref, sems):
+    each = block_refs[0].shape[0]
+    for slot in range(held_ref.shape[0]):
 
         @pl.when(slot < count)
         def _():
-            fetch(blocks_ref, held_ref, sems, slot).start()
-
-
-def moments_kernel(
-    mode, orders, count_ref, coords_ref, blocks_ref, first_ref, second_ref, out_ref, held_ref, sems, order_ref
-):
+            fetch(block_refs[slot // each], first + slot % each, held_ref, sems, slot).start()
+
+
+def moments_kernel(mode, orders, arrays, count_ref, coords_ref, *refs):
+    block_refs, refs = refs[:arrays], refs[arrays:]
+    first_ref, second_ref, out_ref, held_ref, sems, order_ref = refs[:6]
     rank = out_ref.shape[1]
     count = count_ref[0, 0]
-    fetch_all(count, blocks_ref, held_ref, sems)
+    if len(refs) > 6:
+        months_ref, month_sem = refs[6:]
+        months = pltpu.make_async_copy(second_ref, months_ref, month_sem)
+        months.start()
+        second_ref = months_ref
+    fetch_all(count, block_refs, 0, held_ref, sems)
     out_ref[...] = jnp.zeros_like(out_ref)
+    if len(refs) > 6:
+        months.wait()
     spread_mode, tile_mode = ((1, 2), (0, 2), (1, 0))[mode]
 
     def add_block(slot, carry):
         first = first_ref[pl.ds(slot_rows(coords_ref, slot, spread_mode, orders[0]), W), :].astype(F32)
         second = second_ref[pl.ds(slot_rows(coords_ref, slot, tile_mode, orders[1]), W), :].astype(BF16).reshape(4, 16, rank)
         target = slot_rows(coords_ref, slot, mode, orders[2])
-        fetch(blocks_ref, held_ref, sems, slot).wait()
+        fetch(block_refs[0], 0, held_ref, sems, slot).wait()
         total = jnp.zeros((W, rank), F32)
         for step in range(W // GROUP):
             left = held_ref[slot, :, step * GROUP * W : (step + 1) * GROUP * W]
@@ -97,32 +105,39 @@
 
 
 def block_moments(mode, orders, blocks, coords, count, first, second, out_rows):
-    slots = blocks.shape[0]
+    slots = sum(part.shape[0] for part in blocks)
+    shape = (slots, *blocks[0].shape[1:])
     rank = first.shape[1]
-    return pl.pallas_call(
-        functools.partial(moments_kernel, mode, orders),
-        in_specs=[SMEM_SPEC, SMEM_SPEC, HBM_SPEC, VMEM_SPEC, VMEM_SPEC],
+    in_hbm = lambda array: pltpu.with_memory_space_constraint(array, pltpu.HBM)
+    scratch = [
+        pltpu.VMEM(shape, BF16),
+        pltpu.SemaphoreType.DMA((slots,)),
+        pltpu.VMEM((rank // LANES, W, LANES), F32),
+    ]
+    second_spec = VMEM_SPEC
+    if mode < 2:
+        second, second_spec = in_hbm(second), HBM_SPEC
+        scratch += [pltpu.VMEM(second.shape, second.dtype), pltpu.SemaphoreType.DMA]
+    return pl.pallas_call(
+        functools.partial(moments_kernel, mode, orders, len(blocks)),
+        in_specs=[SMEM_SPEC, SMEM_SPEC] + [HBM_SPEC] * len(blocks) + [VMEM_SPEC, second_spec],
         out_specs=VMEM_SPEC,
         out_shape=jax.ShapeDtypeStruct((out_rows, rank), F32),
-        scratch_shapes=[
-            pltpu.VMEM(blocks.shape, BF16),
-            pltpu.SemaphoreType.DMA((slots,)),
-            pltpu.VMEM((rank // LANES, W, LANES), F32),
-        ],
+        scratch_shapes=scratch,
         compiler_params=pltpu.CompilerParams(vmem_limit_bytes=18 << 20),
         cost_estimate=pl.CostEstimate(
-            flops=2 * slots * W**3 * rank, bytes_accessed=blocks.size * 2, transcendentals=0
+            flops=2 * slots * W**3 * rank, bytes_accessed=slots * W**3 * 2, transcendentals=0
         ),
-    )(count, coords, pltpu.with_memory_space_constraint(blocks, pltpu.HBM), first, second)
-
-
-def turn_kernel(mode, count_ref, blocks_ref, out_ref, held_ref, turned_ref, in_sems, out_sems, lanes_ref):
-    count = count_ref[0, 0]
-    fetch_all(count, blocks_ref, held_ref, in_sems)
+    )(count, coords, *[in_hbm(part) for part in blocks], first, second)
+
+
+def turn_kernel(mode, first, count_ref, blocks_ref, out_ref, held_ref, turned_ref, in_sems, out_sems, lanes_ref):
+    count = jnp.clip(count_ref[0, 0] - first, 0, held_ref.shape[0])
+    fetch_all(count, [blocks_ref], first, held_ref, in_sems)
     columns = W * W // LANES
 
     def turn(slot, carry):
-        fetch(blocks_ref, held_ref, in_sems, slot).wait()
+        fetch(blocks_ref, 0, held_ref, in_sems, slot).wait()
         if mode == 1:
             for column in range(columns):
                 lanes_ref[pl.ds(column, W, stride=STRIDE), :] = held_ref[
@@ -141,34 +156,35 @@
                 turned_ref[slot, :, pair * LANES : (pair + 1) * LANES] = jnp.concatenate(
                     [turned[:W], turned[W:]], 1
                 )
-        fetch(turned_ref, out_ref, out_sems, slot).start()
+        fetch(turned_ref, slot, out_ref, out_sems, slot).start()
         return carry
 
     lax.fori_loop(0, count, turn, 0)
 
     def finish(slot, carry):
-        fetch(turned_ref, out_ref, out_sems, slot).wait()
+        fetch(turned_ref, slot, out_ref, out_sems, slot).wait()
         return carry
 
     lax.fori_loop(0, count, finish, 0)
 
 
-def turned_blocks(mode, blocks, count):
-    slots = blocks.shape[0]
-    return pl.pallas_call(
-        functools.partial(turn_kernel, mode),
+def turned_blocks(mode, blocks, count, half):
+    slots = blocks.shape[0] // 2
+    shape = (slots, *blocks.shape[1:])
+    return pl.pallas_call(
+        functools.partial(turn_kernel, mode, half * slots),
         in_specs=[SMEM_SPEC, HBM_SPEC],
         out_specs=HBM_SPEC,
-        out_shape=pltpu.HBM(blocks.shape, blocks.dtype),
+        out_shape=pltpu.HBM(shape, blocks.dtype),
         scratch_shapes=[
-            pltpu.VMEM(blocks.shape, BF16),
-            pltpu.VMEM(blocks.shape, BF16),
+            pltpu.VMEM(shape, BF16),
+            pltpu.VMEM(shape, BF16),
             pltpu.SemaphoreType.DMA((slots,)),
             pltpu.SemaphoreType.DMA((slots,)),
             pltpu.VMEM((W * STRIDE, LANES), F32),
         ],
-        compiler_params=pltpu.CompilerParams(vmem_limit_bytes=24 << 20),
-        cost_estimate=pl.CostEstimate(flops=0, bytes_accessed=blocks.size * 8, transcendentals=0),
+        compiler_params=pltpu.CompilerParams(vmem_limit_bytes=14 << 20),
+        cost_estimate=pl.CostEstimate(flops=0, bytes_accessed=blocks.size * 4, transcendentals=0),
     )(count, pltpu.with_memory_space_constraint(blocks, pltpu.HBM))
 
 
@@ -478,23 +494,25 @@
     ones = jnp.ones((1, c_init.shape[1]), F32)
     b_rounded, b_held = lax.optimization_barrier((b_init.astype(BF16), b_init))
     term_panel = swap_gather(b_rounded, "slab")
-    messages_b = swap_all(gram_message(b_held, devices))
+    held_blocks, term_panel = lax.optimization_barrier((local_blocks, term_panel))
+    terms_one = turned_blocks(1, held_blocks, counts, 0)
+    messages_b, terms_one = lax.optimization_barrier((swap_all(gram_message(b_held, devices)), terms_one))
     spread_b, term_panel = lax.optimization_barrier((fold(messages_b, devices), term_panel))
     gram_b = (swap_all(spread_b), term_total, ones)
     moments_a = block_moments(
-        0, (TERM_ORDER, None, DOC_ORDER), local_blocks, coords, counts, term_panel, c_init, doc_rows
+        0, (TERM_ORDER, None, DOC_ORDER), [local_blocks], coords, counts, term_panel, c_init, doc_rows
     )
     others_a = swap_pieces(moments_a, "grid")
     c_held, _ = lax.optimization_barrier((c_init, moments_a))
     gram_c = (gram_local(c_held), month_total, ones)
     inverse_a = product_inverse(gram_b, gram_c, devices)
-    blocks_b, inverse_a = lax.optimization_barrier((local_blocks, inverse_a))
-    blocks_b = turned_blocks(1, blocks_b, counts)
-    inverse_a, blocks_b = lax.optimization_barrier((inverse_a, blocks_b))
+    held_blocks, inverse_a = lax.optimization_barrier((local_blocks, inverse_a))
+    terms_two = turned_blocks(1, held_blocks, counts, 1)
+    inverse_a, terms_two = lax.optimization_barrier((inverse_a, terms_two))
     raw_a, messages_a = solve_swapped(moments_a, others_a, inverse_a, devices)
-    blocks_c, messages_a = lax.optimization_barrier((local_blocks, messages_a))
-    blocks_c = turned_blocks(2, blocks_c, counts)
-    messages_a, blocks_c = lax.optimization_barrier((swap_all(messages_a), blocks_c))
+    held_blocks, messages_a = lax.optimization_barrier((local_blocks, messages_a))
+    months_one = turned_blocks(2, held_blocks, counts, 0)
+    messages_a, months_one = lax.optimization_barrier((swap_all(messages_a), months_one))
     factor_a, rounded_a, scale_a = scale_rows(messages_a, raw_a, doc_total, devices)
     pieces = [rounded_a] + [swap(rounded_a, "grid", k) for k in range(1, grid_count)]
     messages_a, pieces[1] = lax.optimization_barrier((messages_a, pieces[1]))
@@ -503,12 +521,14 @@
     gram_a = (swap_all(spread_a), doc_total, scale_a)
 
     moments_b = block_moments(
-        1, (DOC_ORDER, None, None), blocks_b, coords, counts, doc_panel, c_init, term_rows
+        1, (DOC_ORDER, None, None), [terms_one, terms_two], coords, counts, doc_panel, c_init, term_rows
     )
     parts_b = exchange(moments_b, "slab")
     inverse_b = product_inverse(gram_a, gram_c, devices)
     raw_b, messages_n = solve_stacked(parts_b, inverse_b, devices, True)
-    messages_n = swap_all(messages_n)
+    held_blocks, messages_n = lax.optimization_barrier((local_blocks, messages_n))
+    months_two = turned_blocks(2, held_blocks, counts, 1)
+    messages_n, months_two = lax.optimization_barrier((swap_all(messages_n), months_two))
     factor_b, rounded_b, scale_b = scale_rows(messages_n, raw_b, term_total, devices)
     term_panel_new = swap_gather(rounded_b, "slab")
     messages_n, _ = lax.optimization_barrier((messages_n, rounded_b))
@@ -516,7 +536,7 @@
     gram_bn = (swap_all(spread_n), term_total, scale_b)
 
     moments_c = block_moments(
-        2, (TERM_ORDER, DOC_ORDER, None), blocks_c, coords, counts, term_panel_new, doc_panel, month_total
+        2, (TERM_ORDER, DOC_ORDER, None), [months_one, months_two], coords, counts, term_panel_new, doc_panel, month_total
     )
     parts_c = exchange(moments_c, BOTH)
     inverse_c = product_inverse(gram_a, gram_bn, devices)

time: 187 us -> 191 us (1.021)
  Pallas kernels: 66.3 us -> 80.5 us
  blocking collectives: 27.7 us -> 15.6 us
  waiting for transfers between devices: 35.2 us -> 40.9 us
  starting transfers between devices: 50 us -> 47.9 us
    pallas_call x5 -> x7, Pallas kernels: 25.4 us -> 38.9 us  [the longest x3 23.6 us: block_moments(): pl.pallas_call(functools.partial(moments_kernel, mode, orders, len(blocks...]
    all_to_all x1 -> x0, blocking collectives: 11.9 us -> none  [swap_all(): lax.all_to_all(messages, BOTH, split_axis=0, concat_axis=0, tiled=True)]
    ppermute x14, waiting for transfers between devices: 15.1 us -> 20.8 us  [swap(): lax.ppermute(rows, axis, [(i, i ^ step) for i in range(lax.axis_size(axis...]
    all_to_all x2, starting transfers between devices: 11.8 us -> 9.23 us  [exchange(): parts = lax.all_to_all(rows, axes, split_axis=0, concat_axis=0, tiled=True)]
    all_to_all x5 -> x6, starting transfers between devices: 21.2 us -> 22 us  [swap_all(): lax.all_to_all(messages, BOTH, split_axis=0, concat_axis=0, tiled=True)]
    all_to_all x5 -> x6, waiting for transfers between devices: 15.6 us -> 15.9 us  [swap_all(): lax.all_to_all(messages, BOTH, split_axis=0, concat_axis=0, tiled=True)]
  transfers between devices with their start and end apart: 21 -> 22, of which waited for: 10 -> 10; matrix products, arithmetic and copies ran while one was open for 1% -> 1% of each run, Pallas kernels for 33% -> 39%
where the time goes in v2:
time: 191 us
  Pallas kernels  80.5 us (42%)
  starting transfers between devices  47.9 us (25%)
  waiting for transfers between devices  40.9 us (21%)
  blocking collectives  15.6 us (8%)
    pallas_call x3, Pallas kernels, product_inverse(): pl.pallas_call(functools.partial(inverse_kernel, devices, (one[1], two[1]...  33 us
    pallas_call x3, Pallas kernels, block_moments(): pl.pallas_call(functools.partial(moments_kernel, mode, orders, len(blocks...  23.6 us
    all_to_all x6, starting transfers between devices, swap_all(): lax.all_to_all(messages, BOTH, split_axis=0, concat_axis=0, tiled=True)  22 us
    ppermute x14, waiting for transfers between devices, swap(): lax.ppermute(rows, axis, [(i, i ^ step) for i in range(lax.axis_size(axis...  20.8 us
    ppermute x14, starting transfers between devices, swap(): lax.ppermute(rows, axis, [(i, i ^ step) for i in range(lax.axis_size(axis...  16.7 us
    all_to_all x6, waiting for transfers between devices, swap_all(): lax.all_to_all(messages, BOTH, split_axis=0, concat_axis=0, tiled=True)  15.9 us
    all_to_all x1, blocking collectives, spread_rows(): lax.all_to_all(jnp.tile(rows, (devices, 1)), axes, split_axis=0, concat_a...  15.6 us
    pallas_call x4, Pallas kernels, turned_blocks(): pl.pallas_call(functools.partial(turn_kernel, mode, half * slots), in_spe...  15.3 us
  transfers between devices with their start and end apart: 22, of which 10 were waited for; matrix products, arithmetic and copies ran while one was open for 1% of the time, Pallas kernels for 39%

profile of v2, /device:TPU:0, one launch (start us, length us, event | category | flops | bytes accessed | tf_op | source)
XLA Modules:
  0.0 190.7 jit_solution(10712207567410175799)
XLA Ops:
  0.6 0.9 convert_element_type.3
  1.5 4.0 %collective-permute-start.2 = (bf16[128,256]{1,0:T(8,128)(2,1)S(1)}, bf16[128,256]{1,0:T(8,128)(2,1)S(1)}, u32[]{:S(2)}, u32[]{:S(2)}) collective-permute-start(bf16[128,256]{1,0:T(8,128)(2,1)S(1)} %convert_element_type.3), channel_id=1, source_target_pairs={{0,24},{4,28},{8,16},{12,20},{16,8},{20,12},{24,0},{28,4},{1,25},{... | collective-permute-start | bytes 196616 | tf_op jit(solution)/shard_map/ppermute | solution.py:203
  5.5 0.5 collective-permute-start.1
  6.0 0.1 collective-permute-start
  6.1 0.9 copy-done
  7.0 1.1 shard_map.76
  8.2 6.2 %all-to-all-start = ((f32[32,16,128]{2,1,0:T(8,128)}), f32[32,16,128]{2,1,0:T(8,128)S(1)}, u32[]{:S(2)}, u32[]{:S(2)}) async-start(f32[32,16,128]{2,1,0:T(8,128)} %bitcast.1), calls=%async_computation | async-start | bytes 524288 | tf_op jit(solution)/shard_map/all_to_all | solution.py:338
  15.1 0.8 copy.8.coords_ref
  15.8 0.0 collective-permute-done.2
  15.9 0.0 collective-permute-done
  15.9 0.3 collective-permute-start.3
  16.2 1.3 collective-permute-done.3
  17.5 4.5 %shard_map.77.refs_0_ = bf16[8,64,4096]{2,1,0:T(8,128)(2,1)} custom-call(s32[1,1]{1,0:T(1,128)S(6)} %copy.22.count_ref, bf16[16,64,4096]{2,1,0:T(8,128)(2,1)} %bitcast.28), custom_call_target="tpu_custom_call" | custom-call | bytes 16777216 | tf_op jit(solution)/shard_map/pallas_call | solution.py:174
  22.1 2.6 %all-to-all-done = f32[32,16,128]{2,1,0:T(8,128)S(1)} async-done(((f32[32,16,128]{2,1,0:T(8,128)}), f32[32,16,128]{2,1,0:T(8,128)S(1)}, u32[]{:S(2)}, u32[]{:S(2)}) %all-to-all-start) | async-done | bytes 262176 | tf_op jit(solution)/shard_map/all_to_all | solution.py:338
  24.6 0.8 shard_map.78
  25.4 3.3 %all-to-all-start.1 = ((f32[32,16,128]{2,1,0:T(8,128)}), f32[32,16,128]{2,1,0:T(8,128)S(1)}, u32[]{:S(2)}, u32[]{:S(2)}) async-start(f32[32,16,128]{2,1,0:T(8,128)} %bitcast.3), calls=%async_computation.1 | async-start | bytes 524288 | tf_op jit(solution)/shard_map/all_to_all | solution.py:338
  28.7 0.0 copy-start.1
  28.7 7.7 %shard_map.79.refs_0_ = f32[1024,256]{1,0:T(8,128)S(1)} custom-call(s32[1,1]{1,0:T(1,128)S(6)} %copy.22.count_ref, s32[1,1,16,3]{3,2,1,0:T(8,128)S(1)} %copy.8.coords_ref, bf16[16,64,4096]{2,1,0:T(8,128)(2,1)} %bitcast.29, bf16[1024,256]{1,0:T(8,128)(2,1)S(1)} %constant_dynamic-update-slice_fusion.refs_1_, f32[256,256]{1,0:T(8,128)} %refs_3_.1), custom_call_target="tpu_custom_call" | custom-call | flops 2147483648 | bytes 8388608 | tf_op jit(solution)/shard_map/pallas_call | solution.py:121
  36.4 0.1 fusion
  36.5 3.7 %collective-permute-start.6 = (f32[256,256]{1,0:T(8,128)S(1)}, f32[256,256]{1,0:T(8,128)S(1)}, u32[]{:S(2)}, u32[]{:S(2)}) collective-permute-start(f32[256,256]{1,0:T(8,128)S(1)} %get-tuple-element.71), channel_id=1, source_target_pairs={{0,3},{1,2},{2,1},{3,0},{4,7},{5,6},{6,5},{7,4},{8,11},{9,10},{10,... | collective-permute-start | bytes 786440 | tf_op jit(solution)/shard_map/ppermute | solution.py:203
  40.2 0.8 collective-permute-start.4
  40.9 0.6 fusion.1.two_ref
  41.5 0.0 all-to-all-done.1
  41.6 11.0 %shard_map.80.refs_4_ = f32[256,256]{1,0:T(8,128)S(1)} custom-call(f32[512,128]{1,0:T(8,128)S(1)} %bitcast.27, f32[1,256]{1,0:T(1,128)S(1)} %broadcast_in_dim.4.one_scale_ref.two_scale_ref, f32[256,256]{1,0:T(8,128)S(1)} %fusion.1.two_ref, f32[1,256]{1,0:T(1,128)S(1)} %broadcast_in_dim.4.one_scale_ref.two_scale_ref), custom_call_target="tpu_custom_call" | custom-call | flops 10000000000 | bytes 786432 | tf_op jit(solution)/shard_map/pallas_call | solution.py:413
  52.5 2.3 %shard_map.81.refs_1_ = bf16[8,64,4096]{2,1,0:T(8,128)(2,1)} custom-call(s32[1,1]{1,0:T(1,128)S(6)} %copy.22.count_ref, bf16[16,64,4096]{2,1,0:T(8,128)(2,1)} %bitcast.30), custom_call_target="tpu_custom_call" | custom-call | bytes 16777216 | tf_op jit(solution)/shard_map/pallas_call | solution.py:174
  54.9 0.0 collective-permute-done.6.refs_3_
  54.9 6.5 %collective-permute-done.5.refs_2_ = f32[256,256]{1,0:T(8,128)S(1)} collective-permute-done((f32[256,256]{1,0:T(8,128)S(1)}, f32[256,256]{1,0:T(8,128)S(1)}, u32[]{:S(2)}, u32[]{:S(2)}) %collective-permute-start.5) | collective-permute-done | bytes 262176 | tf_op jit(solution)/shard_map/ppermute | solution.py:203
  61.4 1.9 shard_map.82
  63.2 4.2 %all-to-all-start.2 = ((f32[32,16,128]{2,1,0:T(8,128)}), f32[32,16,128]{2,1,0:T(8,128)S(1)}, u32[]{:S(2)}, u32[]{:S(2)}) async-start(f32[32,16,128]{2,1,0:T(8,128)} %bitcast.5), calls=%async_computation.2 | async-start | bytes 524288 | tf_op jit(solution)/shard_map/all_to_all | solution.py:338
  67.5 5.9 %shard_map.83.refs_0_ = bf16[8,64,4096]{2,1,0:T(8,128)(2,1)} custom-call(s32[1,1]{1,0:T(1,128)S(6)} %copy.22.count_ref, bf16[16,64,4096]{2,1,0:T(8,128)(2,1)} %bitcast.31), custom_call_target="tpu_custom_call" | custom-call | bytes 16777216 | tf_op jit(solution)/shard_map/pallas_call | solution.py:174
  73.4 4.2 %all-to-all-done.2 = f32[32,16,128]{2,1,0:T(8,128)S(1)} async-done(((f32[32,16,128]{2,1,0:T(8,128)}), f32[32,16,128]{2,1,0:T(8,128)S(1)}, u32[]{:S(2)}, u32[]{:S(2)}) %all-to-all-start.2) | async-done | bytes 262176 | tf_op jit(solution)/shard_map/all_to_all | solution.py:338
  77.7 0.8 shard_map.84
  78.4 1.1 collective-permute-start.7
  79.5 1.1 collective-permute-start.9
  80.7 1.3 collective-permute-start.8
  81.9 2.6 %collective-permute-done.7 = bf16[256,256]{1,0:T(8,128)(2,1)S(1)} collective-permute-done((bf16[256,256]{1,0:T(8,128)(2,1)S(1)}, bf16[256,256]{1,0:T(8,128)(2,1)S(1)}, u32[]{:S(2)}, u32[]{:S(2)}) %collective-permute-start.7) | collective-permute-done | bytes 131104 | tf_op jit(solution)/shard_map/ppermute | solution.py:203
  84.5 0.8 shard_map.86
  85.3 3.0 %all-to-all-start.4 = ((f32[32,16,128]{2,1,0:T(8,128)}), f32[32,16,128]{2,1,0:T(8,128)S(1)}, u32[]{:S(2)}, u32[]{:S(2)}) async-start(f32[32,16,128]{2,1,0:T(8,128)} %bitcast.8), calls=%async_computation.4 | async-start | bytes 524288 | tf_op jit(solution)/shard_map/all_to_all | solution.py:338
  88.3 9.2 %collective-permute-done.8 = bf16[256,256]{1,0:T(8,128)(2,1)S(1)} collective-permute-done((bf16[256,256]{1,0:T(8,128)(2,1)S(1)}, bf16[256,256]{1,0:T(8,128)(2,1)S(1)}, u32[]{:S(2)}, u32[]{:S(2)}) %collective-permute-start.8) | collective-permute-done | bytes 131104 | tf_op jit(solution)/shard_map/ppermute | solution.py:203
  97.6 8.7 %shard_map.85 = f32[1024,256]{1,0:T(8,128)} custom-call(s32[1,1]{1,0:T(1,128)S(6)} %copy.22.count_ref, s32[1,1,16,3]{3,2,1,0:T(8,128)S(1)} %copy.8.coords_ref, bf16[8,64,4096]{2,1,0:T(8,128)(2,1)} %shard_map.77.refs_0_, bf16[8,64,4096]{2,1,0:T(8,128)(2,1)} %shard_map.81.refs_1_, bf16[1024,256]{1,0:T(8,128)(2,1)S(1)} %constant_dynamic-update-slice_fusion.5.refs_2_.refs_3_, ...), custom_call_target="tpu_custom_call" | custom-call | flops 2147483648 | bytes 8388608 | tf_op jit(solution)/shard_map/pallas_call | solution.py:121
  106.3 0.0 all-to-all-done.4
  106.3 3.7 %all-to-all-start.3 = ((f32[8,128,256]{2,1,0:T(8,128)}), f32[8,128,256]{2,1,0:T(8,128)S(1)}, u32[]{:S(2)}, u32[]{:S(2)}) async-start(f32[8,128,256]{2,1,0:T(8,128)} %bitcast.7), calls=%async_computation.3 | async-start | bytes 2097152 | tf_op jit(solution)/shard_map/all_to_all | solution.py:193
  110.0 11.0 %shard_map.87.refs_1_ = f32[256,256]{1,0:T(8,128)S(1)} custom-call(f32[512,128]{1,0:T(8,128)S(1)} %bitcast.24, f32[1,256]{1,0:T(1,128)S(1)} %get-tuple-element.59.one_scale_ref, f32[256,256]{1,0:T(8,128)S(1)} %fusion.1.two_ref, f32[1,256]{1,0:T(1,128)S(1)} %broadcast_in_dim.4.one_scale_ref.two_scale_ref), custom_call_target="tpu_custom_call" | custom-call | flops 10000000000 | bytes 786432 | tf_op jit(solution)/shard_map/pallas_call | solution.py:413
  121.0 4.2 %all-to-all-done.3.refs_0_ = f32[8,128,256]{2,1,0:T(8,128)S(1)} async-done(((f32[8,128,256]{2,1,0:T(8,128)}), f32[8,128,256]{2,1,0:T(8,128)S(1)}, u32[]{:S(2)}, u32[]{:S(2)}) %all-to-all-start.3) | async-done | bytes 1048608 | tf_op jit(solution)/shard_map/all_to_all | solution.py:193
  125.2 1.6 shard_map.88
  126.8 2.6 %all-to-all-start.5 = ((f32[32,16,128]{2,1,0:T(8,128)}), f32[32,16,128]{2,1,0:T(8,128)S(1)}, u32[]{:S(2)}, u32[]{:S(2)}) async-start(f32[32,16,128]{2,1,0:T(8,128)} %bitcast.10), calls=%async_computation.5 | async-start | bytes 524288 | tf_op jit(solution)/shard_map/all_to_all | solution.py:338
  129.4 2.5 %shard_map.89.refs_1_ = bf16[8,64,4096]{2,1,0:T(8,128)(2,1)} custom-call(s32[1,1]{1,0:T(1,128)S(6)} %copy.22.count_ref, bf16[16,64,4096]{2,1,0:T(8,128)(2,1)} %bitcast.32), custom_call_target="tpu_custom_call" | custom-call | bytes 16777216 | tf_op jit(solution)/shard_map/pallas_call | solution.py:174
  131.9 7.7 %all-to-all-done.5 = f32[32,16,128]{2,1,0:T(8,128)S(1)} async-done(((f32[32,16,128]{2,1,0:T(8,128)}), f32[32,16,128]{2,1,0:T(8,128)S(1)}, u32[]{:S(2)}, u32[]{:S(2)}) %all-to-all-start.5) | async-done | bytes 262176 | tf_op jit(solution)/shard_map/all_to_all | solution.py:338
  139.6 0.7 shard_map.90
  140.3 1.0 collective-permute-start.12
  141.3 1.5 collective-permute-start.11
  142.8 1.0 collective-permute-start.10
  143.8 0.8 shard_map.92
  144.6 2.7 %all-to-all-start.7 = ((f32[32,16,128]{2,1,0:T(8,128)}), f32[32,16,128]{2,1,0:T(8,128)S(1)}, u32[]{:S(2)}, u32[]{:S(2)}) async-start(f32[32,16,128]{2,1,0:T(8,128)} %bitcast.13), calls=%async_computation.7 | async-start | bytes 524288 | tf_op jit(solution)/shard_map/all_to_all | solution.py:338
  147.3 0.0 collective-permute-done.11
  147.3 0.3 collective-permute-start.13
  147.7 1.3 collective-permute-done.13
  149.0 7.1 %shard_map.91 = f32[256,256]{1,0:T(8,128)} custom-call(s32[1,1]{1,0:T(1,128)S(6)} %copy.22.count_ref, s32[1,1,16,3]{3,2,1,0:T(8,128)S(1)} %copy.8.coords_ref, bf16[8,64,4096]{2,1,0:T(8,128)(2,1)} %shard_map.83.refs_0_, bf16[8,64,4096]{2,1,0:T(8,128)(2,1)} %shard_map.89.refs_1_, bf16[1024,256]{1,0:T(8,128)(2,1)S(1)} %constant_dynamic-update-slice_fusion.9.refs_2_, ...), custom_call_target="tpu_custom_call" | custom-call | flops 2147483648 | bytes 8388608 | tf_op jit(solution)/shard_map/pallas_call | solution.py:121
  156.1 1.4 all-to-all-done.7
  157.5 5.5 %all-to-all-start.6 = ((f32[32,8,256]{2,1,0:T(8,128)}), f32[32,8,256]{2,1,0:T(8,128)S(1)}, u32[]{:S(2)}, u32[]{:S(2)}) async-start(f32[32,8,256]{2,1,0:T(8,128)} %bitcast.12), calls=%async_computation.6 | async-start | bytes 524288 | tf_op jit(solution)/shard_map/all_to_all | solution.py:193
  162.9 11.0 %shard_map.93.refs_1_ = f32[256,256]{1,0:T(8,128)S(1)} custom-call(f32[512,128]{1,0:T(8,128)S(1)} %bitcast.25, f32[1,256]{1,0:T(1,128)S(1)} %get-tuple-element.59.one_scale_ref, f32[512,128]{1,0:T(8,128)S(1)} %bitcast.26, f32[1,256]{1,0:T(1,128)S(1)} %get-tuple-element.70.two_scale_ref), custom_call_target="tpu_custom_call" | custom-call | flops 10000000000 | bytes 786432 | tf_op jit(solution)/shard_map/pallas_call | solution.py:413
  174.0 0.2 shard_map.94
  174.3 15.6 %all_to_all.96 = f32[32,8,256]{2,1,0:T(8,128)S(1)} all-to-all(f32[32,8,256]{2,1,0:T(8,128)S(1)} %tile.2), channel_id=1, replica_groups=mesh['slab'=8,'grid'=4] {'slab','grid'}, dimensions={0} | all-to-all | bytes 524288 | tf_op jit(solution)/shard_map/all_to_all | solution.py:199
  190.0 0.7 bitcast_divide_fusion
  (29 shorter events, 0.3 us)
Async XLA Ops:
  1.5 14.3 %collective-permute-start.2 = (bf16[128,256]{1,0:T(8,128)(2,1)S(1)}, bf16[128,256]{1,0:T(8,128)(2,1)S(1)}, u32[]{:S(2)}, u32[]{:S(2)}) collective-permute-start(bf16[128,256]{1,0:T(8,128)(2,1)S(1)} %convert_element_type.3), channel_id=1, source_target_pairs={{0,24},{4,28},{8,16},{12,20},{16,8},{20,12},{24,0},{28,4},{1,25},{... | collective-permute-start | bytes 196616 | tf_op jit(solution)/shard_map/ppermute | solution.py:203
  5.5 10.4 %collective-permute-start.1 = (bf16[128,256]{1,0:T(8,128)(2,1)S(1)}, bf16[128,256]{1,0:T(8,128)(2,1)S(1)}, u32[]{:S(2)}, u32[]{:S(2)}) collective-permute-start(bf16[128,256]{1,0:T(8,128)(2,1)S(1)} %convert_element_type.3), channel_id=1, source_target_pairs={{0,16},{4,20},{8,24},{12,28},{16,0},{20,4},{24,8},{28,12},{1,17},{... | collective-permute-start | bytes 196616 | tf_op jit(solution)/shard_map/ppermute | solution.py:203
  6.0 9.9 %collective-permute-start = (bf16[128,256]{1,0:T(8,128)(2,1)S(1)}, bf16[128,256]{1,0:T(8,128)(2,1)S(1)}, u32[]{:S(2)}, u32[]{:S(2)}) collective-permute-start(bf16[128,256]{1,0:T(8,128)(2,1)S(1)} %convert_element_type.3), channel_id=1, source_target_pairs={{0,8},{4,12},{8,0},{12,4},{16,24},{20,28},{24,16},{28,20},{1,9},{5... | collective-permute-start | bytes 196616 | tf_op jit(solution)/shard_map/ppermute | solution.py:203
  6.1 0.9 copy-start
  8.2 16.4 %all-to-all-start = ((f32[32,16,128]{2,1,0:T(8,128)}), f32[32,16,128]{2,1,0:T(8,128)S(1)}, u32[]{:S(2)}, u32[]{:S(2)}) async-start(f32[32,16,128]{2,1,0:T(8,128)} %bitcast.1), calls=%async_computation | async-start | bytes 524288 | tf_op jit(solution)/shard_map/all_to_all | solution.py:338
  15.9 1.6 collective-permute-start.3
  25.4 16.2 %all-to-all-start.1 = ((f32[32,16,128]{2,1,0:T(8,128)}), f32[32,16,128]{2,1,0:T(8,128)S(1)}, u32[]{:S(2)}, u32[]{:S(2)}) async-start(f32[32,16,128]{2,1,0:T(8,128)} %bitcast.3), calls=%async_computation.1 | async-start | bytes 524288 | tf_op jit(solution)/shard_map/all_to_all | solution.py:338
  28.7 12.3 %copy-start.1 = (f32[256,256]{1,0:T(8,128)S(1)}, f32[256,256]{1,0:T(8,128)}, u32[]{:S(2)}) copy-start(f32[256,256]{1,0:T(8,128)} %refs_3_.1) | copy-start | bytes 786436
  36.5 18.4 %collective-permute-start.6 = (f32[256,256]{1,0:T(8,128)S(1)}, f32[256,256]{1,0:T(8,128)S(1)}, u32[]{:S(2)}, u32[]{:S(2)}) collective-permute-start(f32[256,256]{1,0:T(8,128)S(1)} %get-tuple-element.71), channel_id=1, source_target_pairs={{0,3},{1,2},{2,1},{3,0},{4,7},{5,6},{6,5},{7,4},{8,11},{9,10},{10,... | collective-permute-start | bytes 786440 | tf_op jit(solution)/shard_map/ppermute | solution.py:203
  40.2 21.2 %collective-permute-start.5 = (f32[256,256]{1,0:T(8,128)S(1)}, f32[256,256]{1,0:T(8,128)S(1)}, u32[]{:S(2)}, u32[]{:S(2)}) collective-permute-start(f32[256,256]{1,0:T(8,128)S(1)} %get-tuple-element.72), channel_id=1, source_target_pairs={{0,2},{1,3},{2,0},{3,1},{4,6},{5,7},{6,4},{7,5},{8,10},{9,11},{10,... | collective-permute-start | bytes 786440 | tf_op jit(solution)/shard_map/ppermute | solution.py:203
  40.2 21.2 %collective-permute-start.4 = (f32[256,256]{1,0:T(8,128)S(1)}, f32[256,256]{1,0:T(8,128)S(1)}, u32[]{:S(2)}, u32[]{:S(2)}) collective-permute-start(f32[256,256]{1,0:T(8,128)S(1)} %get-tuple-element.73), channel_id=1, source_target_pairs={{0,1},{1,0},{2,3},{3,2},{4,5},{5,4},{6,7},{7,6},{8,9},{9,8},{10,11... | collective-permute-start | bytes 786440 | tf_op jit(solution)/shard_map/ppermute | solution.py:203
  63.2 14.4 %all-to-all-start.2 = ((f32[32,16,128]{2,1,0:T(8,128)}), f32[32,16,128]{2,1,0:T(8,128)S(1)}, u32[]{:S(2)}, u32[]{:S(2)}) async-start(f32[32,16,128]{2,1,0:T(8,128)} %bitcast.5), calls=%async_computation.2 | async-start | bytes 524288 | tf_op jit(solution)/shard_map/all_to_all | solution.py:338
  78.4 6.1 %collective-permute-start.7 = (bf16[256,256]{1,0:T(8,128)(2,1)S(1)}, bf16[256,256]{1,0:T(8,128)(2,1)S(1)}, u32[]{:S(2)}, u32[]{:S(2)}) collective-permute-start(bf16[256,256]{1,0:T(8,128)(2,1)S(1)} %get-tuple-element.56), channel_id=1, source_target_pairs={{0,1},{1,0},{2,3},{3,2},{4,5},{5,4},{6,7},{7,6},{8,9},{9,8},{10,11... | collective-permute-start | bytes 393224 | tf_op jit(solution)/shard_map/ppermute | solution.py:203
  79.5 18.0 %collective-permute-start.9 = (bf16[256,256]{1,0:T(8,128)(2,1)S(1)}, bf16[256,256]{1,0:T(8,128)(2,1)S(1)}, u32[]{:S(2)}, u32[]{:S(2)}) collective-permute-start(bf16[256,256]{1,0:T(8,128)(2,1)S(1)} %get-tuple-element.56), channel_id=1, source_target_pairs={{0,3},{1,2},{2,1},{3,0},{4,7},{5,6},{6,5},{7,4},{8,11},{9,10},{10,... | collective-permute-start | bytes 393224 | tf_op jit(solution)/shard_map/ppermute | solution.py:203
  80.7 16.9 %collective-permute-start.8 = (bf16[256,256]{1,0:T(8,128)(2,1)S(1)}, bf16[256,256]{1,0:T(8,128)(2,1)S(1)}, u32[]{:S(2)}, u32[]{:S(2)}) collective-permute-start(bf16[256,256]{1,0:T(8,128)(2,1)S(1)} %get-tuple-element.56), channel_id=1, source_target_pairs={{0,2},{1,3},{2,0},{3,1},{4,6},{5,7},{6,4},{7,5},{8,10},{9,11},{10,... | collective-permute-start | bytes 393224 | tf_op jit(solution)/shard_map/ppermute | solution.py:203
  85.3 21.0 %all-to-all-start.4 = ((f32[32,16,128]{2,1,0:T(8,128)}), f32[32,16,128]{2,1,0:T(8,128)S(1)}, u32[]{:S(2)}, u32[]{:S(2)}) async-start(f32[32,16,128]{2,1,0:T(8,128)} %bitcast.8), calls=%async_computation.4 | async-start | bytes 524288 | tf_op jit(solution)/shard_map/all_to_all | solution.py:338
  106.3 18.9 %all-to-all-start.3 = ((f32[8,128,256]{2,1,0:T(8,128)}), f32[8,128,256]{2,1,0:T(8,128)S(1)}, u32[]{:S(2)}, u32[]{:S(2)}) async-start(f32[8,128,256]{2,1,0:T(8,128)} %bitcast.7), calls=%async_computation.3 | async-start | bytes 2097152 | tf_op jit(solution)/shard_map/all_to_all | solution.py:193
  126.8 12.8 %all-to-all-start.5 = ((f32[32,16,128]{2,1,0:T(8,128)}), f32[32,16,128]{2,1,0:T(8,128)S(1)}, u32[]{:S(2)}, u32[]{:S(2)}) async-start(f32[32,16,128]{2,1,0:T(8,128)} %bitcast.10), calls=%async_computation.5 | async-start | bytes 524288 | tf_op jit(solution)/shard_map/all_to_all | solution.py:338
  140.3 7.0 %collective-permute-start.12 = (bf16[128,256]{1,0:T(8,128)(2,1)S(1)}, bf16[128,256]{1,0:T(8,128)(2,1)S(1)}, u32[]{:S(2)}, u32[]{:S(2)}) collective-permute-start(bf16[128,256]{1,0:T(8,128)(2,1)S(1)} %get-tuple-element.68), channel_id=1, source_target_pairs={{0,24},{4,28},{8,16},{12,20},{16,8},{20,12},{24,0},{28,4},{1,25},{... | collective-permute-start | bytes 196616 | tf_op jit(solution)/shard_map/ppermute | solution.py:203
  141.3 6.0 %collective-permute-start.11 = (bf16[128,256]{1,0:T(8,128)(2,1)S(1)}, bf16[128,256]{1,0:T(8,128)(2,1)S(1)}, u32[]{:S(2)}, u32[]{:S(2)}) collective-permute-start(bf16[128,256]{1,0:T(8,128)(2,1)S(1)} %get-tuple-element.68), channel_id=1, source_target_pairs={{0,16},{4,20},{8,24},{12,28},{16,0},{20,4},{24,8},{28,12},{1,17},{... | collective-permute-start | bytes 196616 | tf_op jit(solution)/shard_map/ppermute | solution.py:203
  142.8 4.5 %collective-permute-start.10 = (bf16[128,256]{1,0:T(8,128)(2,1)S(1)}, bf16[128,256]{1,0:T(8,128)(2,1)S(1)}, u32[]{:S(2)}, u32[]{:S(2)}) collective-permute-start(bf16[128,256]{1,0:T(8,128)(2,1)S(1)} %get-tuple-element.68), channel_id=1, source_target_pairs={{0,8},{4,12},{8,0},{12,4},{16,24},{20,28},{24,16},{28,20},{1,9},{5... | collective-permute-start | bytes 196616 | tf_op jit(solution)/shard_map/ppermute | solution.py:203
  144.6 12.9 %all-to-all-start.7 = ((f32[32,16,128]{2,1,0:T(8,128)}), f32[32,16,128]{2,1,0:T(8,128)S(1)}, u32[]{:S(2)}, u32[]{:S(2)}) async-start(f32[32,16,128]{2,1,0:T(8,128)} %bitcast.13), calls=%async_computation.7 | async-start | bytes 524288 | tf_op jit(solution)/shard_map/all_to_all | solution.py:338
  147.3 1.6 collective-permute-start.13
  157.5 16.5 %all-to-all-start.6 = ((f32[32,8,256]{2,1,0:T(8,128)}), f32[32,8,256]{2,1,0:T(8,128)S(1)}, u32[]{:S(2)}, u32[]{:S(2)}) async-start(f32[32,8,256]{2,1,0:T(8,128)} %bitcast.12), calls=%async_computation.6 | async-start | bytes 524288 | tf_op jit(solution)/shard_map/all_to_all | solution.py:193

commit v3 on v2

--- a/solution.py
+++ b/solution.py
@@ -60,18 +60,11 @@
 
 def moments_kernel(mode, orders, arrays, count_ref, coords_ref, *refs):
     block_refs, refs = refs[:arrays], refs[arrays:]
-    first_ref, second_ref, out_ref, held_ref, sems, order_ref = refs[:6]
+    first_ref, second_ref, out_ref, held_ref, sems, order_ref = refs
     rank = out_ref.shape[1]
     count = count_ref[0, 0]
-    if len(refs) > 6:
-        months_ref, month_sem = refs[6:]
-        months = pltpu.make_async_copy(second_ref, months_ref, month_sem)
-        months.start()
-        second_ref = months_ref
     fetch_all(count, block_refs, 0, held_ref, sems)
     out_ref[...] = jnp.zeros_like(out_ref)
-    if len(refs) > 6:
-        months.wait()
     spread_mode, tile_mode = ((1, 2), (0, 2), (1, 0))[mode]
 
     def add_block(slot, carry):
@@ -114,13 +107,9 @@
         pltpu.SemaphoreType.DMA((slots,)),
         pltpu.VMEM((rank // LANES, W, LANES), F32),
     ]
-    second_spec = VMEM_SPEC
-    if mode < 2:
-        second, second_spec = in_hbm(second), HBM_SPEC
-        scratch += [pltpu.VMEM(second.shape, second.dtype), pltpu.SemaphoreType.DMA]
     return pl.pallas_call(
         functools.partial(moments_kernel, mode, orders, len(blocks)),
-        in_specs=[SMEM_SPEC, SMEM_SPEC] + [HBM_SPEC] * len(blocks) + [VMEM_SPEC, second_spec],
+        in_specs=[SMEM_SPEC, SMEM_SPEC] + [HBM_SPEC] * len(blocks) + [VMEM_SPEC, VMEM_SPEC],
         out_specs=VMEM_SPEC,
         out_shape=jax.ShapeDtypeStruct((out_rows, rank), F32),
         scratch_shapes=scratch,
@@ -492,11 +481,14 @@
     month_total = c_init.shape[0]
     devices = slab_count * grid_count
     ones = jnp.ones((1, c_init.shape[1]), F32)
-    b_rounded, b_held = lax.optimization_barrier((b_init.astype(BF16), b_init))
-    term_panel = swap_gather(b_rounded, "slab")
-    held_blocks, term_panel = lax.optimization_barrier((local_blocks, term_panel))
+    messages_b, b_rounded = lax.optimization_barrier((gram_message(b_init, devices), b_init.astype(BF16)))
+    messages_b = swap_all(messages_b)
+    even = [b_rounded] + [swap(b_rounded, "slab", k) for k in range(2, slab_count, 2)]
+    held_blocks, even[-1] = lax.optimization_barrier((local_blocks, even[-1]))
     terms_one = turned_blocks(1, held_blocks, counts, 0)
-    messages_b, terms_one = lax.optimization_barrier((swap_all(gram_message(b_held, devices)), terms_one))
+    messages_b, terms_one = lax.optimization_barrier((messages_b, terms_one))
+    even = jnp.concatenate(even, 0)
+    term_panel = jnp.concatenate([even, swap(even, "slab", 1)], 0)
     spread_b, term_panel = lax.optimization_barrier((fold(messages_b, devices), term_panel))
     gram_b = (swap_all(spread_b), term_total, ones)
     moments_a = block_moments(

time: 191 us -> 188 us (0.984)
  Pallas kernels: 80.5 us -> 69.5 us
  waiting for transfers between devices: 40.9 us -> 48.7 us
    pallas_call x3, Pallas kernels: 23.6 us -> 17.8 us  [block_moments(): pl.pallas_call(functools.partial(moments_kernel, mode, orders, len(blocks...]
    all_to_all x6, waiting for transfers between devices: 15.9 us -> 21.2 us  [swap_all(): lax.all_to_all(messages, BOTH, split_axis=0, concat_axis=0, tiled=True)]
    pallas_call x4, Pallas kernels: 15.3 us -> 10 us  [turned_blocks(): pl.pallas_call(functools.partial(turn_kernel, mode, half * slots), in_spe...]
    ppermute x14, waiting for transfers between devices: 20.8 us -> 23.2 us  [swap(): lax.ppermute(rows, axis, [(i, i ^ step) for i in range(lax.axis_size(axis...]
  transfers between devices with their start and end apart: 22 -> 22, of which waited for: 10 -> 9; matrix products, arithmetic and copies ran while one was open for 1% -> 1% of each run, Pallas kernels for 39% -> 33%
where the time goes in v3:
time: 188 us; the launch traced here: 189 us
  Pallas kernels  69.5 us (37%)
  starting transfers between devices  48.9 us (26%)
  waiting for transfers between devices  48.7 us (26%)
  blocking collectives  15.6 us (8%)
    pallas_call x3, Pallas kernels, product_inverse(): pl.pallas_call(functools.partial(inverse_kernel, devices, (one[1], two[1]...  33 us
    ppermute x14, waiting for transfers between devices, swap(): lax.ppermute(rows, axis, [(i, i ^ step) for i in range(lax.axis_size(axis...  23.2 us
    all_to_all x6, starting transfers between devices, swap_all(): lax.all_to_all(messages, BOTH, split_axis=0, concat_axis=0, tiled=True)  22.3 us
    all_to_all x6, waiting for transfers between devices, swap_all(): lax.all_to_all(messages, BOTH, split_axis=0, concat_axis=0, tiled=True)  21.2 us
    pallas_call x3, Pallas kernels, block_moments(): pl.pallas_call(functools.partial(moments_kernel, mode, orders, len(blocks...  17.8 us
    ppermute x14, starting transfers between devices, swap(): lax.ppermute(rows, axis, [(i, i ^ step) for i in range(lax.axis_size(axis...  16.5 us
    all_to_all x1, blocking collectives, spread_rows(): lax.all_to_all(jnp.tile(rows, (devices, 1)), axes, split_axis=0, concat_a...  15.6 us
    all_to_all x2, starting transfers between devices, exchange(): parts = lax.all_to_all(rows, axes, split_axis=0, concat_axis=0, tiled=True)  10.1 us
  transfers between devices with their start and end apart: 22, of which 9 were waited for; matrix products, arithmetic and copies ran while one was open for 1% of the time, Pallas kernels for 33%

profile of v3, /device:TPU:0, one launch (start us, length us, event | category | flops | bytes accessed | tf_op | source)
XLA Modules:
  0.0 188.6 jit_solution(560693369798716303)
XLA Ops:
  0.6 0.9 convert_element_type.3
  1.6 0.9 copy-done.1
  2.4 1.1 shard_map.76
  3.6 3.0 %collective-permute-start.2 = (bf16[128,256]{1,0:T(8,128)(2,1)S(1)}, bf16[128,256]{1,0:T(8,128)(2,1)S(1)}, u32[]{:S(2)}, u32[]{:S(2)}) collective-permute-start(bf16[128,256]{1,0:T(8,128)(2,1)S(1)} %convert_element_type.3), channel_id=1, source_target_pairs={{0,16},{4,20},{8,24},{12,28},{16,0},{20,4},{24,8},{28,12},{1,17},{... | collective-permute-start | bytes 196616 | tf_op jit(solution)/shard_map/ppermute | solution.py:192
  6.6 1.5 collective-permute-start.1
  8.0 0.0 collective-permute-start
  8.1 6.3 %all-to-all-start = ((f32[32,16,128]{2,1,0:T(8,128)}), f32[32,16,128]{2,1,0:T(8,128)S(1)}, u32[]{:S(2)}, u32[]{:S(2)}) async-start(f32[32,16,128]{2,1,0:T(8,128)} %bitcast.1), calls=%async_computation | async-start | bytes 524288 | tf_op jit(solution)/shard_map/all_to_all | solution.py:327
  15.0 0.8 copy.8.coords_ref
  15.8 0.0 collective-permute-done
  15.8 0.0 collective-permute-done.2
  15.8 0.0 collective-permute-done.1
  15.9 0.3 collective-permute-start.3
  16.2 4.2 %shard_map.77.refs_0_ = bf16[8,64,4096]{2,1,0:T(8,128)(2,1)} custom-call(s32[1,1]{1,0:T(1,128)S(6)} %copy.22.count_ref, bf16[16,64,4096]{2,1,0:T(8,128)(2,1)} %bitcast.28), custom_call_target="tpu_custom_call" | custom-call | bytes 16777216 | tf_op jit(solution)/shard_map/pallas_call | solution.py:163
  20.5 0.0 collective-permute-done.3
  20.5 4.1 %all-to-all-done = f32[32,16,128]{2,1,0:T(8,128)S(1)} async-done(((f32[32,16,128]{2,1,0:T(8,128)}), f32[32,16,128]{2,1,0:T(8,128)S(1)}, u32[]{:S(2)}, u32[]{:S(2)}) %all-to-all-start) | async-done | bytes 262176 | tf_op jit(solution)/shard_map/all_to_all | solution.py:327
  24.6 0.8 shard_map.78
  25.3 2.7 %all-to-all-start.1 = ((f32[32,16,128]{2,1,0:T(8,128)}), f32[32,16,128]{2,1,0:T(8,128)S(1)}, u32[]{:S(2)}, u32[]{:S(2)}) async-start(f32[32,16,128]{2,1,0:T(8,128)} %bitcast.3), calls=%async_computation.1 | async-start | bytes 524288 | tf_op jit(solution)/shard_map/all_to_all | solution.py:327
  28.1 5.4 %shard_map.79.refs_0_ = f32[1024,256]{1,0:T(8,128)S(1)} custom-call(s32[1,1]{1,0:T(1,128)S(6)} %copy.22.count_ref, s32[1,1,16,3]{3,2,1,0:T(8,128)S(1)} %copy.8.coords_ref, bf16[16,64,4096]{2,1,0:T(8,128)(2,1)} %bitcast.29, bf16[1024,256]{1,0:T(8,128)(2,1)S(1)} %constant_dynamic-update-slice_fusion.refs_1_, f32[256,256]{1,0:T(8,128)S(1)} %copy-done), custom_call_target="tpu_custom_call" | custom-call | flops 2147483648 | bytes 8388608 | tf_op jit(solution)/shard_map/pallas_call | solution.py:110
  33.5 0.1 fusion
  33.5 1.7 collective-permute-start.6
  35.2 1.2 collective-permute-start.5
  36.3 1.6 collective-permute-start.4
  38.0 0.6 fusion.1.two_ref
  38.6 11.0 %shard_map.80.refs_4_ = f32[256,256]{1,0:T(8,128)S(1)} custom-call(f32[512,128]{1,0:T(8,128)S(1)} %bitcast.27, f32[1,256]{1,0:T(1,128)S(1)} %broadcast_in_dim.4.one_scale_ref.two_scale_ref, f32[256,256]{1,0:T(8,128)S(1)} %fusion.1.two_ref, f32[1,256]{1,0:T(1,128)S(1)} %broadcast_in_dim.4.one_scale_ref.two_scale_ref), custom_call_target="tpu_custom_call" | custom-call | flops 10000000000 | bytes 786432 | tf_op jit(solution)/shard_map/pallas_call | solution.py:402
  49.6 0.2 shard_map.81.refs_1_
  49.8 0.0 collective-permute-done.6.refs_3_
  49.8 10.2 %collective-permute-done.5.refs_2_ = f32[256,256]{1,0:T(8,128)S(1)} collective-permute-done((f32[256,256]{1,0:T(8,128)S(1)}, f32[256,256]{1,0:T(8,128)S(1)}, u32[]{:S(2)}, u32[]{:S(2)}) %collective-permute-start.5) | collective-permute-done | bytes 262176 | tf_op jit(solution)/shard_map/ppermute | solution.py:192
  59.9 0.0 collective-permute-done.4.refs_1_
  59.9 1.9 shard_map.82
  61.8 5.0 %all-to-all-start.2 = ((f32[32,16,128]{2,1,0:T(8,128)}), f32[32,16,128]{2,1,0:T(8,128)S(1)}, u32[]{:S(2)}, u32[]{:S(2)}) async-start(f32[32,16,128]{2,1,0:T(8,128)} %bitcast.5), calls=%async_computation.2 | async-start | bytes 524288 | tf_op jit(solution)/shard_map/all_to_all | solution.py:327
  66.8 5.5 %shard_map.83.refs_0_ = bf16[8,64,4096]{2,1,0:T(8,128)(2,1)} custom-call(s32[1,1]{1,0:T(1,128)S(6)} %copy.22.count_ref, bf16[16,64,4096]{2,1,0:T(8,128)(2,1)} %bitcast.31), custom_call_target="tpu_custom_call" | custom-call | bytes 16777216 | tf_op jit(solution)/shard_map/pallas_call | solution.py:163
  72.3 4.7 %all-to-all-done.2 = f32[32,16,128]{2,1,0:T(8,128)S(1)} async-done(((f32[32,16,128]{2,1,0:T(8,128)}), f32[32,16,128]{2,1,0:T(8,128)S(1)}, u32[]{:S(2)}, u32[]{:S(2)}) %all-to-all-start.2) | async-done | bytes 262176 | tf_op jit(solution)/shard_map/all_to_all | solution.py:327
  77.0 0.8 shard_map.84
  77.8 1.1 collective-permute-start.7
  78.9 1.1 collective-permute-start.9
  80.0 1.3 collective-permute-start.8
  81.3 2.6 %collective-permute-done.7 = bf16[256,256]{1,0:T(8,128)(2,1)S(1)} collective-permute-done((bf16[256,256]{1,0:T(8,128)(2,1)S(1)}, bf16[256,256]{1,0:T(8,128)(2,1)S(1)}, u32[]{:S(2)}, u32[]{:S(2)}) %collective-permute-start.7) | collective-permute-done | bytes 131104 | tf_op jit(solution)/shard_map/ppermute | solution.py:192
  83.9 0.8 shard_map.86
  84.6 3.0 %all-to-all-start.4 = ((f32[32,16,128]{2,1,0:T(8,128)}), f32[32,16,128]{2,1,0:T(8,128)S(1)}, u32[]{:S(2)}, u32[]{:S(2)}) async-start(f32[32,16,128]{2,1,0:T(8,128)} %bitcast.8), calls=%async_computation.4 | async-start | bytes 524288 | tf_op jit(solution)/shard_map/all_to_all | solution.py:327
  87.6 9.2 %collective-permute-done.8 = bf16[256,256]{1,0:T(8,128)(2,1)S(1)} collective-permute-done((bf16[256,256]{1,0:T(8,128)(2,1)S(1)}, bf16[256,256]{1,0:T(8,128)(2,1)S(1)}, u32[]{:S(2)}, u32[]{:S(2)}) %collective-permute-start.8) | collective-permute-done | bytes 131104 | tf_op jit(solution)/shard_map/ppermute | solution.py:192
  96.9 0.0 collective-permute-done.9
  96.9 6.4 %shard_map.85 = f32[1024,256]{1,0:T(8,128)} custom-call(s32[1,1]{1,0:T(1,128)S(6)} %copy.22.count_ref, s32[1,1,16,3]{3,2,1,0:T(8,128)S(1)} %copy.8.coords_ref, bf16[8,64,4096]{2,1,0:T(8,128)(2,1)} %shard_map.77.refs_0_, bf16[8,64,4096]{2,1,0:T(8,128)(2,1)} %shard_map.81.refs_1_, bf16[1024,256]{1,0:T(8,128)(2,1)S(1)} %constant_dynamic-update-slice_fusion.5.refs_2_.refs_3_, ...), custom_call_target="tpu_custom_call" | custom-call | flops 2147483648 | bytes 8388608 | tf_op jit(solution)/shard_map/pallas_call | solution.py:110
  103.3 3.7 %all-to-all-start.3 = ((f32[8,128,256]{2,1,0:T(8,128)}), f32[8,128,256]{2,1,0:T(8,128)S(1)}, u32[]{:S(2)}, u32[]{:S(2)}) async-start(f32[8,128,256]{2,1,0:T(8,128)} %bitcast.7), calls=%async_computation.3 | async-start | bytes 2097152 | tf_op jit(solution)/shard_map/all_to_all | solution.py:182
  107.0 11.0 %shard_map.87.refs_1_ = f32[256,256]{1,0:T(8,128)S(1)} custom-call(f32[512,128]{1,0:T(8,128)S(1)} %bitcast.24, f32[1,256]{1,0:T(1,128)S(1)} %get-tuple-element.59.one_scale_ref, f32[256,256]{1,0:T(8,128)S(1)} %fusion.1.two_ref, f32[1,256]{1,0:T(1,128)S(1)} %broadcast_in_dim.4.one_scale_ref.two_scale_ref), custom_call_target="tpu_custom_call" | custom-call | flops 10000000000 | bytes 786432 | tf_op jit(solution)/shard_map/pallas_call | solution.py:402
  118.0 4.2 %all-to-all-done.3.refs_0_ = f32[8,128,256]{2,1,0:T(8,128)S(1)} async-done(((f32[8,128,256]{2,1,0:T(8,128)}), f32[8,128,256]{2,1,0:T(8,128)S(1)}, u32[]{:S(2)}, u32[]{:S(2)}) %all-to-all-start.3) | async-done | bytes 1048608 | tf_op jit(solution)/shard_map/all_to_all | solution.py:182
  122.2 1.6 shard_map.88
  123.8 2.6 %all-to-all-start.5 = ((f32[32,16,128]{2,1,0:T(8,128)}), f32[32,16,128]{2,1,0:T(8,128)S(1)}, u32[]{:S(2)}, u32[]{:S(2)}) async-start(f32[32,16,128]{2,1,0:T(8,128)} %bitcast.10), calls=%async_computation.5 | async-start | bytes 524288 | tf_op jit(solution)/shard_map/all_to_all | solution.py:327
  126.4 0.2 shard_map.89.refs_1_
  126.6 10.0 %all-to-all-done.5 = f32[32,16,128]{2,1,0:T(8,128)S(1)} async-done(((f32[32,16,128]{2,1,0:T(8,128)}), f32[32,16,128]{2,1,0:T(8,128)S(1)}, u32[]{:S(2)}, u32[]{:S(2)}) %all-to-all-start.5) | async-done | bytes 262176 | tf_op jit(solution)/shard_map/all_to_all | solution.py:327
  136.6 0.7 shard_map.90
  137.3 1.0 collective-permute-start.12
  138.3 1.5 collective-permute-start.11
  139.8 1.0 collective-permute-start.10
  140.8 0.8 shard_map.92
  141.5 2.7 %all-to-all-start.7 = ((f32[32,16,128]{2,1,0:T(8,128)}), f32[32,16,128]{2,1,0:T(8,128)S(1)}, u32[]{:S(2)}, u32[]{:S(2)}) async-start(f32[32,16,128]{2,1,0:T(8,128)} %bitcast.13), calls=%async_computation.7 | async-start | bytes 524288 | tf_op jit(solution)/shard_map/all_to_all | solution.py:327
  144.3 0.3 collective-permute-start.13
  144.7 1.3 collective-permute-done.13
  145.9 6.1 %shard_map.91 = f32[256,256]{1,0:T(8,128)} custom-call(s32[1,1]{1,0:T(1,128)S(6)} %copy.22.count_ref, s32[1,1,16,3]{3,2,1,0:T(8,128)S(1)} %copy.8.coords_ref, bf16[8,64,4096]{2,1,0:T(8,128)(2,1)} %shard_map.83.refs_0_, bf16[8,64,4096]{2,1,0:T(8,128)(2,1)} %shard_map.89.refs_1_, bf16[1024,256]{1,0:T(8,128)(2,1)S(1)} %constant_dynamic-update-slice_fusion.9.refs_2_, ...), custom_call_target="tpu_custom_call" | custom-call | flops 2147483648 | bytes 8388608 | tf_op jit(solution)/shard_map/pallas_call | solution.py:110
  152.0 2.4 %all-to-all-done.7 = f32[32,16,128]{2,1,0:T(8,128)S(1)} async-done(((f32[32,16,128]{2,1,0:T(8,128)}), f32[32,16,128]{2,1,0:T(8,128)S(1)}, u32[]{:S(2)}, u32[]{:S(2)}) %all-to-all-start.7) | async-done | bytes 262176 | tf_op jit(solution)/shard_map/all_to_all | solution.py:327
  154.4 6.4 %all-to-all-start.6 = ((f32[32,8,256]{2,1,0:T(8,128)}), f32[32,8,256]{2,1,0:T(8,128)S(1)}, u32[]{:S(2)}, u32[]{:S(2)}) async-start(f32[32,8,256]{2,1,0:T(8,128)} %bitcast.12), calls=%async_computation.6 | async-start | bytes 524288 | tf_op jit(solution)/shard_map/all_to_all | solution.py:182
  160.8 11.0 %shard_map.93.refs_1_ = f32[256,256]{1,0:T(8,128)S(1)} custom-call(f32[512,128]{1,0:T(8,128)S(1)} %bitcast.25, f32[1,256]{1,0:T(1,128)S(1)} %get-tuple-element.59.one_scale_ref, f32[512,128]{1,0:T(8,128)S(1)} %bitcast.26, f32[1,256]{1,0:T(1,128)S(1)} %get-tuple-element.70.two_scale_ref), custom_call_target="tpu_custom_call" | custom-call | flops 10000000000 | bytes 786432 | tf_op jit(solution)/shard_map/pallas_call | solution.py:402
  171.9 0.2 shard_map.94
  172.2 15.6 %all_to_all.96 = f32[32,8,256]{2,1,0:T(8,128)S(1)} all-to-all(f32[32,8,256]{2,1,0:T(8,128)S(1)} %tile.2), channel_id=1, replica_groups=mesh['slab'=8,'grid'=4] {'slab','grid'}, dimensions={0} | all-to-all | bytes 524288 | tf_op jit(solution)/shard_map/all_to_all | solution.py:188
  187.8 0.7 bitcast_divide_fusion
  (29 shorter events, 0.3 us)
Async XLA Ops:
  1.5 0.9 copy-start.1
  3.6 12.2 %collective-permute-start.2 = (bf16[128,256]{1,0:T(8,128)(2,1)S(1)}, bf16[128,256]{1,0:T(8,128)(2,1)S(1)}, u32[]{:S(2)}, u32[]{:S(2)}) collective-permute-start(bf16[128,256]{1,0:T(8,128)(2,1)S(1)} %convert_element_type.3), channel_id=1, source_target_pairs={{0,16},{4,20},{8,24},{12,28},{16,0},{20,4},{24,8},{28,12},{1,17},{... | collective-permute-start | bytes 196616 | tf_op jit(solution)/shard_map/ppermute | solution.py:192
  6.6 9.3 %collective-permute-start.1 = (bf16[128,256]{1,0:T(8,128)(2,1)S(1)}, bf16[128,256]{1,0:T(8,128)(2,1)S(1)}, u32[]{:S(2)}, u32[]{:S(2)}) collective-permute-start(bf16[128,256]{1,0:T(8,128)(2,1)S(1)} %convert_element_type.3), channel_id=1, source_target_pairs={{0,8},{4,12},{8,0},{12,4},{16,24},{20,28},{24,16},{28,20},{1,9},{5... | collective-permute-start | bytes 196616 | tf_op jit(solution)/shard_map/ppermute | solution.py:192
  8.0 7.8 %collective-permute-start = (bf16[128,256]{1,0:T(8,128)(2,1)S(1)}, bf16[128,256]{1,0:T(8,128)(2,1)S(1)}, u32[]{:S(2)}, u32[]{:S(2)}) collective-permute-start(bf16[128,256]{1,0:T(8,128)(2,1)S(1)} %convert_element_type.3), channel_id=1, source_target_pairs={{0,24},{4,28},{8,16},{12,20},{16,8},{20,12},{24,0},{28,4},{1,25},{... | collective-permute-start | bytes 196616 | tf_op jit(solution)/shard_map/ppermute | solution.py:192
  8.1 16.5 %all-to-all-start = ((f32[32,16,128]{2,1,0:T(8,128)}), f32[32,16,128]{2,1,0:T(8,128)S(1)}, u32[]{:S(2)}, u32[]{:S(2)}) async-start(f32[32,16,128]{2,1,0:T(8,128)} %bitcast.1), calls=%async_computation | async-start | bytes 524288 | tf_op jit(solution)/shard_map/all_to_all | solution.py:327
  15.9 4.6 %collective-permute-start.3 = (bf16[512,256]{1,0:T(8,128)(2,1)S(1)}, bf16[512,256]{1,0:T(8,128)(2,1)S(1)}, u32[]{:S(2)}, u32[]{:S(2)}) collective-permute-start(bf16[512,256]{1,0:T(8,128)(2,1)S(1)} %pad_maximum_fusion), channel_id=1, source_target_pairs={{0,4},{4,0},{8,12},{12,8},{16,20},{20,16},{24,28},{28,24},{1,5},{5... | collective-permute-start | bytes 786440 | tf_op jit(solution)/shard_map/ppermute | solution.py:192
  16.2 11.9 %copy-start = (f32[256,256]{1,0:T(8,128)S(1)}, f32[256,256]{1,0:T(8,128)}, u32[]{:S(2)}) copy-start(f32[256,256]{1,0:T(8,128)} %refs_3_.1) | copy-start | bytes 786436
  25.3 13.2 %all-to-all-start.1 = ((f32[32,16,128]{2,1,0:T(8,128)}), f32[32,16,128]{2,1,0:T(8,128)S(1)}, u32[]{:S(2)}, u32[]{:S(2)}) async-start(f32[32,16,128]{2,1,0:T(8,128)} %bitcast.3), calls=%async_computation.1 | async-start | bytes 524288 | tf_op jit(solution)/shard_map/all_to_all | solution.py:327
  33.5 16.2 %collective-permute-start.6 = (f32[256,256]{1,0:T(8,128)S(1)}, f32[256,256]{1,0:T(8,128)S(1)}, u32[]{:S(2)}, u32[]{:S(2)}) collective-permute-start(f32[256,256]{1,0:T(8,128)S(1)} %get-tuple-element.71), channel_id=1, source_target_pairs={{0,3},{1,2},{2,1},{3,0},{4,7},{5,6},{6,5},{7,4},{8,11},{9,10},{10,... | collective-permute-start | bytes 786440 | tf_op jit(solution)/shard_map/ppermute | solution.py:192
  35.2 24.7 %collective-permute-start.5 = (f32[256,256]{1,0:T(8,128)S(1)}, f32[256,256]{1,0:T(8,128)S(1)}, u32[]{:S(2)}, u32[]{:S(2)}) collective-permute-start(f32[256,256]{1,0:T(8,128)S(1)} %get-tuple-element.72), channel_id=1, source_target_pairs={{0,2},{1,3},{2,0},{3,1},{4,6},{5,7},{6,4},{7,5},{8,10},{9,11},{10,... | collective-permute-start | bytes 786440 | tf_op jit(solution)/shard_map/ppermute | solution.py:192
  36.3 23.6 %collective-permute-start.4 = (f32[256,256]{1,0:T(8,128)S(1)}, f32[256,256]{1,0:T(8,128)S(1)}, u32[]{:S(2)}, u32[]{:S(2)}) collective-permute-start(f32[256,256]{1,0:T(8,128)S(1)} %get-tuple-element.73), channel_id=1, source_target_pairs={{0,1},{1,0},{2,3},{3,2},{4,5},{5,4},{6,7},{7,6},{8,9},{9,8},{10,11... | collective-permute-start | bytes 786440 | tf_op jit(solution)/shard_map/ppermute | solution.py:192
  61.8 15.2 %all-to-all-start.2 = ((f32[32,16,128]{2,1,0:T(8,128)}), f32[32,16,128]{2,1,0:T(8,128)S(1)}, u32[]{:S(2)}, u32[]{:S(2)}) async-start(f32[32,16,128]{2,1,0:T(8,128)} %bitcast.5), calls=%async_computation.2 | async-start | bytes 524288 | tf_op jit(solution)/shard_map/all_to_all | solution.py:327
  77.8 6.1 %collective-permute-start.7 = (bf16[256,256]{1,0:T(8,128)(2,1)S(1)}, bf16[256,256]{1,0:T(8,128)(2,1)S(1)}, u32[]{:S(2)}, u32[]{:S(2)}) collective-permute-start(bf16[256,256]{1,0:T(8,128)(2,1)S(1)} %get-tuple-element.56), channel_id=1, source_target_pairs={{0,1},{1,0},{2,3},{3,2},{4,5},{5,4},{6,7},{7,6},{8,9},{9,8},{10,11... | collective-permute-start | bytes 393224 | tf_op jit(solution)/shard_map/ppermute | solution.py:192
  78.9 18.0 %collective-permute-start.9 = (bf16[256,256]{1,0:T(8,128)(2,1)S(1)}, bf16[256,256]{1,0:T(8,128)(2,1)S(1)}, u32[]{:S(2)}, u32[]{:S(2)}) collective-permute-start(bf16[256,256]{1,0:T(8,128)(2,1)S(1)} %get-tuple-element.56), channel_id=1, source_target_pairs={{0,3},{1,2},{2,1},{3,0},{4,7},{5,6},{6,5},{7,4},{8,11},{9,10},{10,... | collective-permute-start | bytes 393224 | tf_op jit(solution)/shard_map/ppermute | solution.py:192
  80.0 16.9 %collective-permute-start.8 = (bf16[256,256]{1,0:T(8,128)(2,1)S(1)}, bf16[256,256]{1,0:T(8,128)(2,1)S(1)}, u32[]{:S(2)}, u32[]{:S(2)}) collective-permute-start(bf16[256,256]{1,0:T(8,128)(2,1)S(1)} %get-tuple-element.56), channel_id=1, source_target_pairs={{0,2},{1,3},{2,0},{3,1},{4,6},{5,7},{6,4},{7,5},{8,10},{9,11},{10,... | collective-permute-start | bytes 393224 | tf_op jit(solution)/shard_map/ppermute | solution.py:192
  84.6 18.6 %all-to-all-start.4 = ((f32[32,16,128]{2,1,0:T(8,128)}), f32[32,16,128]{2,1,0:T(8,128)S(1)}, u32[]{:S(2)}, u32[]{:S(2)}) async-start(f32[32,16,128]{2,1,0:T(8,128)} %bitcast.8), calls=%async_computation.4 | async-start | bytes 524288 | tf_op jit(solution)/shard_map/all_to_all | solution.py:327
  103.3 18.9 %all-to-all-start.3 = ((f32[8,128,256]{2,1,0:T(8,128)}), f32[8,128,256]{2,1,0:T(8,128)S(1)}, u32[]{:S(2)}, u32[]{:S(2)}) async-start(f32[8,128,256]{2,1,0:T(8,128)} %bitcast.7), calls=%async_computation.3 | async-start | bytes 2097152 | tf_op jit(solution)/shard_map/all_to_all | solution.py:182
  123.8 12.8 %all-to-all-start.5 = ((f32[32,16,128]{2,1,0:T(8,128)}), f32[32,16,128]{2,1,0:T(8,128)S(1)}, u32[]{:S(2)}, u32[]{:S(2)}) async-start(f32[32,16,128]{2,1,0:T(8,128)} %bitcast.10), calls=%async_computation.5 | async-start | bytes 524288 | tf_op jit(solution)/shard_map/all_to_all | solution.py:327
  137.3 7.0 %collective-permute-start.12 = (bf16[128,256]{1,0:T(8,128)(2,1)S(1)}, bf16[128,256]{1,0:T(8,128)(2,1)S(1)}, u32[]{:S(2)}, u32[]{:S(2)}) collective-permute-start(bf16[128,256]{1,0:T(8,128)(2,1)S(1)} %get-tuple-element.68), channel_id=1, source_target_pairs={{0,24},{4,28},{8,16},{12,20},{16,8},{20,12},{24,0},{28,4},{1,25},{... | collective-permute-start | bytes 196616 | tf_op jit(solution)/shard_map/ppermute | solution.py:192
  138.3 6.0 %collective-permute-start.11 = (bf16[128,256]{1,0:T(8,128)(2,1)S(1)}, bf16[128,256]{1,0:T(8,128)(2,1)S(1)}, u32[]{:S(2)}, u32[]{:S(2)}) collective-permute-start(bf16[128,256]{1,0:T(8,128)(2,1)S(1)} %get-tuple-element.68), channel_id=1, source_target_pairs={{0,16},{4,20},{8,24},{12,28},{16,0},{20,4},{24,8},{28,12},{1,17},{... | collective-permute-start | bytes 196616 | tf_op jit(solution)/shard_map/ppermute | solution.py:192
  139.8 4.5 %collective-permute-start.10 = (bf16[128,256]{1,0:T(8,128)(2,1)S(1)}, bf16[128,256]{1,0:T(8,128)(2,1)S(1)}, u32[]{:S(2)}, u32[]{:S(2)}) collective-permute-start(bf16[128,256]{1,0:T(8,128)(2,1)S(1)} %get-tuple-element.68), channel_id=1, source_target_pairs={{0,8},{4,12},{8,0},{12,4},{16,24},{20,28},{24,16},{28,20},{1,9},{5... | collective-permute-start | bytes 196616 | tf_op jit(solution)/shard_map/ppermute | solution.py:192
  141.5 12.9 %all-to-all-start.7 = ((f32[32,16,128]{2,1,0:T(8,128)}), f32[32,16,128]{2,1,0:T(8,128)S(1)}, u32[]{:S(2)}, u32[]{:S(2)}) async-start(f32[32,16,128]{2,1,0:T(8,128)} %bitcast.13), calls=%async_computation.7 | async-start | bytes 524288 | tf_op jit(solution)/shard_map/all_to_all | solution.py:327
  144.3 1.6 collective-permute-start.13
  154.4 17.4 %all-to-all-start.6 = ((f32[32,8,256]{2,1,0:T(8,128)}), f32[32,8,256]{2,1,0:T(8,128)S(1)}, u32[]{:S(2)}, u32[]{:S(2)}) async-start(f32[32,8,256]{2,1,0:T(8,128)} %bitcast.12), calls=%async_computation.6 | async-start | bytes 524288 | tf_op jit(solution)/shard_map/all_to_all | solution.py:182

commit v4 on v3

--- a/solution.py
+++ b/solution.py
@@ -68,7 +68,7 @@
     spread_mode, tile_mode = ((1, 2), (0, 2), (1, 0))[mode]
 
     def add_block(slot, carry):
-        first = first_ref[pl.ds(slot_rows(coords_ref, slot, spread_mode, orders[0]), W), :].astype(F32)
+        first = first_ref[pl.ds(slot_rows(coords_ref, slot, spread_mode, orders[0]), W), :].astype(BF16).astype(F32)
         second = second_ref[pl.ds(slot_rows(coords_ref, slot, tile_mode, orders[1]), W), :].astype(BF16).reshape(4, 16, rank)
         target = slot_rows(coords_ref, slot, mode, orders[2])
         fetch(block_refs[0], 0, held_ref, sems, slot).wait()
@@ -287,9 +287,13 @@
     return own, -(-(own + 2) // 8) * 8
 
 
+def packed_blocks(gram):
+    return jnp.concatenate([gram[:LANES, :LANES], gram[:LANES, LANES:], gram[LANES:, LANES:]], 0)
+
+
 def pack_gram(message_ref, gram, squares, devices):
     own, rows = message_rows(devices)
-    packed = jnp.concatenate([gram[:LANES, :LANES], gram[:LANES, LANES:], gram[LANES:, LANES:]], 0)
+    packed = packed_blocks(gram)
     if devices * own > 3 * LANES or rows > own + 2:
         message_ref[...] = jnp.zeros_like(message_ref)
     for e in range(own):
@@ -311,12 +315,15 @@
 def unpack_gram(ref, devices):
     if ref.shape[1] != LANES:
         return ref[...]
-    own, rows = message_rows(devices)
-    pieces = []
-    for e in range(own):
-        held = min(devices, 3 * LANES - devices * e)
-        pieces.append(ref[pl.ds(e, held, stride=rows), :])
-    packed = jnp.concatenate(pieces, 0)
+    if ref.shape[0] == 3 * LANES:
+        packed = ref[...]
+    else:
+        own, rows = message_rows(devices)
+        pieces = []
+        for e in range(own):
+            held = min(devices, 3 * LANES - devices * e)
+            pieces.append(ref[pl.ds(e, held, stride=rows), :])
+        packed = jnp.concatenate(pieces, 0)
     first, corner, last = packed[:LANES], packed[LANES : 2 * LANES], packed[2 * LANES :]
     return jnp.concatenate(
         [jnp.concatenate([first, corner], 1), jnp.concatenate([corner.T, last], 1)], 0
@@ -327,10 +334,9 @@
     return lax.all_to_all(messages, BOTH, split_axis=0, concat_axis=0, tiled=True)
 
 
-def gram_message_kernel(devices, factor_ref, message_ref):
-    factor = factor_ref[...]
-    squares = jnp.sum(factor * factor, 0, keepdims=True)
-    pack_gram(message_ref, exact_dot(factor, factor, ((0,), (0,))), squares, devices)
+def panel_gram_kernel(panel_ref, packed_ref):
+    panel = panel_ref[...]
+    packed_ref[...] = packed_blocks(exact_dot(panel, panel, ((0,), (0,))))
 
 
 def fold_kernel(devices, parts_ref, spread_ref):
@@ -341,12 +347,12 @@
     return jax.ShapeDtypeStruct((devices * message_rows(devices)[1], LANES), F32)
 
 
-def gram_message(factor, devices):
-    return pl.pallas_call(
-        functools.partial(gram_message_kernel, devices),
-        out_shape=message_shape(devices),
+def panel_gram(panel):
+    return pl.pallas_call(
+        panel_gram_kernel,
+        out_shape=jax.ShapeDtypeStruct((3 * LANES, LANES), F32),
         compiler_params=pltpu.CompilerParams(vmem_limit_bytes=10 << 20),
-    )(factor)
+    )(panel)
 
 
 def fold(parts, devices):
@@ -481,20 +487,21 @@
     month_total = c_init.shape[0]
     devices = slab_count * grid_count
     ones = jnp.ones((1, c_init.shape[1]), F32)
-    messages_b, b_rounded = lax.optimization_barrier((gram_message(b_init, devices), b_init.astype(BF16)))
-    messages_b = swap_all(messages_b)
-    even = [b_rounded] + [swap(b_rounded, "slab", k) for k in range(2, slab_count, 2)]
-    held_blocks, even[-1] = lax.optimization_barrier((local_blocks, even[-1]))
+    even = [b_init] + [swap(b_init, "slab", k) for k in range(2, slab_count, 2)]
+    held_blocks, even[1] = lax.optimization_barrier((local_blocks, even[1]))
     terms_one = turned_blocks(1, held_blocks, counts, 0)
-    messages_b, terms_one = lax.optimization_barrier((messages_b, terms_one))
+    even, terms_one = lax.optimization_barrier((even, terms_one))
     even = jnp.concatenate(even, 0)
     term_panel = jnp.concatenate([even, swap(even, "slab", 1)], 0)
-    spread_b, term_panel = lax.optimization_barrier((fold(messages_b, devices), term_panel))
-    gram_b = (swap_all(spread_b), term_total, ones)
+    own_gram_b = panel_gram(term_panel)
+    own_gram_b, term_panel = lax.optimization_barrier((own_gram_b, term_panel))
+    grams_b = [own_gram_b] + [swap(own_gram_b, "grid", k) for k in range(1, grid_count)]
     moments_a = block_moments(
         0, (TERM_ORDER, None, DOC_ORDER), [local_blocks], coords, counts, term_panel, c_init, doc_rows
     )
+    grams_b, moments_a = lax.optimization_barrier((grams_b, moments_a))
     others_a = swap_pieces(moments_a, "grid")
+    gram_b = (functools.reduce(jnp.add, grams_b), term_total, ones)
     c_held, _ = lax.optimization_barrier((c_init, moments_a))
     gram_c = (gram_local(c_held), month_total, ones)
     inverse_a = product_inverse(gram_b, gram_c, devices)

time: 188 us -> 189 us (level)
  waiting for transfers between devices: 48.7 us -> 57.3 us
  starting transfers between devices: 48.9 us -> 43 us
    ppermute x14 -> x17, waiting for transfers between devices: 23.2 us -> 35.9 us  [swap(): lax.ppermute(rows, axis, [(i, i ^ step) for i in range(lax.axis_size(axis...]
    all_to_all x6 -> x4, starting transfers between devices: 22.3 us -> 13.2 us  [swap_all(): lax.all_to_all(messages, BOTH, split_axis=0, concat_axis=0, tiled=True)]
    ppermute x14 -> x17, starting transfers between devices: 16.5 us -> 20.8 us  [swap(): lax.ppermute(rows, axis, [(i, i ^ step) for i in range(lax.axis_size(axis...]
    all_to_all x6 -> x4, waiting for transfers between devices: 21.2 us -> 17.1 us  [swap_all(): lax.all_to_all(messages, BOTH, split_axis=0, concat_axis=0, tiled=True)]
  transfers between devices with their start and end apart: 22 -> 23, of which waited for: 9 -> 11; matrix products, arithmetic and copies ran while one was open for 1% -> 0% of each run, Pallas kernels for 33% -> 33%
where the time goes in v4:
time: 189 us; the launch traced here: 188 us
  Pallas kernels  68.8 us (36%)
  waiting for transfers between devices  57.3 us (30%)
  starting transfers between devices  43 us (23%)
  blocking collectives  15.6 us (8%)
    ppermute x17, waiting for transfers between devices, swap(): lax.ppermute(rows, axis, [(i, i ^ step) for i in range(lax.axis_size(axis...  35.9 us
    pallas_call x3, Pallas kernels, product_inverse(): pl.pallas_call(functools.partial(inverse_kernel, devices, (one[1], two[1]...  33 us
    ppermute x17, starting transfers between devices, swap(): lax.ppermute(rows, axis, [(i, i ^ step) for i in range(lax.axis_size(axis...  20.8 us
    pallas_call x3, Pallas kernels, block_moments(): pl.pallas_call(functools.partial(moments_kernel, mode, orders, len(blocks...  17.8 us
    all_to_all x4, waiting for transfers between devices, swap_all(): lax.all_to_all(messages, BOTH, split_axis=0, concat_axis=0, tiled=True)  17.1 us
    all_to_all x1, blocking collectives, spread_rows(): lax.all_to_all(jnp.tile(rows, (devices, 1)), axes, split_axis=0, concat_a...  15.6 us
    all_to_all x4, starting transfers between devices, swap_all(): lax.all_to_all(messages, BOTH, split_axis=0, concat_axis=0, tiled=True)  13.2 us
    pallas_call x4, Pallas kernels, turned_blocks(): pl.pallas_call(functools.partial(turn_kernel, mode, half * slots), in_spe...  10 us
  transfers between devices with their start and end apart: 23, of which 11 were waited for; matrix products, arithmetic and copies ran while one was open for 0% of the time, Pallas kernels for 33%

profile of v4, /device:TPU:0, one launch (start us, length us, event | category | flops | bytes accessed | tf_op | source)
XLA Modules:
  0.0 188.2 jit_solution(10026310149453255421)
XLA Ops:
  0.6 3.0 %collective-permute-start = (f32[128,256]{1,0:T(8,128)}, f32[128,256]{1,0:T(8,128)S(1)}, u32[]{:S(2)}, u32[]{:S(2)}) collective-permute-start(f32[128,256]{1,0:T(8,128)} %param.8), channel_id=1, source_target_pairs={{0,8},{4,12},{8,0},{12,4},{16,24},{20,28},{24,16},{28,20},{1,9},{5... | collective-permute-start | bytes 393224 | tf_op jit(solution)/shard_map/ppermute | solution.py:192
  3.6 1.5 collective-permute-start.1
  5.2 0.0 collective-permute-start.2
  5.8 2.0 %collective-permute-done = f32[128,256]{1,0:T(8,128)S(1)} collective-permute-done((f32[128,256]{1,0:T(8,128)}, f32[128,256]{1,0:T(8,128)S(1)}, u32[]{:S(2)}, u32[]{:S(2)}) %collective-permute-start) | collective-permute-done | bytes 131104 | tf_op jit(solution)/shard_map/ppermute | solution.py:192
  7.9 4.2 %shard_map.76.refs_0_ = bf16[8,64,4096]{2,1,0:T(8,128)(2,1)} custom-call(s32[1,1]{1,0:T(1,128)S(6)} %copy.22.count_ref, bf16[16,64,4096]{2,1,0:T(8,128)(2,1)} %bitcast.22), custom_call_target="tpu_custom_call" | custom-call | bytes 16777216 | tf_op jit(solution)/shard_map/pallas_call | solution.py:163
  12.1 0.0 copy-start
  12.1 0.0 collective-permute-done.1
  12.1 0.0 collective-permute-done.2
  12.2 0.1 collective-permute-start.3
  12.3 0.1 copy.8.coords_ref
  12.4 1.7 collective-permute-done.3
  14.2 1.2 shard_map.77
  15.4 3.2 %collective-permute-start.6 = (f32[384,128]{1,0:T(8,128)S(1)}, f32[384,128]{1,0:T(8,128)S(1)}, u32[]{:S(2)}, u32[]{:S(2)}) collective-permute-start(f32[384,128]{1,0:T(8,128)S(1)} %shard_map.77), channel_id=1, source_target_pairs={{0,3},{1,2},{2,1},{3,0},{4,7},{5,6},{6,5},{7,4},{8,11},{9,10},{10,... | collective-permute-start | bytes 589832 | tf_op jit(solution)/shard_map/ppermute | solution.py:192
  18.6 0.0 collective-permute-start.5
  18.6 1.3 collective-permute-start.4
  19.9 5.4 %shard_map.78.refs_0_ = f32[1024,256]{1,0:T(8,128)S(1)} custom-call(s32[1,1]{1,0:T(1,128)S(6)} %copy.22.count_ref, s32[1,1,16,3]{3,2,1,0:T(8,128)S(1)} %copy.8.coords_ref, bf16[16,64,4096]{2,1,0:T(8,128)(2,1)} %bitcast.23, f32[1024,256]{1,0:T(8,128)S(1)} %constant_dynamic-update-slice_fusion.panel_ref.refs_1_, f32[256,256]{1,0:T(8,128)S(1)} %copy-done), custom_call_target="tpu_custom_call" | custom-call | flops 2147483648 | bytes 8388608 | tf_op jit(solution)/shard_map/pallas_call | solution.py:110
  25.3 0.0 collective-permute-done.6
  25.3 11.1 %collective-permute-done.5 = f32[384,128]{1,0:T(8,128)S(1)} collective-permute-done((f32[384,128]{1,0:T(8,128)S(1)}, f32[384,128]{1,0:T(8,128)S(1)}, u32[]{:S(2)}, u32[]{:S(2)}) %collective-permute-start.5) | collective-permute-done | bytes 196640 | tf_op jit(solution)/shard_map/ppermute | solution.py:192
  36.3 0.0 collective-permute-done.4
  36.3 0.1 fusion
  36.4 0.6 fusion.1.two_ref
  37.0 2.7 %collective-permute-start.9 = (f32[256,256]{1,0:T(8,128)S(1)}, f32[256,256]{1,0:T(8,128)S(1)}, u32[]{:S(2)}, u32[]{:S(2)}) collective-permute-start(f32[256,256]{1,0:T(8,128)S(1)} %get-tuple-element.83), channel_id=1, source_target_pairs={{0,3},{1,2},{2,1},{3,0},{4,7},{5,6},{6,5},{7,4},{8,11},{9,10},{10,... | collective-permute-start | bytes 786440 | tf_op jit(solution)/shard_map/ppermute | solution.py:192
  39.7 0.0 collective-permute-start.8
  39.7 1.7 collective-permute-start.7
  41.5 0.1 add_add_fusion.one_ref
  41.5 11.0 %shard_map.79.refs_4_ = f32[256,256]{1,0:T(8,128)S(1)} custom-call(f32[384,128]{1,0:T(8,128)S(1)} %add_add_fusion.one_ref, f32[1,256]{1,0:T(1,128)S(1)} %broadcast_in_dim.4.one_scale_ref.two_scale_ref, f32[256,256]{1,0:T(8,128)S(1)} %fusion.1.two_ref, f32[1,256]{1,0:T(1,128)S(1)} %broadcast_in_dim.4.one_scale_ref.two_scale_ref), custom_call_target="tpu_custom_call" | custom-call | flops 10000000000 | bytes 786432 | tf_op jit(solution)/shard_map/pallas_call | solution.py:408
  52.5 0.2 shard_map.80.refs_1_
  52.7 0.0 collective-permute-done.9.refs_3_
  52.7 8.0 %collective-permute-done.8.refs_2_ = f32[256,256]{1,0:T(8,128)S(1)} collective-permute-done((f32[256,256]{1,0:T(8,128)S(1)}, f32[256,256]{1,0:T(8,128)S(1)}, u32[]{:S(2)}, u32[]{:S(2)}) %collective-permute-start.8) | collective-permute-done | bytes 262176 | tf_op jit(solution)/shard_map/ppermute | solution.py:192
  60.7 1.9 %shard_map.81 = (f32[256,256]{1,0:T(8,128)S(1)}, f32[512,128]{1,0:T(8,128)}) custom-call(f32[1024,256]{1,0:T(8,128)S(1)} %shard_map.78.refs_0_, f32[256,256]{1,0:T(8,128)S(1)} %collective-permute-done.7.refs_1_, f32[256,256]{1,0:T(8,128)S(1)} %collective-permute-done.8.refs_2_, f32[256,256]{1,0:T(8,128)S(1)} %collective-permute-done.9.refs_3_, ...), custom_call_target="tpu_custom_call" | custom-call | tf_op jit(solution)/shard_map/pallas_call | solution.py:435
  62.6 5.0 %all-to-all-start = ((f32[32,16,128]{2,1,0:T(8,128)}), f32[32,16,128]{2,1,0:T(8,128)S(1)}, u32[]{:S(2)}, u32[]{:S(2)}) async-start(f32[32,16,128]{2,1,0:T(8,128)} %bitcast.1), calls=%async_computation | async-start | bytes 524288 | tf_op jit(solution)/shard_map/all_to_all | solution.py:334
  67.6 5.5 %shard_map.82.refs_0_ = bf16[8,64,4096]{2,1,0:T(8,128)(2,1)} custom-call(s32[1,1]{1,0:T(1,128)S(6)} %copy.22.count_ref, bf16[16,64,4096]{2,1,0:T(8,128)(2,1)} %bitcast.25), custom_call_target="tpu_custom_call" | custom-call | bytes 16777216 | tf_op jit(solution)/shard_map/pallas_call | solution.py:163
  73.0 4.7 %all-to-all-done = f32[32,16,128]{2,1,0:T(8,128)S(1)} async-done(((f32[32,16,128]{2,1,0:T(8,128)}), f32[32,16,128]{2,1,0:T(8,128)S(1)}, u32[]{:S(2)}, u32[]{:S(2)}) %all-to-all-start) | async-done | bytes 262176 | tf_op jit(solution)/shard_map/all_to_all | solution.py:334
  77.8 0.8 shard_map.83
  78.5 1.1 collective-permute-start.10
  79.6 1.1 collective-permute-start.12
  80.8 1.3 collective-permute-start.11
  82.0 2.6 %collective-permute-done.10 = bf16[256,256]{1,0:T(8,128)(2,1)S(1)} collective-permute-done((bf16[256,256]{1,0:T(8,128)(2,1)S(1)}, bf16[256,256]{1,0:T(8,128)(2,1)S(1)}, u32[]{:S(2)}, u32[]{:S(2)}) %collective-permute-start.10) | collective-permute-done | bytes 131104 | tf_op jit(solution)/shard_map/ppermute | solution.py:192
  84.6 0.8 shard_map.85
  85.4 3.0 %all-to-all-start.2 = ((f32[32,16,128]{2,1,0:T(8,128)}), f32[32,16,128]{2,1,0:T(8,128)S(1)}, u32[]{:S(2)}, u32[]{:S(2)}) async-start(f32[32,16,128]{2,1,0:T(8,128)} %bitcast.4), calls=%async_computation.2 | async-start | bytes 524288 | tf_op jit(solution)/shard_map/all_to_all | solution.py:334
  88.4 9.2 %collective-permute-done.11 = bf16[256,256]{1,0:T(8,128)(2,1)S(1)} collective-permute-done((bf16[256,256]{1,0:T(8,128)(2,1)S(1)}, bf16[256,256]{1,0:T(8,128)(2,1)S(1)}, u32[]{:S(2)}, u32[]{:S(2)}) %collective-permute-start.11) | collective-permute-done | bytes 131104 | tf_op jit(solution)/shard_map/ppermute | solution.py:192
  97.7 6.4 %shard_map.84 = f32[1024,256]{1,0:T(8,128)} custom-call(s32[1,1]{1,0:T(1,128)S(6)} %copy.22.count_ref, s32[1,1,16,3]{3,2,1,0:T(8,128)S(1)} %copy.8.coords_ref, bf16[8,64,4096]{2,1,0:T(8,128)(2,1)} %shard_map.76.refs_0_, bf16[8,64,4096]{2,1,0:T(8,128)(2,1)} %shard_map.80.refs_1_, bf16[1024,256]{1,0:T(8,128)(2,1)S(1)} %constant_dynamic-update-slice_fusion.5.refs_2_.refs_3_, ...), custom_call_target="tpu_custom_call" | custom-call | flops 2147483648 | bytes 8388608 | tf_op jit(solution)/shard_map/pallas_call | solution.py:110
  104.0 3.7 %all-to-all-start.1 = ((f32[8,128,256]{2,1,0:T(8,128)}), f32[8,128,256]{2,1,0:T(8,128)S(1)}, u32[]{:S(2)}, u32[]{:S(2)}) async-start(f32[8,128,256]{2,1,0:T(8,128)} %bitcast.3), calls=%async_computation.1 | async-start | bytes 2097152 | tf_op jit(solution)/shard_map/all_to_all | solution.py:182
  107.8 11.0 %shard_map.86.refs_1_ = f32[256,256]{1,0:T(8,128)S(1)} custom-call(f32[512,128]{1,0:T(8,128)S(1)} %bitcast.19, f32[1,256]{1,0:T(1,128)S(1)} %get-tuple-element.71.one_scale_ref, f32[256,256]{1,0:T(8,128)S(1)} %fusion.1.two_ref, f32[1,256]{1,0:T(1,128)S(1)} %broadcast_in_dim.4.one_scale_ref.two_scale_ref), custom_call_target="tpu_custom_call" | custom-call | flops 10000000000 | bytes 786432 | tf_op jit(solution)/shard_map/pallas_call | solution.py:408
  118.8 4.2 %all-to-all-done.1.refs_0_ = f32[8,128,256]{2,1,0:T(8,128)S(1)} async-done(((f32[8,128,256]{2,1,0:T(8,128)}), f32[8,128,256]{2,1,0:T(8,128)S(1)}, u32[]{:S(2)}, u32[]{:S(2)}) %all-to-all-start.1) | async-done | bytes 1048608 | tf_op jit(solution)/shard_map/all_to_all | solution.py:182
  123.0 1.6 shard_map.87
  124.6 2.6 %all-to-all-start.3 = ((f32[32,16,128]{2,1,0:T(8,128)}), f32[32,16,128]{2,1,0:T(8,128)S(1)}, u32[]{:S(2)}, u32[]{:S(2)}) async-start(f32[32,16,128]{2,1,0:T(8,128)} %bitcast.6), calls=%async_computation.3 | async-start | bytes 524288 | tf_op jit(solution)/shard_map/all_to_all | solution.py:334
  127.2 0.2 shard_map.88.refs_1_
  127.3 10.0 %all-to-all-done.3 = f32[32,16,128]{2,1,0:T(8,128)S(1)} async-done(((f32[32,16,128]{2,1,0:T(8,128)}), f32[32,16,128]{2,1,0:T(8,128)S(1)}, u32[]{:S(2)}, u32[]{:S(2)}) %all-to-all-start.3) | async-done | bytes 262176 | tf_op jit(solution)/shard_map/all_to_all | solution.py:334
  137.4 0.7 shard_map.89
  138.1 1.0 collective-permute-start.15
  139.1 1.5 collective-permute-start.14
  140.6 1.0 collective-permute-start.13
  141.6 0.8 shard_map.91
  142.3 2.7 %all-to-all-start.5 = ((f32[32,16,128]{2,1,0:T(8,128)}), f32[32,16,128]{2,1,0:T(8,128)S(1)}, u32[]{:S(2)}, u32[]{:S(2)}) async-start(f32[32,16,128]{2,1,0:T(8,128)} %bitcast.9), calls=%async_computation.5 | async-start | bytes 524288 | tf_op jit(solution)/shard_map/all_to_all | solution.py:334
  145.1 0.3 collective-permute-start.16
  145.4 1.3 collective-permute-done.16
  146.7 6.1 %shard_map.90 = f32[256,256]{1,0:T(8,128)} custom-call(s32[1,1]{1,0:T(1,128)S(6)} %copy.22.count_ref, s32[1,1,16,3]{3,2,1,0:T(8,128)S(1)} %copy.8.coords_ref, bf16[8,64,4096]{2,1,0:T(8,128)(2,1)} %shard_map.82.refs_0_, bf16[8,64,4096]{2,1,0:T(8,128)(2,1)} %shard_map.88.refs_1_, bf16[1024,256]{1,0:T(8,128)(2,1)S(1)} %constant_dynamic-update-slice_fusion.9.refs_2_, ...), custom_call_target="tpu_custom_call" | custom-call | flops 2147483648 | bytes 8388608 | tf_op jit(solution)/shard_map/pallas_call | solution.py:110
  152.8 2.4 %all-to-all-done.5 = f32[32,16,128]{2,1,0:T(8,128)S(1)} async-done(((f32[32,16,128]{2,1,0:T(8,128)}), f32[32,16,128]{2,1,0:T(8,128)S(1)}, u32[]{:S(2)}, u32[]{:S(2)}) %all-to-all-start.5) | async-done | bytes 262176 | tf_op jit(solution)/shard_map/all_to_all | solution.py:334
  155.2 5.2 %all-to-all-start.4 = ((f32[32,8,256]{2,1,0:T(8,128)}), f32[32,8,256]{2,1,0:T(8,128)S(1)}, u32[]{:S(2)}, u32[]{:S(2)}) async-start(f32[32,8,256]{2,1,0:T(8,128)} %bitcast.8), calls=%async_computation.4 | async-start | bytes 524288 | tf_op jit(solution)/shard_map/all_to_all | solution.py:182
  160.5 11.0 %shard_map.92.refs_1_ = f32[256,256]{1,0:T(8,128)S(1)} custom-call(f32[512,128]{1,0:T(8,128)S(1)} %bitcast.20, f32[1,256]{1,0:T(1,128)S(1)} %get-tuple-element.71.one_scale_ref, f32[512,128]{1,0:T(8,128)S(1)} %bitcast.21, f32[1,256]{1,0:T(1,128)S(1)} %get-tuple-element.82.two_scale_ref), custom_call_target="tpu_custom_call" | custom-call | flops 10000000000 | bytes 786432 | tf_op jit(solution)/shard_map/pallas_call | solution.py:408
  171.5 0.2 shard_map.93
  171.8 15.6 %all_to_all.73 = f32[32,8,256]{2,1,0:T(8,128)S(1)} all-to-all(f32[32,8,256]{2,1,0:T(8,128)S(1)} %tile.2), channel_id=1, replica_groups=mesh['slab'=8,'grid'=4] {'slab','grid'}, dimensions={0} | all-to-all | bytes 524288 | tf_op jit(solution)/shard_map/all_to_all | solution.py:188
  187.5 0.7 bitcast_divide_fusion
  (32 shorter events, 0.3 us)
Async XLA Ops:
  0.6 7.2 %collective-permute-start = (f32[128,256]{1,0:T(8,128)}, f32[128,256]{1,0:T(8,128)S(1)}, u32[]{:S(2)}, u32[]{:S(2)}) collective-permute-start(f32[128,256]{1,0:T(8,128)} %param.8), channel_id=1, source_target_pairs={{0,8},{4,12},{8,0},{12,4},{16,24},{20,28},{24,16},{28,20},{1,9},{5... | collective-permute-start | bytes 393224 | tf_op jit(solution)/shard_map/ppermute | solution.py:192
  3.6 8.5 %collective-permute-start.1 = (f32[128,256]{1,0:T(8,128)}, f32[128,256]{1,0:T(8,128)S(1)}, u32[]{:S(2)}, u32[]{:S(2)}) collective-permute-start(f32[128,256]{1,0:T(8,128)} %param.8), channel_id=1, source_target_pairs={{0,16},{4,20},{8,24},{12,28},{16,0},{20,4},{24,8},{28,12},{1,17},{... | collective-permute-start | bytes 393224 | tf_op jit(solution)/shard_map/ppermute | solution.py:192
  5.2 7.0 %collective-permute-start.2 = (f32[128,256]{1,0:T(8,128)}, f32[128,256]{1,0:T(8,128)S(1)}, u32[]{:S(2)}, u32[]{:S(2)}) collective-permute-start(f32[128,256]{1,0:T(8,128)} %param.8), channel_id=1, source_target_pairs={{0,24},{4,28},{8,16},{12,20},{16,8},{20,12},{24,0},{28,4},{1,25},{... | collective-permute-start | bytes 393224 | tf_op jit(solution)/shard_map/ppermute | solution.py:192
  7.9 4.3 %copy-start.1 = (f32[128,256]{1,0:T(8,128)S(1)}, f32[128,256]{1,0:T(8,128)}, u32[]{:S(2)}) copy-start(f32[128,256]{1,0:T(8,128)} %param.8) | copy-start | bytes 393220
  7.9 4.4 %copy-start.2 = (s32[1,1,16,3]{2,1,3,0:T(1,128)S(1)}, s32[1,1,16,3]{2,1,3,0:T(1,128)}, u32[]{:S(2)}) copy-start(s32[1,1,16,3]{2,1,3,0:T(1,128)} %param.6) | copy-start | bytes 580
  12.1 7.8 %copy-start = (f32[256,256]{1,0:T(8,128)S(1)}, f32[256,256]{1,0:T(8,128)}, u32[]{:S(2)}) copy-start(f32[256,256]{1,0:T(8,128)} %refs_3_.1) | copy-start | bytes 786436
  12.2 2.0 %collective-permute-start.3 = (f32[512,256]{1,0:T(8,128)S(1)}, f32[512,256]{1,0:T(8,128)S(1)}, u32[]{:S(2)}, u32[]{:S(2)}) collective-permute-start(f32[512,256]{1,0:T(8,128)S(1)} %pad_maximum_fusion), channel_id=1, source_target_pairs={{0,4},{4,0},{8,12},{12,8},{16,20},{20,16},{24,28},{28,24},{1,5},{5... | collective-permute-start | bytes 1572872 | tf_op jit(solution)/shard_map/ppermute | solution.py:192
  15.4 9.9 %collective-permute-start.6 = (f32[384,128]{1,0:T(8,128)S(1)}, f32[384,128]{1,0:T(8,128)S(1)}, u32[]{:S(2)}, u32[]{:S(2)}) collective-permute-start(f32[384,128]{1,0:T(8,128)S(1)} %shard_map.77), channel_id=1, source_target_pairs={{0,3},{1,2},{2,1},{3,0},{4,7},{5,6},{6,5},{7,4},{8,11},{9,10},{10,... | collective-permute-start | bytes 589832 | tf_op jit(solution)/shard_map/ppermute | solution.py:192
  18.6 17.8 %collective-permute-start.5 = (f32[384,128]{1,0:T(8,128)S(1)}, f32[384,128]{1,0:T(8,128)S(1)}, u32[]{:S(2)}, u32[]{:S(2)}) collective-permute-start(f32[384,128]{1,0:T(8,128)S(1)} %shard_map.77), channel_id=1, source_target_pairs={{0,2},{1,3},{2,0},{3,1},{4,6},{5,7},{6,4},{7,5},{8,10},{9,11},{10,... | collective-permute-start | bytes 589832 | tf_op jit(solution)/shard_map/ppermute | solution.py:192
  18.6 17.8 %collective-permute-start.4 = (f32[384,128]{1,0:T(8,128)S(1)}, f32[384,128]{1,0:T(8,128)S(1)}, u32[]{:S(2)}, u32[]{:S(2)}) collective-permute-start(f32[384,128]{1,0:T(8,128)S(1)} %shard_map.77), channel_id=1, source_target_pairs={{0,1},{1,0},{2,3},{3,2},{4,5},{5,4},{6,7},{7,6},{8,9},{9,8},{10,11... | collective-permute-start | bytes 589832 | tf_op jit(solution)/shard_map/ppermute | solution.py:192
  37.0 15.7 %collective-permute-start.9 = (f32[256,256]{1,0:T(8,128)S(1)}, f32[256,256]{1,0:T(8,128)S(1)}, u32[]{:S(2)}, u32[]{:S(2)}) collective-permute-start(f32[256,256]{1,0:T(8,128)S(1)} %get-tuple-element.83), channel_id=1, source_target_pairs={{0,3},{1,2},{2,1},{3,0},{4,7},{5,6},{6,5},{7,4},{8,11},{9,10},{10,... | collective-permute-start | bytes 786440 | tf_op jit(solution)/shard_map/ppermute | solution.py:192
  39.7 21.0 %collective-permute-start.8 = (f32[256,256]{1,0:T(8,128)S(1)}, f32[256,256]{1,0:T(8,128)S(1)}, u32[]{:S(2)}, u32[]{:S(2)}) collective-permute-start(f32[256,256]{1,0:T(8,128)S(1)} %get-tuple-element.84), channel_id=1, source_target_pairs={{0,2},{1,3},{2,0},{3,1},{4,6},{5,7},{6,4},{7,5},{8,10},{9,11},{10,... | collective-permute-start | bytes 786440 | tf_op jit(solution)/shard_map/ppermute | solution.py:192
  39.7 21.0 %collective-permute-start.7 = (f32[256,256]{1,0:T(8,128)S(1)}, f32[256,256]{1,0:T(8,128)S(1)}, u32[]{:S(2)}, u32[]{:S(2)}) collective-permute-start(f32[256,256]{1,0:T(8,128)S(1)} %get-tuple-element.85), channel_id=1, source_target_pairs={{0,1},{1,0},{2,3},{3,2},{4,5},{5,4},{6,7},{7,6},{8,9},{9,8},{10,11... | collective-permute-start | bytes 786440 | tf_op jit(solution)/shard_map/ppermute | solution.py:192
  62.6 15.2 %all-to-all-start = ((f32[32,16,128]{2,1,0:T(8,128)}), f32[32,16,128]{2,1,0:T(8,128)S(1)}, u32[]{:S(2)}, u32[]{:S(2)}) async-start(f32[32,16,128]{2,1,0:T(8,128)} %bitcast.1), calls=%async_computation | async-start | bytes 524288 | tf_op jit(solution)/shard_map/all_to_all | solution.py:334
  78.5 6.1 %collective-permute-start.10 = (bf16[256,256]{1,0:T(8,128)(2,1)S(1)}, bf16[256,256]{1,0:T(8,128)(2,1)S(1)}, u32[]{:S(2)}, u32[]{:S(2)}) collective-permute-start(bf16[256,256]{1,0:T(8,128)(2,1)S(1)} %get-tuple-element.68), channel_id=1, source_target_pairs={{0,1},{1,0},{2,3},{3,2},{4,5},{5,4},{6,7},{7,6},{8,9},{9,8},{10,11... | collective-permute-start | bytes 393224 | tf_op jit(solution)/shard_map/ppermute | solution.py:192
  79.6 18.0 %collective-permute-start.12 = (bf16[256,256]{1,0:T(8,128)(2,1)S(1)}, bf16[256,256]{1,0:T(8,128)(2,1)S(1)}, u32[]{:S(2)}, u32[]{:S(2)}) collective-permute-start(bf16[256,256]{1,0:T(8,128)(2,1)S(1)} %get-tuple-element.68), channel_id=1, source_target_pairs={{0,3},{1,2},{2,1},{3,0},{4,7},{5,6},{6,5},{7,4},{8,11},{9,10},{10,... | collective-permute-start | bytes 393224 | tf_op jit(solution)/shard_map/ppermute | solution.py:192
  80.8 16.9 %collective-permute-start.11 = (bf16[256,256]{1,0:T(8,128)(2,1)S(1)}, bf16[256,256]{1,0:T(8,128)(2,1)S(1)}, u32[]{:S(2)}, u32[]{:S(2)}) collective-permute-start(bf16[256,256]{1,0:T(8,128)(2,1)S(1)} %get-tuple-element.68), channel_id=1, source_target_pairs={{0,2},{1,3},{2,0},{3,1},{4,6},{5,7},{6,4},{7,5},{8,10},{9,11},{10,... | collective-permute-start | bytes 393224 | tf_op jit(solution)/shard_map/ppermute | solution.py:192
  85.4 18.6 %all-to-all-start.2 = ((f32[32,16,128]{2,1,0:T(8,128)}), f32[32,16,128]{2,1,0:T(8,128)S(1)}, u32[]{:S(2)}, u32[]{:S(2)}) async-start(f32[32,16,128]{2,1,0:T(8,128)} %bitcast.4), calls=%async_computation.2 | async-start | bytes 524288 | tf_op jit(solution)/shard_map/all_to_all | solution.py:334
  104.0 18.9 %all-to-all-start.1 = ((f32[8,128,256]{2,1,0:T(8,128)}), f32[8,128,256]{2,1,0:T(8,128)S(1)}, u32[]{:S(2)}, u32[]{:S(2)}) async-start(f32[8,128,256]{2,1,0:T(8,128)} %bitcast.3), calls=%async_computation.1 | async-start | bytes 2097152 | tf_op jit(solution)/shard_map/all_to_all | solution.py:182
  124.6 12.8 %all-to-all-start.3 = ((f32[32,16,128]{2,1,0:T(8,128)}), f32[32,16,128]{2,1,0:T(8,128)S(1)}, u32[]{:S(2)}, u32[]{:S(2)}) async-start(f32[32,16,128]{2,1,0:T(8,128)} %bitcast.6), calls=%async_computation.3 | async-start | bytes 524288 | tf_op jit(solution)/shard_map/all_to_all | solution.py:334
  138.1 7.0 %collective-permute-start.15 = (bf16[128,256]{1,0:T(8,128)(2,1)S(1)}, bf16[128,256]{1,0:T(8,128)(2,1)S(1)}, u32[]{:S(2)}, u32[]{:S(2)}) collective-permute-start(bf16[128,256]{1,0:T(8,128)(2,1)S(1)} %get-tuple-element.80), channel_id=1, source_target_pairs={{0,24},{4,28},{8,16},{12,20},{16,8},{20,12},{24,0},{28,4},{1,25},{... | collective-permute-start | bytes 196616 | tf_op jit(solution)/shard_map/ppermute | solution.py:192
  139.1 6.0 %collective-permute-start.14 = (bf16[128,256]{1,0:T(8,128)(2,1)S(1)}, bf16[128,256]{1,0:T(8,128)(2,1)S(1)}, u32[]{:S(2)}, u32[]{:S(2)}) collective-permute-start(bf16[128,256]{1,0:T(8,128)(2,1)S(1)} %get-tuple-element.80), channel_id=1, source_target_pairs={{0,16},{4,20},{8,24},{12,28},{16,0},{20,4},{24,8},{28,12},{1,17},{... | collective-permute-start | bytes 196616 | tf_op jit(solution)/shard_map/ppermute | solution.py:192
  140.6 4.5 %collective-permute-start.13 = (bf16[128,256]{1,0:T(8,128)(2,1)S(1)}, bf16[128,256]{1,0:T(8,128)(2,1)S(1)}, u32[]{:S(2)}, u32[]{:S(2)}) collective-permute-start(bf16[128,256]{1,0:T(8,128)(2,1)S(1)} %get-tuple-element.80), channel_id=1, source_target_pairs={{0,8},{4,12},{8,0},{12,4},{16,24},{20,28},{24,16},{28,20},{1,9},{5... | collective-permute-start | bytes 196616 | tf_op jit(solution)/shard_map/ppermute | solution.py:192
  142.3 12.9 %all-to-all-start.5 = ((f32[32,16,128]{2,1,0:T(8,128)}), f32[32,16,128]{2,1,0:T(8,128)S(1)}, u32[]{:S(2)}, u32[]{:S(2)}) async-start(f32[32,16,128]{2,1,0:T(8,128)} %bitcast.9), calls=%async_computation.5 | async-start | bytes 524288 | tf_op jit(solution)/shard_map/all_to_all | solution.py:334
  145.1 1.6 collective-permute-start.16
  155.2 16.3 %all-to-all-start.4 = ((f32[32,8,256]{2,1,0:T(8,128)}), f32[32,8,256]{2,1,0:T(8,128)S(1)}, u32[]{:S(2)}, u32[]{:S(2)}) async-start(f32[32,8,256]{2,1,0:T(8,128)} %bitcast.8), calls=%async_computation.4 | async-start | bytes 524288 | tf_op jit(solution)/shard_map/all_to_all | solution.py:182

commit v5 on v4

--- a/solution.py
+++ b/solution.py
@@ -336,7 +336,9 @@
 
 def panel_gram_kernel(panel_ref, packed_ref):
     panel = panel_ref[...]
-    packed_ref[...] = packed_blocks(exact_dot(panel, panel, ((0,), (0,))))
+    packed = packed_blocks(exact_dot(panel, panel, ((0,), (0,))))
+    rows = packed_ref.shape[0]
+    packed_ref[...] = jnp.where(lax.axis_index("slab") % 2 == 0, packed[:rows], packed[rows:])
 
 
 def fold_kernel(devices, parts_ref, spread_ref):
@@ -350,7 +352,7 @@
 def panel_gram(panel):
     return pl.pallas_call(
         panel_gram_kernel,
-        out_shape=jax.ShapeDtypeStruct((3 * LANES, LANES), F32),
+        out_shape=jax.ShapeDtypeStruct((3 * LANES // 2, LANES), F32),
         compiler_params=pltpu.CompilerParams(vmem_limit_bytes=10 << 20),
     )(panel)
 
@@ -501,7 +503,13 @@
     )
     grams_b, moments_a = lax.optimization_barrier((grams_b, moments_a))
     others_a = swap_pieces(moments_a, "grid")
-    gram_b = (functools.reduce(jnp.add, grams_b), term_total, ones)
+    half_b = functools.reduce(jnp.add, grams_b)
+    other_b = swap(half_b, "slab", 1)
+    even_device = lax.axis_index("slab") % 2 == 0
+    packed_b = jnp.concatenate(
+        [jnp.where(even_device, half_b, other_b), jnp.where(even_device, other_b, half_b)], 0
+    )
+    gram_b = (packed_b, term_total, ones)
     c_held, _ = lax.optimization_barrier((c_init, moments_a))
     gram_c = (gram_local(c_held), month_total, ones)
     inverse_a = product_inverse(gram_b, gram_c, devices)

time: 189 us -> 182 us (0.963)
  Pallas kernels: 68.8 us -> 59.4 us
    pallas_call x3, Pallas kernels: 17.8 us -> 11.8 us  [block_moments(): pl.pallas_call(functools.partial(moments_kernel, mode, orders, len(blocks...]
    all_to_all x4, waiting for transfers between devices: 17.1 us -> 21.2 us  [swap_all(): lax.all_to_all(messages, BOTH, split_axis=0, concat_axis=0, tiled=True)]
    ppermute x17 -> x18, waiting for transfers between devices: 35.9 us -> 32.1 us  [swap(): lax.ppermute(rows, axis, [(i, i ^ step) for i in range(lax.axis_size(axis...]
    pallas_call x4, Pallas kernels: 10 us -> 6.74 us  [turned_blocks(): pl.pallas_call(functools.partial(turn_kernel, mode, half * slots), in_spe...]
    ppermute x17 -> x18, starting transfers between devices: 20.8 us -> 21 us  [swap(): lax.ppermute(rows, axis, [(i, i ^ step) for i in range(lax.axis_size(axis...]
  transfers between devices with their start and end apart: 23 -> 24, of which waited for: 11 -> 12; matrix products, arithmetic and copies ran while one was open for 0% -> 0% of each run, Pallas kernels for 33% -> 29%
where the time goes in v5:
time: 182 us; the launch traced here: 181 us
  Pallas kernels  59.4 us (33%)
  waiting for transfers between devices  57.7 us (32%)
  starting transfers between devices  44.2 us (24%)
  blocking collectives  15.6 us (9%)
    pallas_call x3, Pallas kernels, product_inverse(): pl.pallas_call(functools.partial(inverse_kernel, devices, (one[1], two[1]...  33 us
    ppermute x18, waiting for transfers between devices, swap(): lax.ppermute(rows, axis, [(i, i ^ step) for i in range(lax.axis_size(axis...  32.1 us
    all_to_all x4, waiting for transfers between devices, swap_all(): lax.all_to_all(messages, BOTH, split_axis=0, concat_axis=0, tiled=True)  21.2 us
    ppermute x18, starting transfers between devices, swap(): lax.ppermute(rows, axis, [(i, i ^ step) for i in range(lax.axis_size(axis...  21 us
    all_to_all x1, blocking collectives, spread_rows(): lax.all_to_all(jnp.tile(rows, (devices, 1)), axes, split_axis=0, concat_a...  15.6 us
    all_to_all x4, starting transfers between devices, swap_all(): lax.all_to_all(messages, BOTH, split_axis=0, concat_axis=0, tiled=True)  14 us
    pallas_call x3, Pallas kernels, block_moments(): pl.pallas_call(functools.partial(moments_kernel, mode, orders, len(blocks...  11.8 us
    all_to_all x2, starting transfers between devices, exchange(): parts = lax.all_to_all(rows, axes, split_axis=0, concat_axis=0, tiled=True)  9.23 us
  transfers between devices with their start and end apart: 24, of which 12 were waited for; matrix products, arithmetic and copies ran while one was open for 0% of the time, Pallas kernels for 29%

profile of v5, /device:TPU:0, one launch (start us, length us, event | category | flops | bytes accessed | tf_op | source)
XLA Modules:
  0.0 180.5 jit_solution(15789376829547444111)
XLA Ops:
  0.6 3.0 %collective-permute-start = (f32[128,256]{1,0:T(8,128)}, f32[128,256]{1,0:T(8,128)S(1)}, u32[]{:S(2)}, u32[]{:S(2)}) collective-permute-start(f32[128,256]{1,0:T(8,128)} %param.8), channel_id=1, source_target_pairs={{0,8},{4,12},{8,0},{12,4},{16,24},{20,28},{24,16},{28,20},{1,9},{5... | collective-permute-start | bytes 393224 | tf_op jit(solution)/shard_map/ppermute | solution.py:192
  3.6 1.5 collective-permute-start.1
  5.2 0.0 collective-permute-start.2
  5.8 2.0 %collective-permute-done = f32[128,256]{1,0:T(8,128)S(1)} collective-permute-done((f32[128,256]{1,0:T(8,128)}, f32[128,256]{1,0:T(8,128)S(1)}, u32[]{:S(2)}, u32[]{:S(2)}) %collective-permute-start) | collective-permute-done | bytes 131104 | tf_op jit(solution)/shard_map/ppermute | solution.py:192
  7.9 2.9 %shard_map.76.refs_0_ = bf16[8,64,4096]{2,1,0:T(8,128)(2,1)} custom-call(s32[1,1]{1,0:T(1,128)S(6)} %copy.22.count_ref, bf16[16,64,4096]{2,1,0:T(8,128)(2,1)} %bitcast.22), custom_call_target="tpu_custom_call" | custom-call | bytes 16777216 | tf_op jit(solution)/shard_map/pallas_call | solution.py:163
  10.8 0.0 copy-start
  10.8 0.8 collective-permute-done.1
  11.6 0.0 collective-permute-done.2
  11.7 0.1 collective-permute-start.3
  11.8 0.1 copy.8.coords_ref
  11.9 1.7 collective-permute-done.3
  13.7 1.2 shard_map.77
  14.9 3.9 %collective-permute-start.6 = (f32[192,128]{1,0:T(8,128)S(1)}, f32[192,128]{1,0:T(8,128)S(1)}, u32[]{:S(2)}, u32[]{:S(2)}) collective-permute-start(f32[192,128]{1,0:T(8,128)S(1)} %shard_map.77), channel_id=1, source_target_pairs={{0,3},{1,2},{2,1},{3,0},{4,7},{5,6},{6,5},{7,4},{8,11},{9,10},{10,... | collective-permute-start | bytes 294920 | tf_op jit(solution)/shard_map/ppermute | solution.py:192
  18.8 0.6 collective-permute-start.4
  19.5 3.4 %shard_map.78.refs_0_ = f32[1024,256]{1,0:T(8,128)S(1)} custom-call(s32[1,1]{1,0:T(1,128)S(6)} %copy.22.count_ref, s32[1,1,16,3]{3,2,1,0:T(8,128)S(1)} %copy.8.coords_ref, bf16[16,64,4096]{2,1,0:T(8,128)(2,1)} %bitcast.23, f32[1024,256]{1,0:T(8,128)S(1)} %constant_dynamic-update-slice_fusion.panel_ref.refs_1_, f32[256,256]{1,0:T(8,128)S(1)} %copy-done), custom_call_target="tpu_custom_call" | custom-call | flops 2147483648 | bytes 8388608 | tf_op jit(solution)/shard_map/pallas_call | solution.py:110
  22.8 0.0 collective-permute-done.6
  22.8 5.1 %collective-permute-done.5 = f32[192,128]{1,0:T(8,128)S(1)} collective-permute-done((f32[192,128]{1,0:T(8,128)S(1)}, f32[192,128]{1,0:T(8,128)S(1)}, u32[]{:S(2)}, u32[]{:S(2)}) %collective-permute-start.5) | collective-permute-done | bytes 98336 | tf_op jit(solution)/shard_map/ppermute | solution.py:192
  27.9 0.1 fusion
  28.0 0.1 collective-permute-start.10
  28.1 0.6 fusion.1.two_ref
  28.7 2.7 %collective-permute-start.9 = (f32[256,256]{1,0:T(8,128)S(1)}, f32[256,256]{1,0:T(8,128)S(1)}, u32[]{:S(2)}, u32[]{:S(2)}) collective-permute-start(f32[256,256]{1,0:T(8,128)S(1)} %get-tuple-element.83), channel_id=1, source_target_pairs={{0,3},{1,2},{2,1},{3,0},{4,7},{5,6},{6,5},{7,4},{8,11},{9,10},{10,... | collective-permute-start | bytes 786440 | tf_op jit(solution)/shard_map/ppermute | solution.py:192
  31.4 0.0 collective-permute-start.8
  31.4 1.7 collective-permute-start.7
  33.1 0.0 collective-permute-done.10
  33.2 11.0 %shard_map.79.refs_4_ = f32[256,256]{1,0:T(8,128)S(1)} custom-call(f32[384,128]{1,0:T(8,128)S(1)} %pad_maximum_fusion.2.one_ref, f32[1,256]{1,0:T(1,128)S(1)} %broadcast_in_dim.4.one_scale_ref.two_scale_ref, f32[256,256]{1,0:T(8,128)S(1)} %fusion.1.two_ref, f32[1,256]{1,0:T(1,128)S(1)} %broadcast_in_dim.4.one_scale_ref.two_scale_ref), custom_call_target="tpu_custom_call" | custom-call | flops 10000000000 | bytes 786432 | tf_op jit(solution)/shard_map/pallas_call | solution.py:410
  44.2 0.2 shard_map.80.refs_1_
  44.4 0.0 collective-permute-done.9.refs_3_
  44.4 9.4 %collective-permute-done.8.refs_2_ = f32[256,256]{1,0:T(8,128)S(1)} collective-permute-done((f32[256,256]{1,0:T(8,128)S(1)}, f32[256,256]{1,0:T(8,128)S(1)}, u32[]{:S(2)}, u32[]{:S(2)}) %collective-permute-start.8) | collective-permute-done | bytes 262176 | tf_op jit(solution)/shard_map/ppermute | solution.py:192
  53.8 1.9 %shard_map.81 = (f32[256,256]{1,0:T(8,128)S(1)}, f32[512,128]{1,0:T(8,128)}) custom-call(f32[1024,256]{1,0:T(8,128)S(1)} %shard_map.78.refs_0_, f32[256,256]{1,0:T(8,128)S(1)} %collective-permute-done.7.refs_1_, f32[256,256]{1,0:T(8,128)S(1)} %collective-permute-done.8.refs_2_, f32[256,256]{1,0:T(8,128)S(1)} %collective-permute-done.9.refs_3_, ...), custom_call_target="tpu_custom_call" | custom-call | tf_op jit(solution)/shard_map/pallas_call | solution.py:437
  55.6 5.5 %all-to-all-start = ((f32[32,16,128]{2,1,0:T(8,128)}), f32[32,16,128]{2,1,0:T(8,128)S(1)}, u32[]{:S(2)}, u32[]{:S(2)}) async-start(f32[32,16,128]{2,1,0:T(8,128)} %bitcast.1), calls=%async_computation | async-start | bytes 524288 | tf_op jit(solution)/shard_map/all_to_all | solution.py:334
  61.1 3.5 %shard_map.82.refs_0_ = bf16[8,64,4096]{2,1,0:T(8,128)(2,1)} custom-call(s32[1,1]{1,0:T(1,128)S(6)} %copy.22.count_ref, bf16[16,64,4096]{2,1,0:T(8,128)(2,1)} %bitcast.25), custom_call_target="tpu_custom_call" | custom-call | bytes 16777216 | tf_op jit(solution)/shard_map/pallas_call | solution.py:163
  64.6 6.7 %all-to-all-done = f32[32,16,128]{2,1,0:T(8,128)S(1)} async-done(((f32[32,16,128]{2,1,0:T(8,128)}), f32[32,16,128]{2,1,0:T(8,128)S(1)}, u32[]{:S(2)}, u32[]{:S(2)}) %all-to-all-start) | async-done | bytes 262176 | tf_op jit(solution)/shard_map/all_to_all | solution.py:334
  71.3 0.8 shard_map.83
  72.1 1.1 collective-permute-start.11
  73.2 1.1 collective-permute-start.13
  74.3 1.3 collective-permute-start.12
  75.6 2.6 %collective-permute-done.11 = bf16[256,256]{1,0:T(8,128)(2,1)S(1)} collective-permute-done((bf16[256,256]{1,0:T(8,128)(2,1)S(1)}, bf16[256,256]{1,0:T(8,128)(2,1)S(1)}, u32[]{:S(2)}, u32[]{:S(2)}) %collective-permute-start.11) | collective-permute-done | bytes 131104 | tf_op jit(solution)/shard_map/ppermute | solution.py:192
  78.2 0.8 shard_map.85
  78.9 3.0 %all-to-all-start.2 = ((f32[32,16,128]{2,1,0:T(8,128)}), f32[32,16,128]{2,1,0:T(8,128)S(1)}, u32[]{:S(2)}, u32[]{:S(2)}) async-start(f32[32,16,128]{2,1,0:T(8,128)} %bitcast.4), calls=%async_computation.2 | async-start | bytes 524288 | tf_op jit(solution)/shard_map/all_to_all | solution.py:334
  81.9 9.2 %collective-permute-done.12 = bf16[256,256]{1,0:T(8,128)(2,1)S(1)} collective-permute-done((bf16[256,256]{1,0:T(8,128)(2,1)S(1)}, bf16[256,256]{1,0:T(8,128)(2,1)S(1)}, u32[]{:S(2)}, u32[]{:S(2)}) %collective-permute-start.12) | collective-permute-done | bytes 131104 | tf_op jit(solution)/shard_map/ppermute | solution.py:192
  91.2 0.0 collective-permute-done.13
  91.2 4.3 %shard_map.84 = f32[1024,256]{1,0:T(8,128)} custom-call(s32[1,1]{1,0:T(1,128)S(6)} %copy.22.count_ref, s32[1,1,16,3]{3,2,1,0:T(8,128)S(1)} %copy.8.coords_ref, bf16[8,64,4096]{2,1,0:T(8,128)(2,1)} %shard_map.76.refs_0_, bf16[8,64,4096]{2,1,0:T(8,128)(2,1)} %shard_map.80.refs_1_, bf16[1024,256]{1,0:T(8,128)(2,1)S(1)} %constant_dynamic-update-slice_fusion.5.refs_2_.refs_3_, ...), custom_call_target="tpu_custom_call" | custom-call | flops 2147483648 | bytes 8388608 | tf_op jit(solution)/shard_map/pallas_call | solution.py:110
  95.6 4.0 %all-to-all-start.1 = ((f32[8,128,256]{2,1,0:T(8,128)}), f32[8,128,256]{2,1,0:T(8,128)S(1)}, u32[]{:S(2)}, u32[]{:S(2)}) async-start(f32[8,128,256]{2,1,0:T(8,128)} %bitcast.3), calls=%async_computation.1 | async-start | bytes 2097152 | tf_op jit(solution)/shard_map/all_to_all | solution.py:182
  99.6 11.0 %shard_map.86.refs_1_ = f32[256,256]{1,0:T(8,128)S(1)} custom-call(f32[512,128]{1,0:T(8,128)S(1)} %bitcast.19, f32[1,256]{1,0:T(1,128)S(1)} %get-tuple-element.71.one_scale_ref, f32[256,256]{1,0:T(8,128)S(1)} %fusion.1.two_ref, f32[1,256]{1,0:T(1,128)S(1)} %broadcast_in_dim.4.one_scale_ref.two_scale_ref), custom_call_target="tpu_custom_call" | custom-call | flops 10000000000 | bytes 786432 | tf_op jit(solution)/shard_map/pallas_call | solution.py:410
  110.5 4.4 %all-to-all-done.1.refs_0_ = f32[8,128,256]{2,1,0:T(8,128)S(1)} async-done(((f32[8,128,256]{2,1,0:T(8,128)}), f32[8,128,256]{2,1,0:T(8,128)S(1)}, u32[]{:S(2)}, u32[]{:S(2)}) %all-to-all-start.1) | async-done | bytes 1048608 | tf_op jit(solution)/shard_map/all_to_all | solution.py:182
  115.0 1.6 shard_map.87
  116.6 2.8 %all-to-all-start.3 = ((f32[32,16,128]{2,1,0:T(8,128)}), f32[32,16,128]{2,1,0:T(8,128)S(1)}, u32[]{:S(2)}, u32[]{:S(2)}) async-start(f32[32,16,128]{2,1,0:T(8,128)} %bitcast.6), calls=%async_computation.3 | async-start | bytes 524288 | tf_op jit(solution)/shard_map/all_to_all | solution.py:334
  119.4 0.2 shard_map.88.refs_1_
  119.6 10.0 %all-to-all-done.3 = f32[32,16,128]{2,1,0:T(8,128)S(1)} async-done(((f32[32,16,128]{2,1,0:T(8,128)}), f32[32,16,128]{2,1,0:T(8,128)S(1)}, u32[]{:S(2)}, u32[]{:S(2)}) %all-to-all-start.3) | async-done | bytes 262176 | tf_op jit(solution)/shard_map/all_to_all | solution.py:334
  129.6 0.7 shard_map.89
  130.3 1.0 collective-permute-start.16
  131.3 1.5 collective-permute-start.15
  132.8 1.0 collective-permute-start.14
  133.8 0.8 shard_map.91
  134.6 2.7 %all-to-all-start.5 = ((f32[32,16,128]{2,1,0:T(8,128)}), f32[32,16,128]{2,1,0:T(8,128)S(1)}, u32[]{:S(2)}, u32[]{:S(2)}) async-start(f32[32,16,128]{2,1,0:T(8,128)} %bitcast.9), calls=%async_computation.5 | async-start | bytes 524288 | tf_op jit(solution)/shard_map/all_to_all | solution.py:334
  137.4 0.3 collective-permute-start.17
  137.8 1.3 collective-permute-done.17
  139.0 4.1 %shard_map.90 = f32[256,256]{1,0:T(8,128)} custom-call(s32[1,1]{1,0:T(1,128)S(6)} %copy.22.count_ref, s32[1,1,16,3]{3,2,1,0:T(8,128)S(1)} %copy.8.coords_ref, bf16[8,64,4096]{2,1,0:T(8,128)(2,1)} %shard_map.82.refs_0_, bf16[8,64,4096]{2,1,0:T(8,128)(2,1)} %shard_map.88.refs_1_, bf16[1024,256]{1,0:T(8,128)(2,1)S(1)} %constant_dynamic-update-slice_fusion.9.refs_2_, ...), custom_call_target="tpu_custom_call" | custom-call | flops 2147483648 | bytes 8388608 | tf_op jit(solution)/shard_map/pallas_call | solution.py:110
  143.1 4.4 %all-to-all-done.5 = f32[32,16,128]{2,1,0:T(8,128)S(1)} async-done(((f32[32,16,128]{2,1,0:T(8,128)}), f32[32,16,128]{2,1,0:T(8,128)S(1)}, u32[]{:S(2)}, u32[]{:S(2)}) %all-to-all-start.5) | async-done | bytes 262176 | tf_op jit(solution)/shard_map/all_to_all | solution.py:334
  147.5 5.2 %all-to-all-start.4 = ((f32[32,8,256]{2,1,0:T(8,128)}), f32[32,8,256]{2,1,0:T(8,128)S(1)}, u32[]{:S(2)}, u32[]{:S(2)}) async-start(f32[32,8,256]{2,1,0:T(8,128)} %bitcast.8), calls=%async_computation.4 | async-start | bytes 524288 | tf_op jit(solution)/shard_map/all_to_all | solution.py:182
  152.8 11.0 %shard_map.92.refs_1_ = f32[256,256]{1,0:T(8,128)S(1)} custom-call(f32[512,128]{1,0:T(8,128)S(1)} %bitcast.20, f32[1,256]{1,0:T(1,128)S(1)} %get-tuple-element.71.one_scale_ref, f32[512,128]{1,0:T(8,128)S(1)} %bitcast.21, f32[1,256]{1,0:T(1,128)S(1)} %get-tuple-element.82.two_scale_ref), custom_call_target="tpu_custom_call" | custom-call | flops 10000000000 | bytes 786432 | tf_op jit(solution)/shard_map/pallas_call | solution.py:410
  163.8 0.2 shard_map.93
  164.1 15.6 %all_to_all.73 = f32[32,8,256]{2,1,0:T(8,128)S(1)} all-to-all(f32[32,8,256]{2,1,0:T(8,128)S(1)} %tile.2), channel_id=1, replica_groups=mesh['slab'=8,'grid'=4] {'slab','grid'}, dimensions={0} | all-to-all | bytes 524288 | tf_op jit(solution)/shard_map/all_to_all | solution.py:188
  179.8 0.7 bitcast_divide_fusion
  (36 shorter events, 0.4 us)
Async XLA Ops:
  0.6 7.2 %collective-permute-start = (f32[128,256]{1,0:T(8,128)}, f32[128,256]{1,0:T(8,128)S(1)}, u32[]{:S(2)}, u32[]{:S(2)}) collective-permute-start(f32[128,256]{1,0:T(8,128)} %param.8), channel_id=1, source_target_pairs={{0,8},{4,12},{8,0},{12,4},{16,24},{20,28},{24,16},{28,20},{1,9},{5... | collective-permute-start | bytes 393224 | tf_op jit(solution)/shard_map/ppermute | solution.py:192
  3.6 8.0 %collective-permute-start.1 = (f32[128,256]{1,0:T(8,128)}, f32[128,256]{1,0:T(8,128)S(1)}, u32[]{:S(2)}, u32[]{:S(2)}) collective-permute-start(f32[128,256]{1,0:T(8,128)} %param.8), channel_id=1, source_target_pairs={{0,16},{4,20},{8,24},{12,28},{16,0},{20,4},{24,8},{28,12},{1,17},{... | collective-permute-start | bytes 393224 | tf_op jit(solution)/shard_map/ppermute | solution.py:192
  5.2 6.5 %collective-permute-start.2 = (f32[128,256]{1,0:T(8,128)}, f32[128,256]{1,0:T(8,128)S(1)}, u32[]{:S(2)}, u32[]{:S(2)}) collective-permute-start(f32[128,256]{1,0:T(8,128)} %param.8), channel_id=1, source_target_pairs={{0,24},{4,28},{8,16},{12,20},{16,8},{20,12},{24,0},{28,4},{1,25},{... | collective-permute-start | bytes 393224 | tf_op jit(solution)/shard_map/ppermute | solution.py:192
  7.9 3.8 %copy-start.1 = (f32[128,256]{1,0:T(8,128)S(1)}, f32[128,256]{1,0:T(8,128)}, u32[]{:S(2)}) copy-start(f32[128,256]{1,0:T(8,128)} %param.8) | copy-start | bytes 393220
  7.9 3.9 %copy-start.2 = (s32[1,1,16,3]{2,1,3,0:T(1,128)S(1)}, s32[1,1,16,3]{2,1,3,0:T(1,128)}, u32[]{:S(2)}) copy-start(s32[1,1,16,3]{2,1,3,0:T(1,128)} %param.6) | copy-start | bytes 580
  10.8 8.7 %copy-start = (f32[256,256]{1,0:T(8,128)S(1)}, f32[256,256]{1,0:T(8,128)}, u32[]{:S(2)}) copy-start(f32[256,256]{1,0:T(8,128)} %refs_3_.1) | copy-start | bytes 786436
  11.7 2.0 %collective-permute-start.3 = (f32[512,256]{1,0:T(8,128)S(1)}, f32[512,256]{1,0:T(8,128)S(1)}, u32[]{:S(2)}, u32[]{:S(2)}) collective-permute-start(f32[512,256]{1,0:T(8,128)S(1)} %pad_maximum_fusion), channel_id=1, source_target_pairs={{0,4},{4,0},{8,12},{12,8},{16,20},{20,16},{24,28},{28,24},{1,5},{5... | collective-permute-start | bytes 1572872 | tf_op jit(solution)/shard_map/ppermute | solution.py:192
  14.9 7.9 %collective-permute-start.6 = (f32[192,128]{1,0:T(8,128)S(1)}, f32[192,128]{1,0:T(8,128)S(1)}, u32[]{:S(2)}, u32[]{:S(2)}) collective-permute-start(f32[192,128]{1,0:T(8,128)S(1)} %shard_map.77), channel_id=1, source_target_pairs={{0,3},{1,2},{2,1},{3,0},{4,7},{5,6},{6,5},{7,4},{8,11},{9,10},{10,... | collective-permute-start | bytes 294920 | tf_op jit(solution)/shard_map/ppermute | solution.py:192
  18.8 9.1 %collective-permute-start.5 = (f32[192,128]{1,0:T(8,128)S(1)}, f32[192,128]{1,0:T(8,128)S(1)}, u32[]{:S(2)}, u32[]{:S(2)}) collective-permute-start(f32[192,128]{1,0:T(8,128)S(1)} %shard_map.77), channel_id=1, source_target_pairs={{0,2},{1,3},{2,0},{3,1},{4,6},{5,7},{6,4},{7,5},{8,10},{9,11},{10,... | collective-permute-start | bytes 294920 | tf_op jit(solution)/shard_map/ppermute | solution.py:192
  18.8 9.1 %collective-permute-start.4 = (f32[192,128]{1,0:T(8,128)S(1)}, f32[192,128]{1,0:T(8,128)S(1)}, u32[]{:S(2)}, u32[]{:S(2)}) collective-permute-start(f32[192,128]{1,0:T(8,128)S(1)} %shard_map.77), channel_id=1, source_target_pairs={{0,1},{1,0},{2,3},{3,2},{4,5},{5,4},{6,7},{7,6},{8,9},{9,8},{10,11... | collective-permute-start | bytes 294920 | tf_op jit(solution)/shard_map/ppermute | solution.py:192
  28.0 5.1 %collective-permute-start.10 = (f32[192,128]{1,0:T(8,128)S(1)}, f32[192,128]{1,0:T(8,128)S(1)}, u32[]{:S(2)}, u32[]{:S(2)}) collective-permute-start(f32[192,128]{1,0:T(8,128)S(1)} %add_add_fusion), channel_id=1, source_target_pairs={{0,4},{4,0},{8,12},{12,8},{16,20},{20,16},{24,28},{28,24},{1,5},{5... | collective-permute-start | bytes 294920 | tf_op jit(solution)/shard_map/ppermute | solution.py:192
  28.7 15.7 %collective-permute-start.9 = (f32[256,256]{1,0:T(8,128)S(1)}, f32[256,256]{1,0:T(8,128)S(1)}, u32[]{:S(2)}, u32[]{:S(2)}) collective-permute-start(f32[256,256]{1,0:T(8,128)S(1)} %get-tuple-element.83), channel_id=1, source_target_pairs={{0,3},{1,2},{2,1},{3,0},{4,7},{5,6},{6,5},{7,4},{8,11},{9,10},{10,... | collective-permute-start | bytes 786440 | tf_op jit(solution)/shard_map/ppermute | solution.py:192
  31.4 22.4 %collective-permute-start.8 = (f32[256,256]{1,0:T(8,128)S(1)}, f32[256,256]{1,0:T(8,128)S(1)}, u32[]{:S(2)}, u32[]{:S(2)}) collective-permute-start(f32[256,256]{1,0:T(8,128)S(1)} %get-tuple-element.84), channel_id=1, source_target_pairs={{0,2},{1,3},{2,0},{3,1},{4,6},{5,7},{6,4},{7,5},{8,10},{9,11},{10,... | collective-permute-start | bytes 786440 | tf_op jit(solution)/shard_map/ppermute | solution.py:192
  31.4 22.4 %collective-permute-start.7 = (f32[256,256]{1,0:T(8,128)S(1)}, f32[256,256]{1,0:T(8,128)S(1)}, u32[]{:S(2)}, u32[]{:S(2)}) collective-permute-start(f32[256,256]{1,0:T(8,128)S(1)} %get-tuple-element.85), channel_id=1, source_target_pairs={{0,1},{1,0},{2,3},{3,2},{4,5},{5,4},{6,7},{7,6},{8,9},{9,8},{10,11... | collective-permute-start | bytes 786440 | tf_op jit(solution)/shard_map/ppermute | solution.py:192
  55.6 15.7 %all-to-all-start = ((f32[32,16,128]{2,1,0:T(8,128)}), f32[32,16,128]{2,1,0:T(8,128)S(1)}, u32[]{:S(2)}, u32[]{:S(2)}) async-start(f32[32,16,128]{2,1,0:T(8,128)} %bitcast.1), calls=%async_computation | async-start | bytes 524288 | tf_op jit(solution)/shard_map/all_to_all | solution.py:334
  72.1 6.1 %collective-permute-start.11 = (bf16[256,256]{1,0:T(8,128)(2,1)S(1)}, bf16[256,256]{1,0:T(8,128)(2,1)S(1)}, u32[]{:S(2)}, u32[]{:S(2)}) collective-permute-start(bf16[256,256]{1,0:T(8,128)(2,1)S(1)} %get-tuple-element.68), channel_id=1, source_target_pairs={{0,1},{1,0},{2,3},{3,2},{4,5},{5,4},{6,7},{7,6},{8,9},{9,8},{10,11... | collective-permute-start | bytes 393224 | tf_op jit(solution)/shard_map/ppermute | solution.py:192
  73.2 18.0 %collective-permute-start.13 = (bf16[256,256]{1,0:T(8,128)(2,1)S(1)}, bf16[256,256]{1,0:T(8,128)(2,1)S(1)}, u32[]{:S(2)}, u32[]{:S(2)}) collective-permute-start(bf16[256,256]{1,0:T(8,128)(2,1)S(1)} %get-tuple-element.68), channel_id=1, source_target_pairs={{0,3},{1,2},{2,1},{3,0},{4,7},{5,6},{6,5},{7,4},{8,11},{9,10},{10,... | collective-permute-start | bytes 393224 | tf_op jit(solution)/shard_map/ppermute | solution.py:192
  74.3 16.9 %collective-permute-start.12 = (bf16[256,256]{1,0:T(8,128)(2,1)S(1)}, bf16[256,256]{1,0:T(8,128)(2,1)S(1)}, u32[]{:S(2)}, u32[]{:S(2)}) collective-permute-start(bf16[256,256]{1,0:T(8,128)(2,1)S(1)} %get-tuple-element.68), channel_id=1, source_target_pairs={{0,2},{1,3},{2,0},{3,1},{4,6},{5,7},{6,4},{7,5},{8,10},{9,11},{10,... | collective-permute-start | bytes 393224 | tf_op jit(solution)/shard_map/ppermute | solution.py:192
  78.9 16.6 %all-to-all-start.2 = ((f32[32,16,128]{2,1,0:T(8,128)}), f32[32,16,128]{2,1,0:T(8,128)S(1)}, u32[]{:S(2)}, u32[]{:S(2)}) async-start(f32[32,16,128]{2,1,0:T(8,128)} %bitcast.4), calls=%async_computation.2 | async-start | bytes 524288 | tf_op jit(solution)/shard_map/all_to_all | solution.py:334
  95.6 19.4 %all-to-all-start.1 = ((f32[8,128,256]{2,1,0:T(8,128)}), f32[8,128,256]{2,1,0:T(8,128)S(1)}, u32[]{:S(2)}, u32[]{:S(2)}) async-start(f32[8,128,256]{2,1,0:T(8,128)} %bitcast.3), calls=%async_computation.1 | async-start | bytes 2097152 | tf_op jit(solution)/shard_map/all_to_all | solution.py:182
  116.6 13.0 %all-to-all-start.3 = ((f32[32,16,128]{2,1,0:T(8,128)}), f32[32,16,128]{2,1,0:T(8,128)S(1)}, u32[]{:S(2)}, u32[]{:S(2)}) async-start(f32[32,16,128]{2,1,0:T(8,128)} %bitcast.6), calls=%async_computation.3 | async-start | bytes 524288 | tf_op jit(solution)/shard_map/all_to_all | solution.py:334
  130.3 7.0 %collective-permute-start.16 = (bf16[128,256]{1,0:T(8,128)(2,1)S(1)}, bf16[128,256]{1,0:T(8,128)(2,1)S(1)}, u32[]{:S(2)}, u32[]{:S(2)}) collective-permute-start(bf16[128,256]{1,0:T(8,128)(2,1)S(1)} %get-tuple-element.80), channel_id=1, source_target_pairs={{0,24},{4,28},{8,16},{12,20},{16,8},{20,12},{24,0},{28,4},{1,25},{... | collective-permute-start | bytes 196616 | tf_op jit(solution)/shard_map/ppermute | solution.py:192
  131.3 6.0 %collective-permute-start.15 = (bf16[128,256]{1,0:T(8,128)(2,1)S(1)}, bf16[128,256]{1,0:T(8,128)(2,1)S(1)}, u32[]{:S(2)}, u32[]{:S(2)}) collective-permute-start(bf16[128,256]{1,0:T(8,128)(2,1)S(1)} %get-tuple-element.80), channel_id=1, source_target_pairs={{0,16},{4,20},{8,24},{12,28},{16,0},{20,4},{24,8},{28,12},{1,17},{... | collective-permute-start | bytes 196616 | tf_op jit(solution)/shard_map/ppermute | solution.py:192
  132.8 4.5 %collective-permute-start.14 = (bf16[128,256]{1,0:T(8,128)(2,1)S(1)}, bf16[128,256]{1,0:T(8,128)(2,1)S(1)}, u32[]{:S(2)}, u32[]{:S(2)}) collective-permute-start(bf16[128,256]{1,0:T(8,128)(2,1)S(1)} %get-tuple-element.80), channel_id=1, source_target_pairs={{0,8},{4,12},{8,0},{12,4},{16,24},{20,28},{24,16},{28,20},{1,9},{5... | collective-permute-start | bytes 196616 | tf_op jit(solution)/shard_map/ppermute | solution.py:192
  134.6 12.9 %all-to-all-start.5 = ((f32[32,16,128]{2,1,0:T(8,128)}), f32[32,16,128]{2,1,0:T(8,128)S(1)}, u32[]{:S(2)}, u32[]{:S(2)}) async-start(f32[32,16,128]{2,1,0:T(8,128)} %bitcast.9), calls=%async_computation.5 | async-start | bytes 524288 | tf_op jit(solution)/shard_map/all_to_all | solution.py:334
  137.4 1.6 collective-permute-start.17
  147.5 16.3 %all-to-all-start.4 = ((f32[32,8,256]{2,1,0:T(8,128)}), f32[32,8,256]{2,1,0:T(8,128)S(1)}, u32[]{:S(2)}, u32[]{:S(2)}) async-start(f32[32,8,256]{2,1,0:T(8,128)} %bitcast.8), calls=%async_computation.4 | async-start | bytes 524288 | tf_op jit(solution)/shard_map/all_to_all | solution.py:182

commit v6 on v5

--- a/solution.py
+++ b/solution.py
@@ -504,13 +504,12 @@
     grams_b, moments_a = lax.optimization_barrier((grams_b, moments_a))
     others_a = swap_pieces(moments_a, "grid")
     half_b = functools.reduce(jnp.add, grams_b)
-    other_b = swap(half_b, "slab", 1)
+    c_held, other_b = lax.optimization_barrier((c_init, swap(half_b, "slab", 1)))
     even_device = lax.axis_index("slab") % 2 == 0
     packed_b = jnp.concatenate(
         [jnp.where(even_device, half_b, other_b), jnp.where(even_device, other_b, half_b)], 0
     )
     gram_b = (packed_b, term_total, ones)
-    c_held, _ = lax.optimization_barrier((c_init, moments_a))
     gram_c = (gram_local(c_held), month_total, ones)
     inverse_a = product_inverse(gram_b, gram_c, devices)
     held_blocks, inverse_a = lax.optimization_barrier((local_blocks, inverse_a))

time: 182 us -> 181 us (level); the launches traced: 181 us -> 182 us
  starting transfers between devices: 44.2 us -> 46.3 us
where the time goes in v6:
time: 181 us; the launch traced here: 182 us
  Pallas kernels  59.4 us (33%)
  waiting for transfers between devices  56.9 us (31%)
  starting transfers between devices  46.3 us (26%)
  blocking collectives  15.6 us (9%)
    pallas_call x3, Pallas kernels, product_inverse(): pl.pallas_call(functools.partial(inverse_kernel, devices, (one[1], two[1]...  33 us
    ppermute x18, waiting for transfers between devices, swap(): lax.ppermute(rows, axis, [(i, i ^ step) for i in range(lax.axis_size(axis...  31.3 us
    all_to_all x4, waiting for transfers between devices, swap_all(): lax.all_to_all(messages, BOTH, split_axis=0, concat_axis=0, tiled=True)  21.2 us
    ppermute x18, starting transfers between devices, swap(): lax.ppermute(rows, axis, [(i, i ^ step) for i in range(lax.axis_size(axis...  20.9 us
    all_to_all x1, blocking collectives, spread_rows(): lax.all_to_all(jnp.tile(rows, (devices, 1)), axes, split_axis=0, concat_a...  15.6 us
    all_to_all x4, starting transfers between devices, swap_all(): lax.all_to_all(messages, BOTH, split_axis=0, concat_axis=0, tiled=True)  15.4 us
    pallas_call x3, Pallas kernels, block_moments(): pl.pallas_call(functools.partial(moments_kernel, mode, orders, len(blocks...  11.8 us
    all_to_all x2, starting transfers between devices, exchange(): parts = lax.all_to_all(rows, axes, split_axis=0, concat_axis=0, tiled=True)  9.98 us
  transfers between devices with their start and end apart: 24, of which 12 were waited for; matrix products, arithmetic and copies ran while one was open for 0% of the time, Pallas kernels for 29%

profile of v6, /device:TPU:0, one launch (start us, length us, event | category | flops | bytes accessed | tf_op | source)
XLA Modules:
  0.0 181.8 jit_solution(10785828019939277568)
XLA Ops:
  0.6 3.0 %collective-permute-start = (f32[128,256]{1,0:T(8,128)}, f32[128,256]{1,0:T(8,128)S(1)}, u32[]{:S(2)}, u32[]{:S(2)}) collective-permute-start(f32[128,256]{1,0:T(8,128)} %param.8), channel_id=1, source_target_pairs={{0,8},{4,12},{8,0},{12,4},{16,24},{20,28},{24,16},{28,20},{1,9},{5... | collective-permute-start | bytes 393224 | tf_op jit(solution)/shard_map/ppermute | solution.py:192
  3.6 1.5 collective-permute-start.1
  5.2 0.0 collective-permute-start.2
  5.8 2.0 %collective-permute-done = f32[128,256]{1,0:T(8,128)S(1)} collective-permute-done((f32[128,256]{1,0:T(8,128)}, f32[128,256]{1,0:T(8,128)S(1)}, u32[]{:S(2)}, u32[]{:S(2)}) %collective-permute-start) | collective-permute-done | bytes 131104 | tf_op jit(solution)/shard_map/ppermute | solution.py:192
  7.9 2.9 %shard_map.76.refs_0_ = bf16[8,64,4096]{2,1,0:T(8,128)(2,1)} custom-call(s32[1,1]{1,0:T(1,128)S(6)} %copy.22.count_ref, bf16[16,64,4096]{2,1,0:T(8,128)(2,1)} %bitcast.22), custom_call_target="tpu_custom_call" | custom-call | bytes 16777216 | tf_op jit(solution)/shard_map/pallas_call | solution.py:163
  10.8 0.0 copy-start
  10.8 0.8 collective-permute-done.1
  11.6 0.0 collective-permute-done.2
  11.7 0.1 collective-permute-start.3
  11.8 0.1 copy.8.coords_ref
  11.9 1.7 collective-permute-done.3
  13.7 1.2 shard_map.77
  14.9 3.7 %collective-permute-start.6 = (f32[192,128]{1,0:T(8,128)S(1)}, f32[192,128]{1,0:T(8,128)S(1)}, u32[]{:S(2)}, u32[]{:S(2)}) collective-permute-start(f32[192,128]{1,0:T(8,128)S(1)} %shard_map.77), channel_id=1, source_target_pairs={{0,3},{1,2},{2,1},{3,0},{4,7},{5,6},{6,5},{7,4},{8,11},{9,10},{10,... | collective-permute-start | bytes 294920 | tf_op jit(solution)/shard_map/ppermute | solution.py:192
  18.6 0.4 collective-permute-start.5
  19.0 0.4 collective-permute-start.4
  19.4 3.4 %shard_map.78.refs_0_ = f32[1024,256]{1,0:T(8,128)S(1)} custom-call(s32[1,1]{1,0:T(1,128)S(6)} %copy.22.count_ref, s32[1,1,16,3]{3,2,1,0:T(8,128)S(1)} %copy.8.coords_ref, bf16[16,64,4096]{2,1,0:T(8,128)(2,1)} %bitcast.23, f32[1024,256]{1,0:T(8,128)S(1)} %constant_dynamic-update-slice_fusion.panel_ref.refs_1_, f32[256,256]{1,0:T(8,128)S(1)} %copy-done), custom_call_target="tpu_custom_call" | custom-call | flops 2147483648 | bytes 8388608 | tf_op jit(solution)/shard_map/pallas_call | solution.py:110
  22.7 0.0 collective-permute-done.6
  22.7 5.3 %collective-permute-done.5 = f32[192,128]{1,0:T(8,128)S(1)} collective-permute-done((f32[192,128]{1,0:T(8,128)S(1)}, f32[192,128]{1,0:T(8,128)S(1)}, u32[]{:S(2)}, u32[]{:S(2)}) %collective-permute-start.5) | collective-permute-done | bytes 98336 | tf_op jit(solution)/shard_map/ppermute | solution.py:192
  28.0 0.0 collective-permute-done.4
  28.0 0.1 collective-permute-start.10
  28.1 0.1 fusion
  28.2 1.7 collective-permute-start.9
  29.9 2.8 %collective-permute-start.7 = (f32[256,256]{1,0:T(8,128)S(1)}, f32[256,256]{1,0:T(8,128)S(1)}, u32[]{:S(2)}, u32[]{:S(2)}) collective-permute-start(f32[256,256]{1,0:T(8,128)S(1)} %get-tuple-element.87), channel_id=1, source_target_pairs={{0,1},{1,0},{2,3},{3,2},{4,5},{5,4},{6,7},{7,6},{8,9},{9,8},{10,11... | collective-permute-start | bytes 786440 | tf_op jit(solution)/shard_map/ppermute | solution.py:192
  32.6 0.0 collective-permute-done.10
  32.6 0.6 fusion.1.two_ref
  33.3 11.0 %shard_map.79.refs_4_ = f32[256,256]{1,0:T(8,128)S(1)} custom-call(f32[384,128]{1,0:T(8,128)S(1)} %pad_maximum_fusion.2.one_ref, f32[1,256]{1,0:T(1,128)S(1)} %broadcast_in_dim.4.one_scale_ref.two_scale_ref, f32[256,256]{1,0:T(8,128)S(1)} %fusion.1.two_ref, f32[1,256]{1,0:T(1,128)S(1)} %broadcast_in_dim.4.one_scale_ref.two_scale_ref), custom_call_target="tpu_custom_call" | custom-call | flops 10000000000 | bytes 786432 | tf_op jit(solution)/shard_map/pallas_call | solution.py:410
  44.3 0.2 shard_map.80.refs_1_
  44.4 8.4 %collective-permute-done.8.refs_2_ = f32[256,256]{1,0:T(8,128)S(1)} collective-permute-done((f32[256,256]{1,0:T(8,128)S(1)}, f32[256,256]{1,0:T(8,128)S(1)}, u32[]{:S(2)}, u32[]{:S(2)}) %collective-permute-start.8) | collective-permute-done | bytes 262176 | tf_op jit(solution)/shard_map/ppermute | solution.py:192
  52.9 1.9 %shard_map.81 = (f32[256,256]{1,0:T(8,128)S(1)}, f32[512,128]{1,0:T(8,128)}) custom-call(f32[1024,256]{1,0:T(8,128)S(1)} %shard_map.78.refs_0_, f32[256,256]{1,0:T(8,128)S(1)} %collective-permute-done.7.refs_1_, f32[256,256]{1,0:T(8,128)S(1)} %collective-permute-done.8.refs_2_, f32[256,256]{1,0:T(8,128)S(1)} %collective-permute-done.9.refs_3_, ...), custom_call_target="tpu_custom_call" | custom-call | tf_op jit(solution)/shard_map/pallas_call | solution.py:437
  54.8 6.6 %all-to-all-start = ((f32[32,16,128]{2,1,0:T(8,128)}), f32[32,16,128]{2,1,0:T(8,128)S(1)}, u32[]{:S(2)}, u32[]{:S(2)}) async-start(f32[32,16,128]{2,1,0:T(8,128)} %bitcast.1), calls=%async_computation | async-start | bytes 524288 | tf_op jit(solution)/shard_map/all_to_all | solution.py:334
  61.4 3.5 %shard_map.82.refs_0_ = bf16[8,64,4096]{2,1,0:T(8,128)(2,1)} custom-call(s32[1,1]{1,0:T(1,128)S(6)} %copy.22.count_ref, bf16[16,64,4096]{2,1,0:T(8,128)(2,1)} %bitcast.25), custom_call_target="tpu_custom_call" | custom-call | bytes 16777216 | tf_op jit(solution)/shard_map/pallas_call | solution.py:163
  64.8 6.7 %all-to-all-done = f32[32,16,128]{2,1,0:T(8,128)S(1)} async-done(((f32[32,16,128]{2,1,0:T(8,128)}), f32[32,16,128]{2,1,0:T(8,128)S(1)}, u32[]{:S(2)}, u32[]{:S(2)}) %all-to-all-start) | async-done | bytes 262176 | tf_op jit(solution)/shard_map/all_to_all | solution.py:334
  71.6 0.8 shard_map.83
  72.3 1.1 collective-permute-start.11
  73.4 1.1 collective-permute-start.13
  74.6 1.3 collective-permute-start.12
  75.8 2.6 %collective-permute-done.11 = bf16[256,256]{1,0:T(8,128)(2,1)S(1)} collective-permute-done((bf16[256,256]{1,0:T(8,128)(2,1)S(1)}, bf16[256,256]{1,0:T(8,128)(2,1)S(1)}, u32[]{:S(2)}, u32[]{:S(2)}) %collective-permute-start.11) | collective-permute-done | bytes 131104 | tf_op jit(solution)/shard_map/ppermute | solution.py:192
  78.4 0.8 shard_map.85
  79.2 3.0 %all-to-all-start.2 = ((f32[32,16,128]{2,1,0:T(8,128)}), f32[32,16,128]{2,1,0:T(8,128)S(1)}, u32[]{:S(2)}, u32[]{:S(2)}) async-start(f32[32,16,128]{2,1,0:T(8,128)} %bitcast.4), calls=%async_computation.2 | async-start | bytes 524288 | tf_op jit(solution)/shard_map/all_to_all | solution.py:334
  82.2 9.2 %collective-permute-done.12 = bf16[256,256]{1,0:T(8,128)(2,1)S(1)} collective-permute-done((bf16[256,256]{1,0:T(8,128)(2,1)S(1)}, bf16[256,256]{1,0:T(8,128)(2,1)S(1)}, u32[]{:S(2)}, u32[]{:S(2)}) %collective-permute-start.12) | collective-permute-done | bytes 131104 | tf_op jit(solution)/shard_map/ppermute | solution.py:192
  91.4 0.0 collective-permute-done.13
  91.5 4.3 %shard_map.84 = f32[1024,256]{1,0:T(8,128)} custom-call(s32[1,1]{1,0:T(1,128)S(6)} %copy.22.count_ref, s32[1,1,16,3]{3,2,1,0:T(8,128)S(1)} %copy.8.coords_ref, bf16[8,64,4096]{2,1,0:T(8,128)(2,1)} %shard_map.76.refs_0_, bf16[8,64,4096]{2,1,0:T(8,128)(2,1)} %shard_map.80.refs_1_, bf16[1024,256]{1,0:T(8,128)(2,1)S(1)} %constant_dynamic-update-slice_fusion.5.refs_2_.refs_3_, ...), custom_call_target="tpu_custom_call" | custom-call | flops 2147483648 | bytes 8388608 | tf_op jit(solution)/shard_map/pallas_call | solution.py:110
  95.8 4.5 %all-to-all-start.1 = ((f32[8,128,256]{2,1,0:T(8,128)}), f32[8,128,256]{2,1,0:T(8,128)S(1)}, u32[]{:S(2)}, u32[]{:S(2)}) async-start(f32[8,128,256]{2,1,0:T(8,128)} %bitcast.3), calls=%async_computation.1 | async-start | bytes 2097152 | tf_op jit(solution)/shard_map/all_to_all | solution.py:182
  100.3 11.0 %shard_map.86.refs_1_ = f32[256,256]{1,0:T(8,128)S(1)} custom-call(f32[512,128]{1,0:T(8,128)S(1)} %bitcast.19, f32[1,256]{1,0:T(1,128)S(1)} %get-tuple-element.73.one_scale_ref, f32[256,256]{1,0:T(8,128)S(1)} %fusion.1.two_ref, f32[1,256]{1,0:T(1,128)S(1)} %broadcast_in_dim.4.one_scale_ref.two_scale_ref), custom_call_target="tpu_custom_call" | custom-call | flops 10000000000 | bytes 786432 | tf_op jit(solution)/shard_map/pallas_call | solution.py:410
  111.3 4.4 %all-to-all-done.1.refs_0_ = f32[8,128,256]{2,1,0:T(8,128)S(1)} async-done(((f32[8,128,256]{2,1,0:T(8,128)}), f32[8,128,256]{2,1,0:T(8,128)S(1)}, u32[]{:S(2)}, u32[]{:S(2)}) %all-to-all-start.1) | async-done | bytes 1048608 | tf_op jit(solution)/shard_map/all_to_all | solution.py:182
  115.7 1.6 shard_map.87
  117.3 3.1 %all-to-all-start.3 = ((f32[32,16,128]{2,1,0:T(8,128)}), f32[32,16,128]{2,1,0:T(8,128)S(1)}, u32[]{:S(2)}, u32[]{:S(2)}) async-start(f32[32,16,128]{2,1,0:T(8,128)} %bitcast.6), calls=%async_computation.3 | async-start | bytes 524288 | tf_op jit(solution)/shard_map/all_to_all | solution.py:334
  120.4 0.2 shard_map.88.refs_1_
  120.6 10.0 %all-to-all-done.3 = f32[32,16,128]{2,1,0:T(8,128)S(1)} async-done(((f32[32,16,128]{2,1,0:T(8,128)}), f32[32,16,128]{2,1,0:T(8,128)S(1)}, u32[]{:S(2)}, u32[]{:S(2)}) %all-to-all-start.3) | async-done | bytes 262176 | tf_op jit(solution)/shard_map/all_to_all | solution.py:334
  130.6 0.7 shard_map.89
  131.3 1.0 collective-permute-start.16
  132.3 1.5 collective-permute-start.15
  133.8 1.0 collective-permute-start.14
  134.8 0.8 shard_map.91
  135.6 2.7 %all-to-all-start.5 = ((f32[32,16,128]{2,1,0:T(8,128)}), f32[32,16,128]{2,1,0:T(8,128)S(1)}, u32[]{:S(2)}, u32[]{:S(2)}) async-start(f32[32,16,128]{2,1,0:T(8,128)} %bitcast.9), calls=%async_computation.5 | async-start | bytes 524288 | tf_op jit(solution)/shard_map/all_to_all | solution.py:334
  138.4 0.3 collective-permute-start.17
  138.7 1.3 collective-permute-done.17
  140.0 4.1 %shard_map.90 = f32[256,256]{1,0:T(8,128)} custom-call(s32[1,1]{1,0:T(1,128)S(6)} %copy.22.count_ref, s32[1,1,16,3]{3,2,1,0:T(8,128)S(1)} %copy.8.coords_ref, bf16[8,64,4096]{2,1,0:T(8,128)(2,1)} %shard_map.82.refs_0_, bf16[8,64,4096]{2,1,0:T(8,128)(2,1)} %shard_map.88.refs_1_, bf16[1024,256]{1,0:T(8,128)(2,1)S(1)} %constant_dynamic-update-slice_fusion.9.refs_2_, ...), custom_call_target="tpu_custom_call" | custom-call | flops 2147483648 | bytes 8388608 | tf_op jit(solution)/shard_map/pallas_call | solution.py:110
  144.1 4.4 %all-to-all-done.5 = f32[32,16,128]{2,1,0:T(8,128)S(1)} async-done(((f32[32,16,128]{2,1,0:T(8,128)}), f32[32,16,128]{2,1,0:T(8,128)S(1)}, u32[]{:S(2)}, u32[]{:S(2)}) %all-to-all-start.5) | async-done | bytes 262176 | tf_op jit(solution)/shard_map/all_to_all | solution.py:334
  148.5 5.5 %all-to-all-start.4 = ((f32[32,8,256]{2,1,0:T(8,128)}), f32[32,8,256]{2,1,0:T(8,128)S(1)}, u32[]{:S(2)}, u32[]{:S(2)}) async-start(f32[32,8,256]{2,1,0:T(8,128)} %bitcast.8), calls=%async_computation.4 | async-start | bytes 524288 | tf_op jit(solution)/shard_map/all_to_all | solution.py:182
  154.0 11.0 %shard_map.92.refs_1_ = f32[256,256]{1,0:T(8,128)S(1)} custom-call(f32[512,128]{1,0:T(8,128)S(1)} %bitcast.20, f32[1,256]{1,0:T(1,128)S(1)} %get-tuple-element.73.one_scale_ref, f32[512,128]{1,0:T(8,128)S(1)} %bitcast.21, f32[1,256]{1,0:T(1,128)S(1)} %get-tuple-element.84.two_scale_ref), custom_call_target="tpu_custom_call" | custom-call | flops 10000000000 | bytes 786432 | tf_op jit(solution)/shard_map/pallas_call | solution.py:410
  165.1 0.2 shard_map.93
  165.3 15.6 %all_to_all.73 = f32[32,8,256]{2,1,0:T(8,128)S(1)} all-to-all(f32[32,8,256]{2,1,0:T(8,128)S(1)} %tile.2), channel_id=1, replica_groups=mesh['slab'=8,'grid'=4] {'slab','grid'}, dimensions={0} | all-to-all | bytes 524288 | tf_op jit(solution)/shard_map/all_to_all | solution.py:188
  181.0 0.7 bitcast_divide_fusion
  (36 shorter events, 0.4 us)
Async XLA Ops:
  0.6 7.2 %collective-permute-start = (f32[128,256]{1,0:T(8,128)}, f32[128,256]{1,0:T(8,128)S(1)}, u32[]{:S(2)}, u32[]{:S(2)}) collective-permute-start(f32[128,256]{1,0:T(8,128)} %param.8), channel_id=1, source_target_pairs={{0,8},{4,12},{8,0},{12,4},{16,24},{20,28},{24,16},{28,20},{1,9},{5... | collective-permute-start | bytes 393224 | tf_op jit(solution)/shard_map/ppermute | solution.py:192
  3.6 8.0 %collective-permute-start.1 = (f32[128,256]{1,0:T(8,128)}, f32[128,256]{1,0:T(8,128)S(1)}, u32[]{:S(2)}, u32[]{:S(2)}) collective-permute-start(f32[128,256]{1,0:T(8,128)} %param.8), channel_id=1, source_target_pairs={{0,16},{4,20},{8,24},{12,28},{16,0},{20,4},{24,8},{28,12},{1,17},{... | collective-permute-start | bytes 393224 | tf_op jit(solution)/shard_map/ppermute | solution.py:192
  5.2 6.5 %collective-permute-start.2 = (f32[128,256]{1,0:T(8,128)}, f32[128,256]{1,0:T(8,128)S(1)}, u32[]{:S(2)}, u32[]{:S(2)}) collective-permute-start(f32[128,256]{1,0:T(8,128)} %param.8), channel_id=1, source_target_pairs={{0,24},{4,28},{8,16},{12,20},{16,8},{20,12},{24,0},{28,4},{1,25},{... | collective-permute-start | bytes 393224 | tf_op jit(solution)/shard_map/ppermute | solution.py:192
  7.9 3.8 %copy-start.1 = (f32[128,256]{1,0:T(8,128)S(1)}, f32[128,256]{1,0:T(8,128)}, u32[]{:S(2)}) copy-start(f32[128,256]{1,0:T(8,128)} %param.8) | copy-start | bytes 393220
  7.9 3.9 %copy-start.2 = (s32[1,1,16,3]{2,1,3,0:T(1,128)S(1)}, s32[1,1,16,3]{2,1,3,0:T(1,128)}, u32[]{:S(2)}) copy-start(s32[1,1,16,3]{2,1,3,0:T(1,128)} %param.6) | copy-start | bytes 580
  10.8 8.5 %copy-start = (f32[256,256]{1,0:T(8,128)S(1)}, f32[256,256]{1,0:T(8,128)}, u32[]{:S(2)}) copy-start(f32[256,256]{1,0:T(8,128)} %refs_3_.1) | copy-start | bytes 786436
  11.7 2.0 %collective-permute-start.3 = (f32[512,256]{1,0:T(8,128)S(1)}, f32[512,256]{1,0:T(8,128)S(1)}, u32[]{:S(2)}, u32[]{:S(2)}) collective-permute-start(f32[512,256]{1,0:T(8,128)S(1)} %pad_maximum_fusion), channel_id=1, source_target_pairs={{0,4},{4,0},{8,12},{12,8},{16,20},{20,16},{24,28},{28,24},{1,5},{5... | collective-permute-start | bytes 1572872 | tf_op jit(solution)/shard_map/ppermute | solution.py:192
  14.9 7.8 %collective-permute-start.6 = (f32[192,128]{1,0:T(8,128)S(1)}, f32[192,128]{1,0:T(8,128)S(1)}, u32[]{:S(2)}, u32[]{:S(2)}) collective-permute-start(f32[192,128]{1,0:T(8,128)S(1)} %shard_map.77), channel_id=1, source_target_pairs={{0,3},{1,2},{2,1},{3,0},{4,7},{5,6},{6,5},{7,4},{8,11},{9,10},{10,... | collective-permute-start | bytes 294920 | tf_op jit(solution)/shard_map/ppermute | solution.py:192
  18.6 9.4 %collective-permute-start.5 = (f32[192,128]{1,0:T(8,128)S(1)}, f32[192,128]{1,0:T(8,128)S(1)}, u32[]{:S(2)}, u32[]{:S(2)}) collective-permute-start(f32[192,128]{1,0:T(8,128)S(1)} %shard_map.77), channel_id=1, source_target_pairs={{0,2},{1,3},{2,0},{3,1},{4,6},{5,7},{6,4},{7,5},{8,10},{9,11},{10,... | collective-permute-start | bytes 294920 | tf_op jit(solution)/shard_map/ppermute | solution.py:192
  19.0 9.0 %collective-permute-start.4 = (f32[192,128]{1,0:T(8,128)S(1)}, f32[192,128]{1,0:T(8,128)S(1)}, u32[]{:S(2)}, u32[]{:S(2)}) collective-permute-start(f32[192,128]{1,0:T(8,128)S(1)} %shard_map.77), channel_id=1, source_target_pairs={{0,1},{1,0},{2,3},{3,2},{4,5},{5,4},{6,7},{7,6},{8,9},{9,8},{10,11... | collective-permute-start | bytes 294920 | tf_op jit(solution)/shard_map/ppermute | solution.py:192
  28.0 4.6 %collective-permute-start.10 = (f32[192,128]{1,0:T(8,128)S(1)}, f32[192,128]{1,0:T(8,128)S(1)}, u32[]{:S(2)}, u32[]{:S(2)}) collective-permute-start(f32[192,128]{1,0:T(8,128)S(1)} %add_add_fusion), channel_id=1, source_target_pairs={{0,4},{4,0},{8,12},{12,8},{16,20},{20,16},{24,28},{28,24},{1,5},{5... | collective-permute-start | bytes 294920 | tf_op jit(solution)/shard_map/ppermute | solution.py:192
  28.2 16.3 %collective-permute-start.9 = (f32[256,256]{1,0:T(8,128)S(1)}, f32[256,256]{1,0:T(8,128)S(1)}, u32[]{:S(2)}, u32[]{:S(2)}) collective-permute-start(f32[256,256]{1,0:T(8,128)S(1)} %get-tuple-element.85), channel_id=1, source_target_pairs={{0,3},{1,2},{2,1},{3,0},{4,7},{5,6},{6,5},{7,4},{8,11},{9,10},{10,... | collective-permute-start | bytes 786440 | tf_op jit(solution)/shard_map/ppermute | solution.py:192
  29.8 23.0 %collective-permute-start.8 = (f32[256,256]{1,0:T(8,128)S(1)}, f32[256,256]{1,0:T(8,128)S(1)}, u32[]{:S(2)}, u32[]{:S(2)}) collective-permute-start(f32[256,256]{1,0:T(8,128)S(1)} %get-tuple-element.86), channel_id=1, source_target_pairs={{0,2},{1,3},{2,0},{3,1},{4,6},{5,7},{6,4},{7,5},{8,10},{9,11},{10,... | collective-permute-start | bytes 786440 | tf_op jit(solution)/shard_map/ppermute | solution.py:192
  29.9 23.0 %collective-permute-start.7 = (f32[256,256]{1,0:T(8,128)S(1)}, f32[256,256]{1,0:T(8,128)S(1)}, u32[]{:S(2)}, u32[]{:S(2)}) collective-permute-start(f32[256,256]{1,0:T(8,128)S(1)} %get-tuple-element.87), channel_id=1, source_target_pairs={{0,1},{1,0},{2,3},{3,2},{4,5},{5,4},{6,7},{7,6},{8,9},{9,8},{10,11... | collective-permute-start | bytes 786440 | tf_op jit(solution)/shard_map/ppermute | solution.py:192
  54.8 16.8 %all-to-all-start = ((f32[32,16,128]{2,1,0:T(8,128)}), f32[32,16,128]{2,1,0:T(8,128)S(1)}, u32[]{:S(2)}, u32[]{:S(2)}) async-start(f32[32,16,128]{2,1,0:T(8,128)} %bitcast.1), calls=%async_computation | async-start | bytes 524288 | tf_op jit(solution)/shard_map/all_to_all | solution.py:334
  72.3 6.1 %collective-permute-start.11 = (bf16[256,256]{1,0:T(8,128)(2,1)S(1)}, bf16[256,256]{1,0:T(8,128)(2,1)S(1)}, u32[]{:S(2)}, u32[]{:S(2)}) collective-permute-start(bf16[256,256]{1,0:T(8,128)(2,1)S(1)} %get-tuple-element.70), channel_id=1, source_target_pairs={{0,1},{1,0},{2,3},{3,2},{4,5},{5,4},{6,7},{7,6},{8,9},{9,8},{10,11... | collective-permute-start | bytes 393224 | tf_op jit(solution)/shard_map/ppermute | solution.py:192
  73.4 18.0 %collective-permute-start.13 = (bf16[256,256]{1,0:T(8,128)(2,1)S(1)}, bf16[256,256]{1,0:T(8,128)(2,1)S(1)}, u32[]{:S(2)}, u32[]{:S(2)}) collective-permute-start(bf16[256,256]{1,0:T(8,128)(2,1)S(1)} %get-tuple-element.70), channel_id=1, source_target_pairs={{0,3},{1,2},{2,1},{3,0},{4,7},{5,6},{6,5},{7,4},{8,11},{9,10},{10,... | collective-permute-start | bytes 393224 | tf_op jit(solution)/shard_map/ppermute | solution.py:192
  74.6 16.9 %collective-permute-start.12 = (bf16[256,256]{1,0:T(8,128)(2,1)S(1)}, bf16[256,256]{1,0:T(8,128)(2,1)S(1)}, u32[]{:S(2)}, u32[]{:S(2)}) collective-permute-start(bf16[256,256]{1,0:T(8,128)(2,1)S(1)} %get-tuple-element.70), channel_id=1, source_target_pairs={{0,2},{1,3},{2,0},{3,1},{4,6},{5,7},{6,4},{7,5},{8,10},{9,11},{10,... | collective-permute-start | bytes 393224 | tf_op jit(solution)/shard_map/ppermute | solution.py:192
  79.2 16.6 %all-to-all-start.2 = ((f32[32,16,128]{2,1,0:T(8,128)}), f32[32,16,128]{2,1,0:T(8,128)S(1)}, u32[]{:S(2)}, u32[]{:S(2)}) async-start(f32[32,16,128]{2,1,0:T(8,128)} %bitcast.4), calls=%async_computation.2 | async-start | bytes 524288 | tf_op jit(solution)/shard_map/all_to_all | solution.py:334
  95.8 19.9 %all-to-all-start.1 = ((f32[8,128,256]{2,1,0:T(8,128)}), f32[8,128,256]{2,1,0:T(8,128)S(1)}, u32[]{:S(2)}, u32[]{:S(2)}) async-start(f32[8,128,256]{2,1,0:T(8,128)} %bitcast.3), calls=%async_computation.1 | async-start | bytes 2097152 | tf_op jit(solution)/shard_map/all_to_all | solution.py:182
  117.3 13.3 %all-to-all-start.3 = ((f32[32,16,128]{2,1,0:T(8,128)}), f32[32,16,128]{2,1,0:T(8,128)S(1)}, u32[]{:S(2)}, u32[]{:S(2)}) async-start(f32[32,16,128]{2,1,0:T(8,128)} %bitcast.6), calls=%async_computation.3 | async-start | bytes 524288 | tf_op jit(solution)/shard_map/all_to_all | solution.py:334
  131.3 7.0 %collective-permute-start.16 = (bf16[128,256]{1,0:T(8,128)(2,1)S(1)}, bf16[128,256]{1,0:T(8,128)(2,1)S(1)}, u32[]{:S(2)}, u32[]{:S(2)}) collective-permute-start(bf16[128,256]{1,0:T(8,128)(2,1)S(1)} %get-tuple-element.82), channel_id=1, source_target_pairs={{0,24},{4,28},{8,16},{12,20},{16,8},{20,12},{24,0},{28,4},{1,25},{... | collective-permute-start | bytes 196616 | tf_op jit(solution)/shard_map/ppermute | solution.py:192
  132.3 6.0 %collective-permute-start.15 = (bf16[128,256]{1,0:T(8,128)(2,1)S(1)}, bf16[128,256]{1,0:T(8,128)(2,1)S(1)}, u32[]{:S(2)}, u32[]{:S(2)}) collective-permute-start(bf16[128,256]{1,0:T(8,128)(2,1)S(1)} %get-tuple-element.82), channel_id=1, source_target_pairs={{0,16},{4,20},{8,24},{12,28},{16,0},{20,4},{24,8},{28,12},{1,17},{... | collective-permute-start | bytes 196616 | tf_op jit(solution)/shard_map/ppermute | solution.py:192
  133.8 4.5 %collective-permute-start.14 = (bf16[128,256]{1,0:T(8,128)(2,1)S(1)}, bf16[128,256]{1,0:T(8,128)(2,1)S(1)}, u32[]{:S(2)}, u32[]{:S(2)}) collective-permute-start(bf16[128,256]{1,0:T(8,128)(2,1)S(1)} %get-tuple-element.82), channel_id=1, source_target_pairs={{0,8},{4,12},{8,0},{12,4},{16,24},{20,28},{24,16},{28,20},{1,9},{5... | collective-permute-start | bytes 196616 | tf_op jit(solution)/shard_map/ppermute | solution.py:192
  135.6 12.9 %all-to-all-start.5 = ((f32[32,16,128]{2,1,0:T(8,128)}), f32[32,16,128]{2,1,0:T(8,128)S(1)}, u32[]{:S(2)}, u32[]{:S(2)}) async-start(f32[32,16,128]{2,1,0:T(8,128)} %bitcast.9), calls=%async_computation.5 | async-start | bytes 524288 | tf_op jit(solution)/shard_map/all_to_all | solution.py:334
  138.4 1.6 collective-permute-start.17
  148.5 16.5 %all-to-all-start.4 = ((f32[32,8,256]{2,1,0:T(8,128)}), f32[32,8,256]{2,1,0:T(8,128)S(1)}, u32[]{:S(2)}, u32[]{:S(2)}) async-start(f32[32,8,256]{2,1,0:T(8,128)} %bitcast.8), calls=%async_computation.4 | async-start | bytes 524288 | tf_op jit(solution)/shard_map/all_to_all | solution.py:182
